TPU v7x, 32 devices: a whole 2x2x4 slice. The times are simulated.
32 devices in a mesh: groups: 1, frames: 32 (over z, y, x, core).
Axes of the slice: x: 2, y: 2, z: 4, core: 2. Of those that a mesh axis runs over, the one named last changes fastest.
Arguments:
- skip: bfloat16 [32, 256, 640], P(('groups', 'frames')), may hold values from -24 to 24
- control: bfloat16 [32, 256, 640], P('groups', 'frames'), may hold values from -6 to 6
- zero_weight: bfloat16 [640, 640], replicated, may hold values from -1 to 1
- gn_gain: float32 [640], replicated, may hold values from 0.1 to 1.9
- gn_bias: float32 [640], replicated, may hold values from -0.5 to 0.5
- conv_weight: bfloat16 [9, 640, 640], replicated, may hold values from -0.078125 to 0.078125
- ln_gain: float32 [640], replicated, may hold values from 0.1 to 1.9
- qkv_weight: bfloat16 [640, 1920], replicated, may hold values from -5 to 5
- out_weight: bfloat16 [640, 640], replicated, may hold values from -0.25 to 0.25
Outputs:
- output: bfloat16 [32, 256, 640], P(('groups', 'frames'))
All inputs are finite; a program needn't handle non-finite values.
Results may differ from a plain program's by a relative error of at most 0.0043.
Values may be sent and summed in bfloat16 or wider, within the bound.
No kernel may reach another device: no remote copies, remote signals or barrier semaphores. Data moves between devices by JAX's collectives and lax.ppermute only.
A program may use at most 64 MiB of HBM per device.

v0:
```python
import math

import jax
import jax.numpy as jnp
from jax import lax
from jax.sharding import PartitionSpec as P

HEADS = 10
HD = 64
GROUPS = 32
CLIP = 32
W = 32


norm_epsilon = 1e-05


def attend_block(qkv_rows, chans):
    frame_count, single, count, _ = qkv_rows.shape
    clip_count = frame_count // CLIP
    shaped = qkv_rows.reshape(clip_count, CLIP, count, 3, HEADS, HD)
    queries = shaped[:, :, :, 0]
    key_rows = shaped[:, :, :, 1]
    value_rows = shaped[:, :, :, 2]
    scores = jnp.einsum(
        "atphd,asphd->aphts", queries, key_rows, preferred_element_type=jnp.float32
    ) * (1.0 / math.sqrt(HD))
    scores = scores - jnp.max(scores, axis=-1, keepdims=True)
    expon = jnp.exp(scores)
    attn_weights = (expon / jnp.sum(expon, axis=-1, keepdims=True)).astype(jnp.bfloat16)
    mixed = jnp.einsum(
        "aphts,asphd->atphd", attn_weights, value_rows, preferred_element_type=jnp.float32
    )
    return mixed.astype(jnp.bfloat16).reshape(frame_count, single, count, chans)


def body(
    skip, control, zero_weight, gn_gain, gn_bias, conv_weight, ln_gain, qkv_weight, out_weight
):
    f_dev, pixels, chans = skip.shape
    devices = lax.axis_size("frames")
    frame_count, pix_dev, _ = control.shape
    height = pixels // W
    zero_out = jnp.dot(control.reshape(-1, chans), zero_weight, preferred_element_type=jnp.float32)
    zero_out = zero_out.astype(jnp.bfloat16).reshape(frame_count, pix_dev, chans)
    zero_frames = lax.all_to_all(zero_out, "frames", split_axis=0, concat_axis=1, tiled=True)
    joined = skip.astype(jnp.float32) + zero_frames.astype(jnp.float32)
    group_size = chans // GROUPS
    grouped = joined.reshape(f_dev, pixels, GROUPS, group_size)
    clip_count = f_dev * devices // CLIP
    frame_ids = lax.axis_index("frames") * f_dev + jnp.arange(f_dev, dtype=jnp.int32)
    member = (
        frame_ids[:, None] // CLIP == jnp.arange(clip_count, dtype=jnp.int32)[None, :]
    ).astype(jnp.float32)
    count_all = float(CLIP * pixels * group_size)
    frame_sums = jnp.sum(grouped, axis=(1, 3))
    clip_sums = jnp.sum(member[:, :, None] * frame_sums[:, None, :], axis=0)
    frame_sq = jnp.sum(jnp.square(grouped), axis=(1, 3))
    clip_sq = jnp.sum(member[:, :, None] * frame_sq[:, None, :], axis=0)
    total_sums, total_sq = lax.psum((clip_sums, clip_sq), "frames")
    clip_mean = total_sums / count_all
    clip_var = total_sq / count_all - jnp.square(clip_mean)
    frame_mean = jnp.sum(member[:, :, None] * clip_mean[None], axis=1)
    centred = grouped - frame_mean[:, None, :, None]
    frame_var = jnp.sum(member[:, :, None] * clip_var[None], axis=1)
    normed_groups = (centred * lax.rsqrt(frame_var + norm_epsilon)[:, None, :, None]).reshape(
        f_dev, pixels, chans
    )
    activated = (
        jax.nn.silu(normed_groups * gn_gain + gn_bias)
        .astype(jnp.bfloat16)
        .reshape(f_dev, height, W, chans)
    )
    padded = jnp.pad(activated, ((0, 0), (1, 1), (1, 1), (0, 0)))
    conv_sum = jnp.zeros((f_dev * pixels, chans), jnp.float32)
    for tap_index in range(9):
        row_shift, col_shift = divmod(tap_index, 3)
        window = padded[:, row_shift : row_shift + height, col_shift : col_shift + W, :].reshape(
            -1, chans
        )
        conv_sum = conv_sum + jnp.dot(
            window, conv_weight[tap_index], preferred_element_type=jnp.float32
        )
    resid = joined.reshape(-1, chans) + conv_sum
    token_mean = jnp.mean(resid, axis=-1, keepdims=True)
    token_var = jnp.mean(jnp.square(resid - token_mean), axis=-1, keepdims=True)
    normed = ((resid - token_mean) * lax.rsqrt(token_var + norm_epsilon) * ln_gain).astype(
        jnp.bfloat16
    )
    per_device = pixels // devices
    qkv_rows = jnp.dot(normed, qkv_weight, preferred_element_type=jnp.float32).astype(jnp.bfloat16)
    qkv_rows = qkv_rows.reshape(f_dev, devices, per_device, 3 * chans)
    attended = attend_block(
        lax.all_to_all(qkv_rows, "frames", split_axis=1, concat_axis=0, tiled=True), chans
    )
    returned = lax.all_to_all(attended, "frames", split_axis=0, concat_axis=1, tiled=True)
    output = resid + jnp.dot(
        returned.reshape(-1, chans), out_weight, preferred_element_type=jnp.float32
    )
    return output.astype(jnp.bfloat16).reshape(f_dev, pixels, chans)


def solution(mesh):
    in_specs = (
        P(("groups", "frames"), None, None),
        P("groups", "frames", None),
        P(),
        P(),
        P(),
        P(),
        P(),
        P(),
        P(),
    )
    out_specs = P(("groups", "frames"), None, None)
    return jax.shard_map(body, mesh=mesh, in_specs=in_specs, out_specs=out_specs, check_vma=False)
```

profile of v0, /device:TPU:0, one launch (start us, length us, event | category | flops | bytes accessed | tf_op | source)
XLA Modules:
  0.0 136.1 jit_solution(5476533162441262583)
XLA Ops:
  0.0 0.0 copy-start
  0.0 0.0 copy-start.2
  0.0 2.6 %fusion.7 = bf16[32,8,640]{2,1,0:T(8,128)(2,1)} fusion(bf16[640,640]{1,0:T(8,128)(2,1)} %param.11, bf16[32,8,640]{2,1,0:T(8,128)(2,1)} %param.10), kind=kOutput, calls=%fused_computation.21 | convolution fusion | flops 209879040 | bytes 1474560 | tf_op jit(solution)/shard_map/dot_general | solution.py:44
  2.6 7.3 %all-to-all-start = ((bf16[32,8,640]{2,1,0:T(8,128)(2,1)}), bf16[32,8,640]{2,1,0:T(8,128)(2,1)S(1)}, u32[]{:S(2)}, u32[]{:S(2)}) async-start(bf16[32,8,640]{2,1,0:T(8,128)(2,1)} %fusion.7), calls=%async_computation | async-start | bytes 655360 | tf_op jit(solution)/shard_map/all_to_all | solution.py:46
  9.9 12.0 %all-to-all-done = bf16[32,8,640]{2,1,0:T(8,128)(2,1)S(1)} async-done(((bf16[32,8,640]{2,1,0:T(8,128)(2,1)}), bf16[32,8,640]{2,1,0:T(8,128)(2,1)S(1)}, u32[]{:S(2)}, u32[]{:S(2)}) %all-to-all-start) | async-done | bytes 327712 | tf_op jit(solution)/shard_map/all_to_all | solution.py:46
  22.0 1.1 multiply_reduce_fusion.1
  23.1 0.1 reduce_sum.79
  23.2 0.1 reduce_sum.76
  23.3 0.1 reduce_sum.80
  23.4 0.1 reduce_sum.77
  23.5 38.5 %all-reduce.1 = (f32[1,32]{1,0:T(1,128)S(1)}, f32[1,32]{1,0:T(1,128)S(1)}) all-reduce(f32[1,32]{1,0:T(1,128)S(1)} %get-tuple-element.27, f32[1,32]{1,0:T(1,128)S(1)} %get-tuple-element.26), channel_id=1, replica_groups=mesh['groups'=1,'frames'=32] {'frames'}, use_global_device_ids=true, to_apply=%region_2.3 | all-reduce | flops 64 | bytes 512 | tf_op jit(solution)/shard_map/psum | solution.py:60
  62.0 0.1 sub.45
  62.1 0.1 sub.46
  62.2 0.1 mul.144
  62.3 0.1 mul.145
  62.4 0.0 copy-done.2
  62.4 0.0 copy-start.1
  62.4 1.1 multiply_convert_fusion.1
  63.5 0.3 pad_slice_fusion
  63.8 2.0 %fusion.17 = f32[256,640]{1,0:T(8,128)S(1)} fusion(bf16[256,640]{1,0:T(8,128)(2,1)S(1)} %bitcast.123, bf16[9,640,640]{2,1,0:T(8,128)(2,1)} %param.14), kind=kOutput, calls=%fused_computation.31 | convolution fusion | flops 209715200 | bytes 1802240 | tf_op jit(solution)/shard_map/dot_general | solution.py:81
  65.8 1.6 %convolution_add_fusion.8 = f32[256,640]{1,0:T(8,128)S(1)} fusion(f32[256,640]{1,0:T(8,128)S(1)} %fusion.17, bf16[256,640]{1,0:T(8,128)(2,1)S(1)} %bitcast.122, bf16[9,640,640]{2,1,0:T(8,128)(2,1)} %param.14), kind=kOutput, calls=%fused_computation.17 | convolution fusion | flops 209879040 | bytes 2457600 | tf_op jit(solution)/shard_map/dot_general | solution.py:81
  67.4 0.0 copy-done.1
  67.4 0.5 convolution_add_fusion.7
  67.9 0.5 convolution_add_fusion.6
  68.3 0.5 convolution_add_fusion.5
  68.8 0.0 copy-start.3
  68.8 0.5 convolution_add_fusion.4
  69.3 0.5 convolution_add_fusion.3
  69.7 0.0 copy-start.4
  69.8 0.5 convolution_add_fusion.2
  70.2 0.0 copy-done.3
  70.2 0.6 fusion.39
  70.8 0.2 multiply_reduce_fusion
  71.0 0.0 copy-done
  71.0 0.0 copy-done.4
  71.1 1.0 fusion.1
  72.1 28.4 %all_to_all.12 = bf16[1,32,8,1920]{3,2,0,1:T(8,128)(2,1)} all-to-all(bf16[1,32,8,1920]{3,2,0,1:T(8,128)(2,1)S(1)} %fusion.1), channel_id=1, replica_groups=mesh['groups'=1,'frames'=32] {'frames'}, dimensions={1} | all-to-all | bytes 1966080 | tf_op jit(solution)/shard_map/all_to_all | solution.py:94
  100.5 4.4 %reshape.253 = bf16[1,32,8,3,10,64]{5,4,3,2,1,0:T(8,128)(2,1)} reshape(bf16[1,32,8,1920]{3,2,0,1:T(8,128)(2,1)} %all_to_all.12) | data formatting | bytes 1966080 | tf_op jit(solution)/shard_map/reshape | solution.py:21
  104.9 4.2 %fusion.38 = (bf16[1,32,8,1,10,64]{5,4,3,2,1,0:T(8,128)(2,1)}, bf16[1,32,8,1,10,64]{5,4,3,2,1,0:T(8,128)(2,1)}, bf16[1,32,8,1,10,64]{5,4,3,2,1,0:T(8,128)(2,1)}) fusion(bf16[1,32,8,3,10,64]{5,4,3,2,1,0:T(8,128)(2,1)} %reshape.253), kind=kLoop, calls=%fused_computation.74 | loop fusion | bytes 1966080 | tf_op jit(solution)/shard_map/slice | solution.py:24
  109.1 3.8 %fusion.40 = (f32[8,10,32]{2,1,0:T(8,128)S(1)}, f32[8,10,32,32]{2,3,1,0:T(8,128)}) fusion(bf16[1,32,8,1,10,64]{5,4,3,2,1,0:T(8,128)(2,1)} %get-tuple-element.11, bf16[1,32,8,1,10,64]{5,4,3,2,1,0:T(8,128)(2,1)} %get-tuple-element.10), kind=kOutput, calls=%fused_computation.76 | convolution fusion | flops 10731551 | bytes 993280 | tf_op jit(solution)/shard_map/sub | solution.py:28
  112.9 2.3 %fusion.4 = bf16[1,32,8,10,64]{4,1,3,2,0:T(8,128)(2,1)S(1)} fusion(f32[8,10,32,32]{2,3,1,0:T(8,128)} %get-tuple-element.25, bf16[1,32,8,1,10,64]{5,4,3,2,1,0:T(8,128)(2,1)} %get-tuple-element.9, f32[8,10,32]{2,1,0:T(8,128)S(1)} %get-tuple-element.24), kind=kOutput, calls=%fused_computation.8 | convolution fusion | flops 10813440 | bytes 993280 | tf_op jit(solution)/shard_map/aphts,asphd->atphd/dot_general | solution.py:31
  115.1 1.3 copy.21
  116.5 1.8 %reshape.257 = bf16[32,1,8,640]{3,2,0,1:T(8,128)(2,1)S(1)} reshape(bf16[1,32,8,10,64]{4,3,2,1,0:T(8,128)(2,1)} %copy.21) | data formatting | bytes 655360 | tf_op jit(solution)/shard_map/reshape | solution.py:34
  118.3 15.5 %all_to_all.13 = bf16[32,1,8,640]{3,2,1,0:T(8,128)(2,1)S(1)} all-to-all(bf16[32,1,8,640]{3,2,1,0:T(8,128)(2,1)S(1)} %bitcast.116), channel_id=1, replica_groups=mesh['groups'=1,'frames'=32] {'frames'}, dimensions={0} | all-to-all | bytes 655360 | tf_op jit(solution)/shard_map/all_to_all | solution.py:96
  133.8 2.3 %fusion.8 = bf16[1,256,640]{2,1,0:T(8,128)(2,1)} fusion(f32[256,640]{1,0:T(8,128)S(1)} %get-tuple-element.23, bf16[640,640]{1,0:T(8,128)(2,1)} %param.17, bf16[32,1,8,640]{3,2,1,0:T(8,128)(2,1)S(1)} %all_to_all.13), kind=kOutput, calls=%fused_computation.22 | convolution fusion | flops 210042880 | bytes 2129920 | tf_op jit(solution)/shard_map/dot_general | solution.py:97
  (4 shorter events, 0.0 us)
Async XLA Ops:
  0.0 71.0 %copy-start = (bf16[640,1920]{1,0:T(8,128)(2,1)S(1)}, bf16[640,1920]{1,0:T(8,128)(2,1)}, u32[]{:S(2)}) copy-start(bf16[640,1920]{1,0:T(8,128)(2,1)} %param.16) | copy-start | bytes 7372804
  0.0 62.4 %copy-start.2 = (bf16[1,256,640]{2,1,0:T(8,128)(2,1)S(1)}, bf16[1,256,640]{2,1,0:T(8,128)(2,1)}, u32[]{:S(2)}) copy-start(bf16[1,256,640]{2,1,0:T(8,128)(2,1)} %param.9) | copy-start | bytes 983044
  2.6 19.4 %all-to-all-start = ((bf16[32,8,640]{2,1,0:T(8,128)(2,1)}), bf16[32,8,640]{2,1,0:T(8,128)(2,1)S(1)}, u32[]{:S(2)}, u32[]{:S(2)}) async-start(bf16[32,8,640]{2,1,0:T(8,128)(2,1)} %fusion.7), calls=%async_computation | async-start | bytes 655360 | tf_op jit(solution)/shard_map/all_to_all | solution.py:46
  62.4 5.0 %copy-start.1 = (bf16[9,640,640]{2,1,0:T(8,128)(2,1)S(1)}, bf16[9,640,640]{2,1,0:T(8,128)(2,1)}, u32[]{:S(2)}) copy-start(bf16[9,640,640]{2,1,0:T(8,128)(2,1)} %param.14) | copy-start | bytes 22118404
  68.8 1.4 %copy-start.3 = (bf16[1,256,640]{2,1,0:T(8,128)(2,1)S(1)}, bf16[1,256,640]{2,1,0:T(8,128)(2,1)}, u32[]{:S(2)}) copy-start(bf16[1,256,640]{2,1,0:T(8,128)(2,1)} %param.9) | copy-start | bytes 983044
  69.7 1.3 copy-start.4
where the time goes:
time: 137 us; the launch traced here: 136 us
  blocking collectives  82.4 us (60%)
  matrix products  18.8 us (14%)
  local copies, waits for them, and re-layouts  12.6 us (9%)
  waiting for transfers between devices  12 us (9%)
  starting transfers between devices  7.33 us (5%)
  other arithmetic  2.73 us (2%)
    psum x1, blocking collectives, body(): total_sums, total_sq = lax.psum((clip_sums, clip_sq), 'frames')  38.5 us
    all_to_all x1, blocking collectives, body(): lax.all_to_all(qkv_rows, 'frames', split_axis=1, concat_axis=0, tiled=True)  28.4 us
    all_to_all x1, blocking collectives, body(): lax.all_to_all(attended, 'frames', split_axis=0, concat_axis=1, tiled=True)  15.5 us
    all_to_all x1, waiting for transfers between devices, body(): lax.all_to_all(zero_out, 'frames', split_axis=0, concat_axis=1, tiled=True)  12 us
    all_to_all x1, starting transfers between devices, body(): lax.all_to_all(zero_out, 'frames', split_axis=0, concat_axis=1, tiled=True)  7.33 us
    dot_general x9, matrix products, body(): jnp.dot(window, conv_weight[tap_index], preferred_element_type=jnp.float32)  6.89 us
    reshape x1, local copies, waits for them, and re-layouts, attend_block(): shaped = qkv_rows.reshape(clip_count, CLIP, count, 3, HEADS, HD)  4.38 us
    slice x1, local copies, waits for them, and re-layouts, attend_block(): value_rows = shaped[:, :, :, 2]  4.21 us
  transfers between devices with their start and end apart: 1, of which 1 were waited for; matrix products, arithmetic and copies ran while one was open for 0% of the time, Pallas kernels for 0%

commit v1 on v0

v1 whole, which is shorter than its diff:
```python
import functools
import math

import jax
import jax.numpy as jnp
from jax import lax
from jax.experimental import pallas as pl
from jax.experimental.pallas import tpu as pltpu
from jax.sharding import PartitionSpec as P

HEADS = 10
HD = 64
GROUPS = 32
CLIP = 32
W = 32
LANES = 128

norm_epsilon = 1e-05
F32 = jnp.float32
BF16 = jnp.bfloat16
VMEM = pl.BlockSpec(memory_space=pltpu.VMEM)
SMEM = pl.BlockSpec(memory_space=pltpu.SMEM)


def params(mib):
    return pltpu.CompilerParams(vmem_limit_bytes=mib * 1024 * 1024)


def exact_dot(left, right, dims):
    return lax.dot_general(
        left, right, (dims, ((), ())), precision=lax.Precision.HIGHEST, preferred_element_type=F32
    )


def group_members(chans, first_lane):
    size = chans // GROUPS
    chan = lax.broadcasted_iota(jnp.int32, (chans, LANES), 0)
    start = (lax.broadcasted_iota(jnp.int32, (chans, LANES), 1) - first_lane) * size
    inside = (chan >= start) & (chan < start + size) & (start >= 0) & (start < chans)
    return inside.astype(F32)


def join_kernel(skip_ref, control_ref, weight_ref, joined_ref, stats_ref):
    pixels, chans = skip_ref.shape
    zero_out = jnp.dot(control_ref[...], weight_ref[...], preferred_element_type=F32).astype(BF16)
    joined = skip_ref[...].astype(F32) + zero_out.astype(F32)
    joined_ref[...] = joined
    sum_lanes = group_members(chans, 0)
    sq_lanes = group_members(chans, GROUPS)
    sums = jnp.broadcast_to(jnp.sum(joined, axis=0, keepdims=True), (8, chans))
    group_sums = exact_dot(sums, sum_lanes, ((1,), (0,)))
    group_mean = group_sums * (1.0 / (pixels * (chans // GROUPS)))
    chan_mean = exact_dot(group_mean, sum_lanes, ((1,), (1,)))[:1]
    spread = jnp.sum(jnp.square(joined - chan_mean), axis=0, keepdims=True)
    group_spread = exact_dot(jnp.broadcast_to(spread, (8, chans)), sq_lanes, ((1,), (0,)))
    stats_ref[...] = jnp.broadcast_to((group_sums + group_spread)[:1], stats_ref.shape)


def conv_kernel(
    clip_ref, joined_ref, stats_ref, gain_ref, bias_ref, weight_ref, resid_ref, window_ref
):
    pixels, chans = joined_ref.shape
    frames = stats_ref.shape[0]
    per_frame = float(pixels * (chans // GROUPS))
    stats = stats_ref[...]
    if frames > CLIP:
        row = lax.broadcasted_iota(jnp.int32, (frames, LANES), 0)
        first = clip_ref[0] * CLIP
        member = (row >= first) & (row < first + CLIP)
    else:
        member = jnp.full((frames, LANES), True)
    stats = jnp.where(member, stats, 0.0)
    mean_rows = stats * (1.0 / per_frame)
    lane_mean = jnp.sum(mean_rows, axis=0, keepdims=True) * (1.0 / CLIP)
    between = jnp.where(member, jnp.square(mean_rows - lane_mean), 0.0)
    lane_between = jnp.sum(between, axis=0, keepdims=True) * (1.0 / CLIP)
    lane_id = lax.broadcasted_iota(jnp.int32, (8, LANES), 1)
    lane_mean = jnp.broadcast_to(lane_mean, (8, LANES))
    lane_between = jnp.broadcast_to(lane_between, (8, LANES))
    sum_lanes = group_members(chans, 0)
    both_lanes = sum_lanes + group_members(chans, GROUPS)
    lane_var = jnp.where(lane_id < GROUPS, lane_between, lane_mean)
    chan_mean = exact_dot(lane_mean, sum_lanes, ((1,), (1,)))[:1]
    chan_var = exact_dot(lane_var, both_lanes, ((1,), (1,)))[:1]
    joined = joined_ref[...]
    scaled = (joined - chan_mean) * lax.rsqrt(chan_var + norm_epsilon)
    activated = jax.nn.silu(scaled * gain_ref[...] + bias_ref[...])
    col = lax.rem(lax.broadcasted_iota(jnp.int32, (pixels, chans), 0), W)
    left = jnp.where(col == 0, 0.0, pltpu.roll(activated, 1, 0))
    right = jnp.where(col == W - 1, 0.0, pltpu.roll(activated, pixels - 1, 0))
    edge = jnp.zeros((W, 3 * chans), BF16)
    window_ref[:W] = edge
    window_ref[W + pixels :] = edge
    window_ref[W : W + pixels, :chans] = left.astype(BF16)
    window_ref[W : W + pixels, chans : 2 * chans] = activated.astype(BF16)
    window_ref[W : W + pixels, 2 * chans :] = right.astype(BF16)
    total = joined
    for shift in range(3):
        total = total + jnp.dot(
            window_ref[shift * W : shift * W + pixels],
            weight_ref[shift],
            preferred_element_type=F32,
        )
    resid_ref[...] = total.astype(BF16)


def attend_kernel(per_dev, resid_ref, gain_ref, qkv_ref, out_ref, result_ref, rows_ref, mixed_ref):
    rows, chans = resid_ref.shape
    resid = resid_ref[...].astype(F32)
    mean = jnp.mean(resid, axis=-1, keepdims=True)
    centred = resid - mean
    var = jnp.mean(jnp.square(centred), axis=-1, keepdims=True)
    normed = (centred * lax.rsqrt(var + norm_epsilon) * gain_ref[...]).astype(BF16)
    rows_ref[...] = jnp.dot(normed, qkv_ref[...], preferred_element_type=F32).astype(BF16)
    row = lax.broadcasted_iota(jnp.int32, (rows, rows), 0)
    col = lax.broadcasted_iota(jnp.int32, (rows, rows), 1)
    paired = lax.rem(row, per_dev) == lax.rem(col, per_dev)
    if rows > per_dev * CLIP:
        paired = paired & (lax.div(row, per_dev * CLIP) == lax.div(col, per_dev * CLIP))
    heads_in = LANES // HD
    head_lane = lax.broadcasted_iota(jnp.int32, (rows, LANES), 1)
    for block in range(chans // LANES):
        start = block * LANES
        queries = rows_ref[:, start : start + LANES]
        keys = rows_ref[:, chans + start : chans + start + LANES]
        values = rows_ref[:, 2 * chans + start : 2 * chans + start + LANES]
        mixed = jnp.zeros((rows, LANES), F32)
        for inner in range(heads_in):
            own = (head_lane >= inner * HD) & (head_lane < (inner + 1) * HD)
            head_queries = jnp.where(own, queries, jnp.zeros_like(queries))
            head_values = jnp.where(own, values, jnp.zeros_like(values))
            scores = lax.dot_general(
                head_queries, keys, (((1,), (1,)), ((), ())), preferred_element_type=F32
            ) * (1.0 / math.sqrt(HD))
            scores = jnp.where(paired, scores, -1e30)
            expon = jnp.exp(scores - jnp.max(scores, axis=-1, keepdims=True))
            weights = (expon / jnp.sum(expon, axis=-1, keepdims=True)).astype(BF16)
            mixed = mixed + jnp.dot(weights, head_values, preferred_element_type=F32)
        mixed_ref[:, start : start + LANES] = mixed.astype(BF16)
    result = resid + jnp.dot(mixed_ref[...], out_ref[...], preferred_element_type=F32)
    result_ref[...] = result.astype(BF16)


def exchange(blocks):
    return lax.all_to_all(blocks, "frames", split_axis=0, concat_axis=0, tiled=True)


def body(
    skip, control, zero_weight, gn_gain, gn_bias, conv_weight, ln_gain, qkv_weight, out_weight
):
    f_dev, pixels, chans = skip.shape
    devices = lax.axis_size("frames")
    frame_count, per_dev, _ = control.shape
    rows = frame_count * per_dev
    own_control = exchange(control.reshape(rows, chans)).reshape(devices, f_dev, per_dev, chans)
    first_frame = lax.axis_index("frames") * f_dev if frame_count > CLIP else jnp.int32(0)
    joined, stats = [], []
    for f in range(f_dev):
        frame_joined, frame_stats = pl.pallas_call(
            join_kernel,
            out_shape=(
                jax.ShapeDtypeStruct((pixels, chans), F32),
                jax.ShapeDtypeStruct((devices, LANES), F32),
            ),
            in_specs=[VMEM] * 3,
            out_specs=(VMEM, VMEM),
            compiler_params=params(12),
            name="join",
        )(skip[f], own_control[:, f].reshape(pixels, chans), zero_weight)
        joined.append(frame_joined)
        stats.append(frame_stats)
    all_stats = exchange(jnp.stack(stats, axis=1).reshape(devices * f_dev, LANES))
    resid = []
    for f in range(f_dev):
        resid.append(
            pl.pallas_call(
                conv_kernel,
                out_shape=jax.ShapeDtypeStruct((pixels, chans), BF16),
                in_specs=[SMEM] + [VMEM] * 5,
                out_specs=VMEM,
                scratch_shapes=[pltpu.VMEM((pixels + 2 * W, 3 * chans), BF16)],
                compiler_params=params(24),
                name="conv",
            )(
                ((first_frame + f) // CLIP).reshape(1),
                joined[f],
                all_stats,
                gn_gain.reshape(1, chans),
                gn_bias.reshape(1, chans),
                conv_weight.reshape(3, 3 * chans, chans),
            )
        )
    by_pixel = jnp.stack(resid).reshape(f_dev, devices, per_dev, chans)
    by_pixel = exchange(by_pixel.transpose(1, 0, 2, 3).reshape(rows, chans))
    result = pl.pallas_call(
        functools.partial(attend_kernel, per_dev),
        out_shape=jax.ShapeDtypeStruct((rows, chans), BF16),
        in_specs=[VMEM] * 4,
        out_specs=VMEM,
        scratch_shapes=[pltpu.VMEM((rows, 3 * chans), BF16), pltpu.VMEM((rows, chans), BF16)],
        compiler_params=params(24),
        name="attend",
    )(by_pixel, ln_gain.reshape(1, chans), qkv_weight, out_weight)
    output = exchange(result).reshape(devices, f_dev, per_dev, chans)
    return output.transpose(1, 0, 2, 3).reshape(f_dev, pixels, chans)


def solution(mesh):
    in_specs = (
        P(("groups", "frames"), None, None),
        P("groups", "frames", None),
        P(),
        P(),
        P(),
        P(),
        P(),
        P(),
        P(),
    )
    out_specs = P(("groups", "frames"), None, None)
    return jax.shard_map(body, mesh=mesh, in_specs=in_specs, out_specs=out_specs, check_vma=False)
```

time: 137 us -> 75.5 us (0.55)
  blocking collectives: 82.4 us -> 33.5 us
  matrix products: 18.8 us -> 0 us
  Pallas kernels: 0 us -> 10.1 us
  waiting for transfers between devices: 12 us -> 17.7 us
  local copies, waits for them, and re-layouts: 12.6 us -> 8.47 us
  other arithmetic: 2.73 us -> 0 us
  starting transfers between devices: 7.33 us -> 5.13 us
    psum x1 -> x0, blocking collectives: 38.5 us -> none  [body(): total_sums, total_sq = lax.psum((clip_sums, clip_sq), 'frames')]
    dot_general x13 -> x0, matrix products: 15.1 us -> none  [the longest x9 6.89 us: body(): jnp.dot(window, conv_weight[tap_index], preferred_element_type=jnp.float32)]
    all_to_all x2, blocking collectives: 43.9 us -> 33.5 us  [exchange(): lax.all_to_all(blocks, 'frames', split_axis=0, concat_axis=0, tiled=True)]
    pallas_call x0 -> x3, Pallas kernels: none -> 10.1 us  [the longest x1 4.28 us: body(): pl.pallas_call(conv_kernel, out_shape=jax.ShapeDtypeStruct((pixels, chans...]
    unnamed x10 -> x13, local copies, waits for them, and re-layouts: 0.03 us -> 7.09 us
    all_to_all x1 -> x2, waiting for transfers between devices: 12 us -> 17.7 us  [exchange(): lax.all_to_all(blocks, 'frames', split_axis=0, concat_axis=0, tiled=True)]
    reshape x2 -> x3, local copies, waits for them, and re-layouts: 6.21 us -> 1.38 us  [the longest x1 0.69 us: body(): gn_gain.reshape(1, chans)]
    slice x2 -> x0, local copies, waits for them, and re-layouts: 4.48 us -> none  [the longest x1 4.21 us: attend_block(): value_rows = shaped[:, :, :, 2]]
  transfers between devices with their start and end apart: 1 -> 2, of which waited for: 1 -> 2; matrix products, arithmetic and copies ran while one was open for 0% -> 2% of each run, Pallas kernels for 0% -> 0%
where the time goes in v1:
time: 75.5 us; the launch traced here: 75 us
  blocking collectives  33.5 us (44%)
  waiting for transfers between devices  17.7 us (23%)
  Pallas kernels  10.1 us (13%)
  local copies, waits for them, and re-layouts  8.47 us (11%)
  starting transfers between devices  5.13 us (7%)
    all_to_all x2, blocking collectives, exchange(): lax.all_to_all(blocks, 'frames', split_axis=0, concat_axis=0, tiled=True)  33.5 us
    all_to_all x2, waiting for transfers between devices, exchange(): lax.all_to_all(blocks, 'frames', split_axis=0, concat_axis=0, tiled=True)  17.7 us
    unnamed x13, local copies, waits for them, and re-layouts  7.09 us
    all_to_all x2, starting transfers between devices, exchange(): lax.all_to_all(blocks, 'frames', split_axis=0, concat_axis=0, tiled=True)  5.13 us
    pallas_call x1, Pallas kernels, body(): pl.pallas_call(conv_kernel, out_shape=jax.ShapeDtypeStruct((pixels, chans...  4.28 us
    pallas_call x1, Pallas kernels, body(): pl.pallas_call(functools.partial(attend_kernel, per_dev), out_shape=jax.S...  3.7 us
    pallas_call x1, Pallas kernels, body(): pl.pallas_call(join_kernel, out_shape=(jax.ShapeDtypeStruct((pixels, chan...  2.13 us
  transfers between devices with their start and end apart: 2, of which 2 were waited for; matrix products, arithmetic and copies ran while one was open for 2% of the time, Pallas kernels for 0%

profile of v1, /device:TPU:0, one launch (start us, length us, event | category | flops | bytes accessed | tf_op | source)
XLA Modules:
  0.0 75.0 jit_solution(1989499751137226199)
XLA Ops:
  0.0 0.0 copy-start.5
  0.0 19.4 %all_to_all.39 = bf16[32,8,640]{2,1,0:T(8,128)(2,1)S(1)} all-to-all(bf16[32,8,640]{2,1,0:T(8,128)(2,1)} %param.10), channel_id=1, replica_groups=mesh['groups'=1,'frames'=32] {'frames'}, dimensions={0} | all-to-all | bytes 655360 | tf_op jit(solution)/shard_map/all_to_all | solution.py:145
  19.4 0.0 copy-start.2
  19.4 1.1 %copy-done.2 = bf16[640,640]{1,0:T(8,128)(2,1)S(1)} copy-done((bf16[640,640]{1,0:T(8,128)(2,1)S(1)}, bf16[640,640]{1,0:T(8,128)(2,1)}, u32[]{:S(2)}) %copy-start.2) | copy-done | bytes 819224
  20.5 0.0 copy-start.4
  20.5 1.0 %copy-done.4 = bf16[1,256,640]{2,1,0:T(8,128)(2,1)S(1)} copy-done((bf16[1,256,640]{2,1,0:T(8,128)(2,1)S(1)}, bf16[1,256,640]{2,1,0:T(8,128)(2,1)}, u32[]{:S(2)}) %copy-start.4) | copy-done | bytes 327704
  21.5 2.1 %join.1 = (f32[256,640]{1,0:T(8,128)S(1)}, f32[32,128]{1,0:T(8,128)}) custom-call(bf16[256,640]{1,0:T(8,128)(2,1)S(1)} %bitcast.15, bf16[256,640]{1,0:T(8,128)(2,1)S(1)} %bitcast.12, bf16[640,640]{1,0:T(8,128)(2,1)S(1)} %copy-done.2), custom_call_target="tpu_custom_call" | custom-call | tf_op jit(solution)/shard_map/join/pallas_call | solution.py:159
  23.6 2.5 %all-to-all-start.1 = ((f32[32,1,128]{2,1,0:T(1,128)}), f32[32,1,128]{2,1,0:T(1,128)S(1)}, u32[]{:S(2)}, u32[]{:S(2)}) async-start(f32[32,1,128]{2,1,0:T(1,128)} %bitcast.3), calls=%async_computation.1 | async-start | bytes 32768 | tf_op jit(solution)/shard_map/all_to_all | solution.py:145
  26.2 0.7 reshape.24.gain_ref
  26.9 0.7 reshape.25.bias_ref
  27.6 5.7 %all-to-all-done.1 = f32[32,1,128]{2,1,0:T(1,128)S(1)} async-done(((f32[32,1,128]{2,1,0:T(1,128)}), f32[32,1,128]{2,1,0:T(1,128)S(1)}, u32[]{:S(2)}, u32[]{:S(2)}) %all-to-all-start.1) | async-done | bytes 16416 | tf_op jit(solution)/shard_map/all_to_all | solution.py:145
  33.3 0.0 copy-start
  33.3 3.1 %copy-done = bf16[9,640,640]{2,1,0:T(8,128)(2,1)S(1)} copy-done((bf16[9,640,640]{2,1,0:T(8,128)(2,1)S(1)}, bf16[9,640,640]{2,1,0:T(8,128)(2,1)}, u32[]{:S(2)}) %copy-start) | copy-done | bytes 7372824
  36.4 0.0 copy-start.1
  36.4 4.3 %conv.1 = bf16[256,640]{1,0:T(8,128)(2,1)} custom-call(s32[1]{0:T(128)} %constant.15.clone.1.clip_ref, f32[256,640]{1,0:T(8,128)S(1)} %get-tuple-element.7.joined_ref, f32[32,128]{1,0:T(8,128)S(1)} %bitcast.16, f32[1,640]{1,0:T(1,128)S(1)} %reshape.24.gain_ref, f32[1,640]{1,0:T(1,128)S(1)} %reshape.25.bias_ref, bf16[3,1920,640]{2,1,0:T(8,128)(2,1)S(1)} %bitcast.11), custom_call_target="tpu_custom_call" | custom-call | tf_op jit(solution)/shard_map/conv/pallas_call | solution.py:176
  40.7 2.6 %all-to-all-start.2 = ((bf16[32,8,640]{2,1,0:T(8,128)(2,1)}), bf16[32,8,640]{2,1,0:T(8,128)(2,1)S(1)}, u32[]{:S(2)}, u32[]{:S(2)}) async-start(bf16[32,8,640]{2,1,0:T(8,128)(2,1)} %bitcast.6), calls=%async_computation.2 | async-start | bytes 655360 | tf_op jit(solution)/shard_map/all_to_all | solution.py:145
  43.3 0.0 copy-done.5
  43.3 12.0 %all-to-all-done.2 = bf16[32,8,640]{2,1,0:T(8,128)(2,1)S(1)} async-done(((bf16[32,8,640]{2,1,0:T(8,128)(2,1)}), bf16[32,8,640]{2,1,0:T(8,128)(2,1)S(1)}, u32[]{:S(2)}, u32[]{:S(2)}) %all-to-all-start.2) | async-done | bytes 327712 | tf_op jit(solution)/shard_map/all_to_all | solution.py:145
  55.3 0.0 copy-done.1
  55.3 0.0 copy-start.3
  55.3 1.1 %copy-done.3 = bf16[640,640]{1,0:T(8,128)(2,1)S(1)} copy-done((bf16[640,640]{1,0:T(8,128)(2,1)S(1)}, bf16[640,640]{1,0:T(8,128)(2,1)}, u32[]{:S(2)}) %copy-start.3) | copy-done | bytes 819224
  56.4 3.7 %attend.1 = bf16[256,640]{1,0:T(8,128)(2,1)S(1)} custom-call(bf16[256,640]{1,0:T(8,128)(2,1)S(1)} %bitcast.13, f32[1,640]{1,0:T(1,128)S(1)} %reshape.27.gain_ref, bf16[640,1920]{1,0:T(8,128)(2,1)S(1)} %copy-done.1, bf16[640,640]{1,0:T(8,128)(2,1)S(1)} %copy-done.3), custom_call_target="tpu_custom_call" | custom-call | tf_op jit(solution)/shard_map/attend/pallas_call | solution.py:195
  60.2 14.1 %all_to_all.40 = bf16[32,8,640]{2,1,0:T(8,128)(2,1)S(1)} all-to-all(bf16[32,8,640]{2,1,0:T(8,128)(2,1)S(1)} %bitcast.14), channel_id=1, replica_groups=mesh['groups'=1,'frames'=32] {'frames'}, dimensions={0} | all-to-all | bytes 655360 | tf_op jit(solution)/shard_map/all_to_all | solution.py:145
  74.2 0.7 copy.12
  (1 shorter events, 0.0 us)
Async XLA Ops:
  0.0 43.3 %copy-start.5 = (f32[640]{0:T(1024)S(1)}, f32[640]{0:T(1024)}, u32[]{:S(2)}) copy-start(f32[640]{0:T(1024)} %param.15) | copy-start | bytes 7684
  19.4 1.1 %copy-start.2 = (bf16[640,640]{1,0:T(8,128)(2,1)S(1)}, bf16[640,640]{1,0:T(8,128)(2,1)}, u32[]{:S(2)}) copy-start(bf16[640,640]{1,0:T(8,128)(2,1)} %weight_ref.1) | copy-start | bytes 2457604
  20.5 1.0 %copy-start.4 = (bf16[1,256,640]{2,1,0:T(8,128)(2,1)S(1)}, bf16[1,256,640]{2,1,0:T(8,128)(2,1)}, u32[]{:S(2)}) copy-start(bf16[1,256,640]{2,1,0:T(8,128)(2,1)} %param.9) | copy-start | bytes 983044
  23.6 9.7 %all-to-all-start.1 = ((f32[32,1,128]{2,1,0:T(1,128)}), f32[32,1,128]{2,1,0:T(1,128)S(1)}, u32[]{:S(2)}, u32[]{:S(2)}) async-start(f32[32,1,128]{2,1,0:T(1,128)} %bitcast.3), calls=%async_computation.1 | async-start | bytes 32768 | tf_op jit(solution)/shard_map/all_to_all | solution.py:145
  33.3 3.1 %copy-start = (bf16[9,640,640]{2,1,0:T(8,128)(2,1)S(1)}, bf16[9,640,640]{2,1,0:T(8,128)(2,1)}, u32[]{:S(2)}) copy-start(bf16[9,640,640]{2,1,0:T(8,128)(2,1)} %param.14) | copy-start | bytes 22118404
  36.4 18.9 %copy-start.1 = (bf16[640,1920]{1,0:T(8,128)(2,1)S(1)}, bf16[640,1920]{1,0:T(8,128)(2,1)}, u32[]{:S(2)}) copy-start(bf16[640,1920]{1,0:T(8,128)(2,1)} %qkv_ref.1) | copy-start | bytes 7372804
  40.7 14.6 %all-to-all-start.2 = ((bf16[32,8,640]{2,1,0:T(8,128)(2,1)}), bf16[32,8,640]{2,1,0:T(8,128)(2,1)S(1)}, u32[]{:S(2)}, u32[]{:S(2)}) async-start(bf16[32,8,640]{2,1,0:T(8,128)(2,1)} %bitcast.6), calls=%async_computation.2 | async-start | bytes 655360 | tf_op jit(solution)/shard_map/all_to_all | solution.py:145
  55.3 1.1 %copy-start.3 = (bf16[640,640]{1,0:T(8,128)(2,1)S(1)}, bf16[640,640]{1,0:T(8,128)(2,1)}, u32[]{:S(2)}) copy-start(bf16[640,640]{1,0:T(8,128)(2,1)} %out_ref.1) | copy-start | bytes 2457604

commit v2 on v1

--- a/solution.py
+++ b/solution.py
@@ -84,7 +84,7 @@
     chan_var = exact_dot(lane_var, both_lanes, ((1,), (1,)))[:1]
     joined = joined_ref[...]
     scaled = (joined - chan_mean) * lax.rsqrt(chan_var + norm_epsilon)
-    activated = jax.nn.silu(scaled * gain_ref[...] + bias_ref[...])
+    activated = jax.nn.silu(scaled * gain_ref[...].reshape(1, chans) + bias_ref[...].reshape(1, chans))
     col = lax.rem(lax.broadcasted_iota(jnp.int32, (pixels, chans), 0), W)
     left = jnp.where(col == 0, 0.0, pltpu.roll(activated, 1, 0))
     right = jnp.where(col == W - 1, 0.0, pltpu.roll(activated, pixels - 1, 0))
@@ -110,7 +110,7 @@
     mean = jnp.mean(resid, axis=-1, keepdims=True)
     centred = resid - mean
     var = jnp.mean(jnp.square(centred), axis=-1, keepdims=True)
-    normed = (centred * lax.rsqrt(var + norm_epsilon) * gain_ref[...]).astype(BF16)
+    normed = (centred * lax.rsqrt(var + norm_epsilon) * gain_ref[...].reshape(1, chans)).astype(BF16)
     rows_ref[...] = jnp.dot(normed, qkv_ref[...], preferred_element_type=F32).astype(BF16)
     row = lax.broadcasted_iota(jnp.int32, (rows, rows), 0)
     col = lax.broadcasted_iota(jnp.int32, (rows, rows), 1)
@@ -141,6 +141,29 @@
     result_ref[...] = result.astype(BF16)
 
 
+def fetch_kernel(*refs):
+    count = len(refs) // 2
+    for i in range(count):
+        refs[count + i][...] = refs[i][...]
+
+
+def fetch(*arrays):
+    size = sum(a.size * a.dtype.itemsize for a in arrays)
+    return pl.pallas_call(
+        fetch_kernel,
+        out_shape=tuple(jax.ShapeDtypeStruct(a.shape, a.dtype) for a in arrays),
+        in_specs=[VMEM] * len(arrays),
+        out_specs=(VMEM,) * len(arrays),
+        compiler_params=params(1),
+        cost_estimate=cost(0, 2 * size),
+        name="fetch",
+    )(*arrays)
+
+
+def cost(flops, moved):
+    return pl.CostEstimate(flops=int(flops), bytes_accessed=int(moved), transcendentals=0)
+
+
 def exchange(blocks):
     return lax.all_to_all(blocks, "frames", split_axis=0, concat_axis=0, tiled=True)
 
@@ -153,6 +176,7 @@
     frame_count, per_dev, _ = control.shape
     rows = frame_count * per_dev
     own_control = exchange(control.reshape(rows, chans)).reshape(devices, f_dev, per_dev, chans)
+    skip, zero_weight = fetch(skip, zero_weight)
     first_frame = lax.axis_index("frames") * f_dev if frame_count > CLIP else jnp.int32(0)
     joined, stats = [], []
     for f in range(f_dev):
@@ -164,7 +188,8 @@
             ),
             in_specs=[VMEM] * 3,
             out_specs=(VMEM, VMEM),
-            compiler_params=params(12),
+            compiler_params=params(8),
+            cost_estimate=cost(2 * pixels * chans * chans, 32e6),
             name="join",
         )(skip[f], own_control[:, f].reshape(pixels, chans), zero_weight)
         joined.append(frame_joined)
@@ -179,14 +204,15 @@
                 in_specs=[SMEM] + [VMEM] * 5,
                 out_specs=VMEM,
                 scratch_shapes=[pltpu.VMEM((pixels + 2 * W, 3 * chans), BF16)],
-                compiler_params=params(24),
+                compiler_params=params(14),
+                cost_estimate=cost(18 * pixels * chans * chans, 9e6),
                 name="conv",
             )(
                 ((first_frame + f) // CLIP).reshape(1),
                 joined[f],
                 all_stats,
-                gn_gain.reshape(1, chans),
-                gn_bias.reshape(1, chans),
+                gn_gain,
+                gn_bias,
                 conv_weight.reshape(3, 3 * chans, chans),
             )
         )
@@ -198,9 +224,10 @@
         in_specs=[VMEM] * 4,
         out_specs=VMEM,
         scratch_shapes=[pltpu.VMEM((rows, 3 * chans), BF16), pltpu.VMEM((rows, chans), BF16)],
-        compiler_params=params(24),
+        compiler_params=params(14),
+        cost_estimate=cost(8 * rows * chans * chans, 4e6),
         name="attend",
-    )(by_pixel, ln_gain.reshape(1, chans), qkv_weight, out_weight)
+    )(by_pixel, ln_gain, qkv_weight, out_weight)
     output = exchange(result).reshape(devices, f_dev, per_dev, chans)
     return output.transpose(1, 0, 2, 3).reshape(f_dev, pixels, chans)
 

time: 75.5 us -> 72.2 us (0.956)
  waiting for transfers between devices: 17.7 us -> 8.91 us
  blocking collectives: 33.5 us -> 37.2 us
  starting transfers between devices: 5.13 us -> 7.33 us
  Pallas kernels: 10.1 us -> 8.86 us
  local copies, waits for them, and re-layouts: 8.47 us -> 9.44 us
    all_to_all x2 -> x1, waiting for transfers between devices: 17.7 us -> 8.91 us  [exchange(): lax.all_to_all(blocks, 'frames', split_axis=0, concat_axis=0, tiled=True)]
    all_to_all x2 -> x3, blocking collectives: 33.5 us -> 37.2 us  [exchange(): lax.all_to_all(blocks, 'frames', split_axis=0, concat_axis=0, tiled=True)]
    unnamed x13 -> x21, local copies, waits for them, and re-layouts: 7.09 us -> 9.44 us
    all_to_all x2 -> x1, starting transfers between devices: 5.13 us -> 7.33 us  [exchange(): lax.all_to_all(blocks, 'frames', split_axis=0, concat_axis=0, tiled=True)]
    reshape x3 -> x0, local copies, waits for them, and re-layouts: 1.38 us -> none  [the longest x1 0.69 us: body(): gn_gain.reshape(1, chans)]
  transfers between devices with their start and end apart: 2 -> 1, of which waited for: 2 -> 1; matrix products, arithmetic and copies ran while one was open for 2% -> 0% of each run, Pallas kernels for 0% -> 0%
where the time goes in v2:
time: 72.2 us; the launch traced here: 71.8 us
  blocking collectives  37.2 us (52%)
  local copies, waits for them, and re-layouts  9.44 us (13%)
  waiting for transfers between devices  8.91 us (12%)
  Pallas kernels  8.86 us (12%)
  starting transfers between devices  7.33 us (10%)
    all_to_all x3, blocking collectives, exchange(): lax.all_to_all(blocks, 'frames', split_axis=0, concat_axis=0, tiled=True)  37.2 us
    unnamed x21, local copies, waits for them, and re-layouts  9.44 us
    all_to_all x1, waiting for transfers between devices, exchange(): lax.all_to_all(blocks, 'frames', split_axis=0, concat_axis=0, tiled=True)  8.91 us
    all_to_all x1, starting transfers between devices, exchange(): lax.all_to_all(blocks, 'frames', split_axis=0, concat_axis=0, tiled=True)  7.33 us
    pallas_call x1, Pallas kernels, body(): pl.pallas_call(functools.partial(attend_kernel, per_dev), out_shape=jax.S...  3.7 us
    pallas_call x1, Pallas kernels, body(): pl.pallas_call(conv_kernel, out_shape=jax.ShapeDtypeStruct((pixels, chans...  3.57 us
    pallas_call x1, Pallas kernels, body(): pl.pallas_call(join_kernel, out_shape=(jax.ShapeDtypeStruct((pixels, chan...  1.5 us
  transfers between devices with their start and end apart: 1, of which 1 were waited for; matrix products, arithmetic and copies ran while one was open for 0% of the time, Pallas kernels for 0%

profile of v2, /device:TPU:0, one launch (start us, length us, event | category | flops | bytes accessed | tf_op | source)
XLA Modules:
  0.0 71.8 jit_solution(14322845993596620355)
XLA Ops:
  0.0 0.0 copy-start.1
  0.0 7.3 %all-to-all-start = ((bf16[32,8,640]{2,1,0:T(8,128)(2,1)}), bf16[32,8,640]{2,1,0:T(8,128)(2,1)S(1)}, u32[]{:S(2)}, u32[]{:S(2)}) async-start(bf16[32,8,640]{2,1,0:T(8,128)(2,1)} %param.10), calls=%async_computation | async-start | bytes 655360 | tf_op jit(solution)/shard_map/all_to_all | solution.py:168
  7.3 0.0 copy-start.3
  7.3 1.1 %copy-done.3 = bf16[640,640]{1,0:T(8,128)(2,1)S(1)} copy-done((bf16[640,640]{1,0:T(8,128)(2,1)S(1)}, bf16[640,640]{1,0:T(8,128)(2,1)}, u32[]{:S(2)}) %copy-start.3) | copy-done | bytes 819224
  8.5 0.0 copy-start.6
  8.5 1.0 %copy-done.6 = bf16[1,256,640]{2,1,0:T(8,128)(2,1)S(1)} copy-done((bf16[1,256,640]{2,1,0:T(8,128)(2,1)S(1)}, bf16[1,256,640]{2,1,0:T(8,128)(2,1)}, u32[]{:S(2)}) %copy-start.6) | copy-done | bytes 327704
  9.5 0.1 fetch.1
  9.6 0.0 copy-start.4
  9.6 0.9 %copy-done.4 = bf16[640,640]{1,0:T(8,128)(2,1)} copy-done((bf16[640,640]{1,0:T(8,128)(2,1)}, bf16[640,640]{1,0:T(8,128)(2,1)S(1)}, u32[]{:S(2)}) %copy-start.4) | copy-done | bytes 819224
  10.5 8.9 %all-to-all-done = bf16[32,8,640]{2,1,0:T(8,128)(2,1)S(1)} async-done(((bf16[32,8,640]{2,1,0:T(8,128)(2,1)}), bf16[32,8,640]{2,1,0:T(8,128)(2,1)S(1)}, u32[]{:S(2)}, u32[]{:S(2)}) %all-to-all-start) | async-done | bytes 327712 | tf_op jit(solution)/shard_map/all_to_all | solution.py:168
  19.4 0.0 copy-start.2
  19.4 0.0 copy-start.5
  19.4 1.2 %copy-done.5 = bf16[640,640]{1,0:T(8,128)(2,1)S(1)} copy-done((bf16[640,640]{1,0:T(8,128)(2,1)S(1)}, bf16[640,640]{1,0:T(8,128)(2,1)}, u32[]{:S(2)}) %copy-start.5) | copy-done | bytes 819224
  20.6 0.0 copy-start.9
  20.6 1.5 %join.1 = (f32[256,640]{1,0:T(8,128)S(1)}, f32[32,128]{1,0:T(8,128)S(1)}) custom-call(bf16[256,640]{1,0:T(8,128)(2,1)S(1)} %bitcast.16, bf16[256,640]{1,0:T(8,128)(2,1)S(1)} %bitcast.15, bf16[640,640]{1,0:T(8,128)(2,1)S(1)} %copy-done.5), custom_call_target="tpu_custom_call" | custom-call | flops 209715200 | bytes 32000000 | tf_op jit(solution)/shard_map/join/pallas_call | solution.py:183
  22.1 9.3 %all_to_all.39 = f32[32,1,128]{2,1,0:T(1,128)S(1)} all-to-all(f32[32,1,128]{2,1,0:T(1,128)S(1)} %bitcast.18), channel_id=1, replica_groups=mesh['groups'=1,'frames'=32] {'frames'}, dimensions={0} | all-to-all | bytes 32768 | tf_op jit(solution)/shard_map/all_to_all | solution.py:168
  31.4 0.0 copy-start
  31.4 3.1 %copy-done = bf16[9,640,640]{2,1,0:T(8,128)(2,1)S(1)} copy-done((bf16[9,640,640]{2,1,0:T(8,128)(2,1)S(1)}, bf16[9,640,640]{2,1,0:T(8,128)(2,1)}, u32[]{:S(2)}) %copy-start) | copy-done | bytes 7372824
  34.5 0.0 copy-start.7
  34.5 0.7 copy-done.7
  35.2 0.0 copy-start.8
  35.2 0.7 copy-done.8
  35.9 3.6 %conv.1 = bf16[256,640]{1,0:T(8,128)(2,1)S(1)} custom-call(s32[1]{0:T(128)} %constant.15.clone.1.clip_ref, f32[256,640]{1,0:T(8,128)S(1)} %get-tuple-element.11.joined_ref, f32[32,128]{1,0:T(8,128)S(1)} %bitcast.17, f32[640]{0:T(1024)S(1)} %copy-done.7, f32[640]{0:T(1024)S(1)} %copy-done.8, bf16[3,1920,640]{2,1,0:T(8,128)(2,1)S(1)} %bitcast.11), custom_call_target="tpu_custom_call" | custom-call | flops 1887436800 | bytes 9000000 | tf_op jit(solution)/shard_map/conv/pallas_call | solution.py:201
  39.5 13.8 %all_to_all.40 = bf16[32,8,640]{2,1,0:T(8,128)(2,1)S(1)} all-to-all(bf16[32,8,640]{2,1,0:T(8,128)(2,1)S(1)} %bitcast.12), channel_id=1, replica_groups=mesh['groups'=1,'frames'=32] {'frames'}, dimensions={0} | all-to-all | bytes 655360 | tf_op jit(solution)/shard_map/all_to_all | solution.py:168
  53.2 0.0 copy-done.1
  53.2 0.0 copy-done.2
  53.2 0.0 copy-done.9
  53.3 3.7 %attend.1 = bf16[256,640]{1,0:T(8,128)(2,1)S(1)} custom-call(bf16[256,640]{1,0:T(8,128)(2,1)S(1)} %bitcast.13, f32[640]{0:T(1024)S(1)} %copy-done.9, bf16[640,1920]{1,0:T(8,128)(2,1)S(1)} %copy-done.1, bf16[640,640]{1,0:T(8,128)(2,1)S(1)} %copy-done.2), custom_call_target="tpu_custom_call" | custom-call | flops 838860800 | bytes 4000000 | tf_op jit(solution)/shard_map/attend/pallas_call | solution.py:221
  57.0 14.1 %all_to_all.41 = bf16[32,8,640]{2,1,0:T(8,128)(2,1)S(1)} all-to-all(bf16[32,8,640]{2,1,0:T(8,128)(2,1)S(1)} %bitcast.14), channel_id=1, replica_groups=mesh['groups'=1,'frames'=32] {'frames'}, dimensions={0} | all-to-all | bytes 655360 | tf_op jit(solution)/shard_map/all_to_all | solution.py:168
  71.1 0.7 %copy.12 = bf16[1,256,640]{2,1,0:T(8,128)(2,1)} copy(bf16[1,256,640]{2,1,0:T(8,128)(2,1)S(1)} %bitcast.19) | data formatting | bytes 655360
Async XLA Ops:
  0.0 53.2 %copy-start.1 = (bf16[640,1920]{1,0:T(8,128)(2,1)S(1)}, bf16[640,1920]{1,0:T(8,128)(2,1)}, u32[]{:S(2)}) copy-start(bf16[640,1920]{1,0:T(8,128)(2,1)} %qkv_ref.1) | copy-start | bytes 7372804
  0.0 19.4 %all-to-all-start = ((bf16[32,8,640]{2,1,0:T(8,128)(2,1)}), bf16[32,8,640]{2,1,0:T(8,128)(2,1)S(1)}, u32[]{:S(2)}, u32[]{:S(2)}) async-start(bf16[32,8,640]{2,1,0:T(8,128)(2,1)} %param.10), calls=%async_computation | async-start | bytes 655360 | tf_op jit(solution)/shard_map/all_to_all | solution.py:168
  7.3 1.1 %copy-start.3 = (bf16[640,640]{1,0:T(8,128)(2,1)S(1)}, bf16[640,640]{1,0:T(8,128)(2,1)}, u32[]{:S(2)}) copy-start(bf16[640,640]{1,0:T(8,128)(2,1)} %refs_1_.1) | copy-start | bytes 2457604
  8.5 1.0 %copy-start.6 = (bf16[1,256,640]{2,1,0:T(8,128)(2,1)S(1)}, bf16[1,256,640]{2,1,0:T(8,128)(2,1)}, u32[]{:S(2)}) copy-start(bf16[1,256,640]{2,1,0:T(8,128)(2,1)} %refs_0_.1) | copy-start | bytes 983044
  9.6 0.9 %copy-start.4 = (bf16[640,640]{1,0:T(8,128)(2,1)}, bf16[640,640]{1,0:T(8,128)(2,1)S(1)}, u32[]{:S(2)}) copy-start(bf16[640,640]{1,0:T(8,128)(2,1)S(1)} %get-tuple-element.10.weight_ref) | copy-start | bytes 2457604
  19.4 33.9 %copy-start.2 = (bf16[640,640]{1,0:T(8,128)(2,1)S(1)}, bf16[640,640]{1,0:T(8,128)(2,1)}, u32[]{:S(2)}) copy-start(bf16[640,640]{1,0:T(8,128)(2,1)} %out_ref.1) | copy-start | bytes 2457604
  19.4 1.2 %copy-start.5 = (bf16[640,640]{1,0:T(8,128)(2,1)S(1)}, bf16[640,640]{1,0:T(8,128)(2,1)}, u32[]{:S(2)}) copy-start(bf16[640,640]{1,0:T(8,128)(2,1)} %copy-done.4) | copy-start | bytes 2457604
  20.6 32.6 %copy-start.9 = (f32[640]{0:T(1024)S(1)}, f32[640]{0:T(1024)}, u32[]{:S(2)}) copy-start(f32[640]{0:T(1024)} %gain_ref.3) | copy-start | bytes 7684
  31.4 3.1 %copy-start = (bf16[9,640,640]{2,1,0:T(8,128)(2,1)S(1)}, bf16[9,640,640]{2,1,0:T(8,128)(2,1)}, u32[]{:S(2)}) copy-start(bf16[9,640,640]{2,1,0:T(8,128)(2,1)} %param.14) | copy-start | bytes 22118404
  34.5 0.7 copy-start.7
  35.2 0.7 copy-start.8

commit v3 on v2

--- a/solution.py
+++ b/solution.py
@@ -57,8 +57,15 @@
 
 
 def conv_kernel(
-    clip_ref, joined_ref, stats_ref, gain_ref, bias_ref, weight_ref, resid_ref, window_ref
+    clip_ref, joined_ref, stats_ref, gains_ref, weight_hbm, resid_ref, sent_ref, window_ref,
+    weight_ref, sems,
 ):
+    copies = [
+        pltpu.make_async_copy(weight_hbm.at[tap], weight_ref.at[tap], sems.at[tap])
+        for tap in range(9)
+    ]
+    for copy in copies:
+        copy.start()
     pixels, chans = joined_ref.shape
     frames = stats_ref.shape[0]
     per_frame = float(pixels * (chans // GROUPS))
@@ -84,7 +91,7 @@
     chan_var = exact_dot(lane_var, both_lanes, ((1,), (1,)))[:1]
     joined = joined_ref[...]
     scaled = (joined - chan_mean) * lax.rsqrt(chan_var + norm_epsilon)
-    activated = jax.nn.silu(scaled * gain_ref[...].reshape(1, chans) + bias_ref[...].reshape(1, chans))
+    activated = jax.nn.silu(scaled * gains_ref[:1] + gains_ref[1:2])
     col = lax.rem(lax.broadcasted_iota(jnp.int32, (pixels, chans), 0), W)
     left = jnp.where(col == 0, 0.0, pltpu.roll(activated, 1, 0))
     right = jnp.where(col == W - 1, 0.0, pltpu.roll(activated, pixels - 1, 0))
@@ -96,21 +103,24 @@
     window_ref[W : W + pixels, 2 * chans :] = right.astype(BF16)
     total = joined
     for shift in range(3):
+        for copy in copies[3 * shift : 3 * shift + 3]:
+            copy.wait()
         total = total + jnp.dot(
             window_ref[shift * W : shift * W + pixels],
-            weight_ref[shift],
+            weight_ref[3 * shift : 3 * shift + 3].reshape(3 * chans, chans),
             preferred_element_type=F32,
         )
-    resid_ref[...] = total.astype(BF16)
-
-
-def attend_kernel(per_dev, resid_ref, gain_ref, qkv_ref, out_ref, result_ref, rows_ref, mixed_ref):
+    resid_ref[...] = total
+    sent_ref[...] = total.astype(BF16)
+
+
+def attend_kernel(per_dev, resid_ref, gains_ref, qkv_ref, out_ref, result_ref, rows_ref, mixed_ref):
     rows, chans = resid_ref.shape
     resid = resid_ref[...].astype(F32)
     mean = jnp.mean(resid, axis=-1, keepdims=True)
     centred = resid - mean
     var = jnp.mean(jnp.square(centred), axis=-1, keepdims=True)
-    normed = (centred * lax.rsqrt(var + norm_epsilon) * gain_ref[...].reshape(1, chans)).astype(BF16)
+    normed = (centred * lax.rsqrt(var + norm_epsilon) * gains_ref[2:3]).astype(BF16)
     rows_ref[...] = jnp.dot(normed, qkv_ref[...], preferred_element_type=F32).astype(BF16)
     row = lax.broadcasted_iota(jnp.int32, (rows, rows), 0)
     col = lax.broadcasted_iota(jnp.int32, (rows, rows), 1)
@@ -137,7 +147,7 @@
             weights = (expon / jnp.sum(expon, axis=-1, keepdims=True)).astype(BF16)
             mixed = mixed + jnp.dot(weights, head_values, preferred_element_type=F32)
         mixed_ref[:, start : start + LANES] = mixed.astype(BF16)
-    result = resid + jnp.dot(mixed_ref[...], out_ref[...], preferred_element_type=F32)
+    result = jnp.dot(mixed_ref[...], out_ref[...], preferred_element_type=F32)
     result_ref[...] = result.astype(BF16)
 
 
@@ -176,7 +186,7 @@
     frame_count, per_dev, _ = control.shape
     rows = frame_count * per_dev
     own_control = exchange(control.reshape(rows, chans)).reshape(devices, f_dev, per_dev, chans)
-    skip, zero_weight = fetch(skip, zero_weight)
+    skip, gains = fetch(skip, jnp.stack((gn_gain, gn_bias, ln_gain)))
     first_frame = lax.axis_index("frames") * f_dev if frame_count > CLIP else jnp.int32(0)
     joined, stats = [], []
     for f in range(f_dev):
@@ -195,28 +205,28 @@
         joined.append(frame_joined)
         stats.append(frame_stats)
     all_stats = exchange(jnp.stack(stats, axis=1).reshape(devices * f_dev, LANES))
-    resid = []
+    resid, sent = [], []
     for f in range(f_dev):
-        resid.append(
-            pl.pallas_call(
-                conv_kernel,
-                out_shape=jax.ShapeDtypeStruct((pixels, chans), BF16),
-                in_specs=[SMEM] + [VMEM] * 5,
-                out_specs=VMEM,
-                scratch_shapes=[pltpu.VMEM((pixels + 2 * W, 3 * chans), BF16)],
-                compiler_params=params(14),
-                cost_estimate=cost(18 * pixels * chans * chans, 9e6),
-                name="conv",
-            )(
-                ((first_frame + f) // CLIP).reshape(1),
-                joined[f],
-                all_stats,
-                gn_gain,
-                gn_bias,
-                conv_weight.reshape(3, 3 * chans, chans),
-            )
-        )
-    by_pixel = jnp.stack(resid).reshape(f_dev, devices, per_dev, chans)
+        frame_resid, frame_sent = pl.pallas_call(
+            conv_kernel,
+            out_shape=(
+                jax.ShapeDtypeStruct((pixels, chans), F32),
+                jax.ShapeDtypeStruct((pixels, chans), BF16),
+            ),
+            in_specs=[SMEM] + [VMEM] * 3 + [pl.BlockSpec(memory_space=pl.ANY)],
+            out_specs=(VMEM, VMEM),
+            scratch_shapes=[
+                pltpu.VMEM((pixels + 2 * W, 3 * chans), BF16),
+                pltpu.VMEM(conv_weight.shape, BF16),
+                pltpu.SemaphoreType.DMA((9,)),
+            ],
+            compiler_params=params(50),
+            cost_estimate=cost(18 * pixels * chans * chans, 9e6),
+            name="conv",
+        )(((first_frame + f) // CLIP).reshape(1), joined[f], all_stats, gains, conv_weight)
+        resid.append(frame_resid)
+        sent.append(frame_sent)
+    by_pixel = jnp.stack(sent).reshape(f_dev, devices, per_dev, chans)
     by_pixel = exchange(by_pixel.transpose(1, 0, 2, 3).reshape(rows, chans))
     result = pl.pallas_call(
         functools.partial(attend_kernel, per_dev),
@@ -227,9 +237,10 @@
         compiler_params=params(14),
         cost_estimate=cost(8 * rows * chans * chans, 4e6),
         name="attend",
-    )(by_pixel, ln_gain, qkv_weight, out_weight)
-    output = exchange(result).reshape(devices, f_dev, per_dev, chans)
-    return output.transpose(1, 0, 2, 3).reshape(f_dev, pixels, chans)
+    )(by_pixel, gains, qkv_weight, out_weight)
+    mixed = exchange(result).reshape(devices, f_dev, per_dev, chans)
+    mixed = mixed.transpose(1, 0, 2, 3).reshape(f_dev, pixels, chans)
+    return (jnp.stack(resid) + mixed.astype(F32)).astype(BF16)
 
 
 def solution(mesh):

time: 72.2 us -> 68.9 us (0.954)
  local copies, waits for them, and re-layouts: 9.44 us -> 4.26 us
  Pallas kernels: 8.86 us -> 9.92 us
  other arithmetic: 0 us -> 0.8 us
    unnamed x21 -> x8, local copies, waits for them, and re-layouts: 9.44 us -> 2.2 us
    another operation x0 -> x3, local copies, waits for them, and re-layouts: none -> 2.07 us  [body(): skip, gains = fetch(skip, jnp.stack((gn_gain, gn_bias, ln_gain)))]
    pallas_call x1, Pallas kernels: 3.57 us -> 4.7 us  [body(): pl.pallas_call(conv_kernel, out_shape=(jax.ShapeDtypeStruct((pixels, chan...]
    convert_element_type x0 -> x1, other arithmetic: none -> 0.78 us  [body(): return (jnp.stack(resid) + mixed.astype(F32)).astype(BF16)]
  transfers between devices with their start and end apart: 1 -> 1, of which waited for: 1 -> 1; matrix products, arithmetic and copies ran while one was open for 0% -> 3% of each run, Pallas kernels for 0% -> 0%
where the time goes in v3:
time: 68.9 us; the launch traced here: 68.5 us
  blocking collectives  37.2 us (54%)
  Pallas kernels  9.92 us (14%)
  waiting for transfers between devices  8.95 us (13%)
  starting transfers between devices  7.33 us (11%)
  local copies, waits for them, and re-layouts  4.26 us (6%)
  other arithmetic  0.8 us (1%)
    all_to_all x3, blocking collectives, exchange(): lax.all_to_all(blocks, 'frames', split_axis=0, concat_axis=0, tiled=True)  37.2 us
    all_to_all x1, waiting for transfers between devices, exchange(): lax.all_to_all(blocks, 'frames', split_axis=0, concat_axis=0, tiled=True)  8.95 us
    all_to_all x1, starting transfers between devices, exchange(): lax.all_to_all(blocks, 'frames', split_axis=0, concat_axis=0, tiled=True)  7.33 us
    pallas_call x1, Pallas kernels, body(): pl.pallas_call(conv_kernel, out_shape=(jax.ShapeDtypeStruct((pixels, chan...  4.7 us
    pallas_call x1, Pallas kernels, body(): pl.pallas_call(functools.partial(attend_kernel, per_dev), out_shape=jax.S...  3.7 us
    unnamed x8, local copies, waits for them, and re-layouts  2.2 us
    another operation x3, local copies, waits for them, and re-layouts, body(): skip, gains = fetch(skip, jnp.stack((gn_gain, gn_bias, ln_gain)))  2.07 us
    pallas_call x1, Pallas kernels, body(): pl.pallas_call(join_kernel, out_shape=(jax.ShapeDtypeStruct((pixels, chan...  1.5 us
  transfers between devices with their start and end apart: 1, of which 1 were waited for; matrix products, arithmetic and copies ran while one was open for 3% of the time, Pallas kernels for 0%

profile of v3, /device:TPU:0, one launch (start us, length us, event | category | flops | bytes accessed | tf_op | source)
XLA Modules:
  0.0 68.5 jit_solution(15228139251687528073)
XLA Ops:
  0.0 0.0 copy-start
  0.0 7.3 %all-to-all-start = ((bf16[32,8,640]{2,1,0:T(8,128)(2,1)}), bf16[32,8,640]{2,1,0:T(8,128)(2,1)S(1)}, u32[]{:S(2)}, u32[]{:S(2)}) async-start(bf16[32,8,640]{2,1,0:T(8,128)(2,1)} %param.10), calls=%async_computation | async-start | bytes 655360 | tf_op jit(solution)/shard_map/all_to_all | solution.py:178
  7.3 0.7 %stack.13 = f32[1,640]{1,0:T(1,128)S(1)} reshape(f32[640]{0:T(1024)} %param.12) | data formatting | bytes 5120 | tf_op jit(solution)/shard_map/stack | solution.py:189
  8.0 0.7 %stack.14 = f32[1,640]{1,0:T(1,128)S(1)} reshape(f32[640]{0:T(1024)} %param.13) | data formatting | bytes 5120 | tf_op jit(solution)/shard_map/stack | solution.py:189
  8.7 0.7 %stack.15 = f32[1,640]{1,0:T(1,128)S(1)} reshape(f32[640]{0:T(1024)} %param.15) | data formatting | bytes 5120 | tf_op jit(solution)/shard_map/stack | solution.py:189
  9.4 0.0 copy-start.3
  9.4 1.0 %copy-done.3 = bf16[1,256,640]{2,1,0:T(8,128)(2,1)S(1)} copy-done((bf16[1,256,640]{2,1,0:T(8,128)(2,1)S(1)}, bf16[1,256,640]{2,1,0:T(8,128)(2,1)}, u32[]{:S(2)}) %copy-start.3) | copy-done | bytes 327704
  10.4 8.9 %all-to-all-done = bf16[32,8,640]{2,1,0:T(8,128)(2,1)S(1)} async-done(((bf16[32,8,640]{2,1,0:T(8,128)(2,1)}), bf16[32,8,640]{2,1,0:T(8,128)(2,1)S(1)}, u32[]{:S(2)}, u32[]{:S(2)}) %all-to-all-start) | async-done | bytes 327712 | tf_op jit(solution)/shard_map/all_to_all | solution.py:178
  19.4 0.0 copy-start.1
  19.4 0.0 copy-start.2
  19.4 1.2 %copy-done.2 = bf16[640,640]{1,0:T(8,128)(2,1)S(1)} copy-done((bf16[640,640]{1,0:T(8,128)(2,1)S(1)}, bf16[640,640]{1,0:T(8,128)(2,1)}, u32[]{:S(2)}) %copy-start.2) | copy-done | bytes 819224
  20.6 1.5 %join.1 = (f32[256,640]{1,0:T(8,128)S(1)}, f32[32,128]{1,0:T(8,128)S(1)}) custom-call(bf16[256,640]{1,0:T(8,128)(2,1)S(1)} %bitcast.18, bf16[256,640]{1,0:T(8,128)(2,1)S(1)} %bitcast.16, bf16[640,640]{1,0:T(8,128)(2,1)S(1)} %copy-done.2), custom_call_target="tpu_custom_call" | custom-call | flops 209715200 | bytes 32000000 | tf_op jit(solution)/shard_map/join/pallas_call | solution.py:193
  22.1 9.3 %all_to_all.39 = f32[32,1,128]{2,1,0:T(1,128)S(1)} all-to-all(f32[32,1,128]{2,1,0:T(1,128)S(1)} %bitcast.20), channel_id=1, replica_groups=mesh['groups'=1,'frames'=32] {'frames'}, dimensions={0} | all-to-all | bytes 32768 | tf_op jit(solution)/shard_map/all_to_all | solution.py:178
  31.4 4.7 %conv.1 = (f32[256,640]{1,0:T(8,128)S(1)}, bf16[256,640]{1,0:T(8,128)(2,1)S(1)}) custom-call(s32[1]{0:T(128)} %constant.15.clone.1.clip_ref, f32[256,640]{1,0:T(8,128)S(1)} %get-tuple-element.12.joined_ref, f32[32,128]{1,0:T(8,128)S(1)} %bitcast.19, f32[3,640]{1,0:T(4,128)S(1)} %get-tuple-element.14.gains_ref, bf16[9,640,640]{2,1,0:T(8,128)(2,1)} %weight_hbm.1), custom_call_target="tpu_custom_call" | custom-call | flops 1887436800 | bytes 9000000 | tf_op jit(solution)/shard_map/conv/pallas_call | solution.py:210
  36.1 13.8 %all_to_all.40 = bf16[32,8,640]{2,1,0:T(8,128)(2,1)S(1)} all-to-all(bf16[32,8,640]{2,1,0:T(8,128)(2,1)S(1)} %bitcast.17), channel_id=1, replica_groups=mesh['groups'=1,'frames'=32] {'frames'}, dimensions={0} | all-to-all | bytes 655360 | tf_op jit(solution)/shard_map/all_to_all | solution.py:178
  49.9 0.0 copy-done
  49.9 0.0 copy-done.1
  49.9 3.7 %attend.1 = bf16[256,640]{1,0:T(8,128)(2,1)S(1)} custom-call(bf16[256,640]{1,0:T(8,128)(2,1)S(1)} %bitcast.14, f32[3,640]{1,0:T(4,128)S(1)} %get-tuple-element.14.gains_ref, bf16[640,1920]{1,0:T(8,128)(2,1)S(1)} %copy-done, bf16[640,640]{1,0:T(8,128)(2,1)S(1)} %copy-done.1), custom_call_target="tpu_custom_call" | custom-call | flops 838860800 | bytes 4000000 | tf_op jit(solution)/shard_map/attend/pallas_call | solution.py:231
  53.6 14.1 %all_to_all.41 = bf16[32,8,640]{2,1,0:T(8,128)(2,1)S(1)} all-to-all(bf16[32,8,640]{2,1,0:T(8,128)(2,1)S(1)} %bitcast.15), channel_id=1, replica_groups=mesh['groups'=1,'frames'=32] {'frames'}, dimensions={0} | all-to-all | bytes 655360 | tf_op jit(solution)/shard_map/all_to_all | solution.py:178
  67.7 0.8 %fusion.1 = bf16[1,256,640]{2,1,0:T(8,128)(2,1)} fusion(f32[256,640]{1,0:T(8,128)S(1)} %get-tuple-element.15, bf16[32,8,640]{2,1,0:T(8,128)(2,1)S(1)} %all_to_all.41), kind=kLoop, calls=%fused_computation.2 | loop fusion | flops 491520 | bytes 1310720 | tf_op jit(solution)/shard_map/convert_element_type | solution.py:243
  (2 shorter events, 0.0 us)
Async XLA Ops:
  0.0 49.9 %copy-start = (bf16[640,1920]{1,0:T(8,128)(2,1)S(1)}, bf16[640,1920]{1,0:T(8,128)(2,1)}, u32[]{:S(2)}) copy-start(bf16[640,1920]{1,0:T(8,128)(2,1)} %qkv_ref.1) | copy-start | bytes 7372804
  0.0 19.4 %all-to-all-start = ((bf16[32,8,640]{2,1,0:T(8,128)(2,1)}), bf16[32,8,640]{2,1,0:T(8,128)(2,1)S(1)}, u32[]{:S(2)}, u32[]{:S(2)}) async-start(bf16[32,8,640]{2,1,0:T(8,128)(2,1)} %param.10), calls=%async_computation | async-start | bytes 655360 | tf_op jit(solution)/shard_map/all_to_all | solution.py:178
  9.4 1.0 %copy-start.3 = (bf16[1,256,640]{2,1,0:T(8,128)(2,1)S(1)}, bf16[1,256,640]{2,1,0:T(8,128)(2,1)}, u32[]{:S(2)}) copy-start(bf16[1,256,640]{2,1,0:T(8,128)(2,1)} %refs_0_.1) | copy-start | bytes 983044
  19.4 30.5 %copy-start.1 = (bf16[640,640]{1,0:T(8,128)(2,1)S(1)}, bf16[640,640]{1,0:T(8,128)(2,1)}, u32[]{:S(2)}) copy-start(bf16[640,640]{1,0:T(8,128)(2,1)} %out_ref.1) | copy-start | bytes 2457604
  19.4 1.2 %copy-start.2 = (bf16[640,640]{1,0:T(8,128)(2,1)S(1)}, bf16[640,640]{1,0:T(8,128)(2,1)}, u32[]{:S(2)}) copy-start(bf16[640,640]{1,0:T(8,128)(2,1)} %weight_ref.1) | copy-start | bytes 2457604

commit v4 on v3

v4 whole, which is shorter than its diff:
```python
import functools
import math

import jax
import jax.numpy as jnp
from jax import lax
from jax.experimental import pallas as pl
from jax.experimental.pallas import tpu as pltpu
from jax.sharding import PartitionSpec as P

HEADS = 10
HD = 64
GROUPS = 32
CLIP = 32
W = 32
LANES = 128

norm_epsilon = 1e-05
F32 = jnp.float32
BF16 = jnp.bfloat16
VMEM = pl.BlockSpec(memory_space=pltpu.VMEM)
SMEM = pl.BlockSpec(memory_space=pltpu.SMEM)


def params(mib):
    return pltpu.CompilerParams(vmem_limit_bytes=mib * 1024 * 1024)


def member_dot(left, members):
    rows = left.shape[0]
    parts, rest = [], left
    for _ in range(3):
        part = rest.astype(BF16)
        parts.append(part.astype(F32))
        rest = rest - parts[-1]
    stacked = jnp.concatenate(parts).astype(BF16)
    product = jnp.dot(stacked, members, preferred_element_type=F32)
    return product[:rows] + product[rows : 2 * rows] + product[2 * rows :]


def group_members(chans, axis):
    size = chans // GROUPS
    first = lax.rem(lax.broadcasted_iota(jnp.int32, (LANES, LANES), 1 - axis), GROUPS) * size
    inner = lax.broadcasted_iota(jnp.int32, (LANES, LANES), axis) - first
    blocks = []
    for start in range(0, chans, LANES):
        place = inner + start
        blocks.append(jnp.where((place >= 0) & (place < size), 1.0, 0.0).astype(BF16))
    return jnp.concatenate(blocks, axis=axis)


def join_kernel(
    skip_ref, control_ref, weight_ref, conv_hbm, joined_ref, stats_ref, conv_ref, sem
):
    copy = pltpu.make_async_copy(conv_hbm.at[pl.ds(0, 3)], conv_ref, sem)
    copy.start()
    pixels, chans = skip_ref.shape
    zero_out = jnp.dot(control_ref[...], weight_ref[...], preferred_element_type=F32).astype(BF16)
    joined = skip_ref[...].astype(F32) + zero_out.astype(F32)
    joined_ref[...] = joined
    members = group_members(chans, 0)
    sums = jnp.broadcast_to(jnp.sum(joined, axis=0, keepdims=True), (8, chans))
    group_sums = member_dot(sums, members)
    lane_id = lax.broadcasted_iota(jnp.int32, (8, LANES), 1)
    group_mean = jnp.where(lane_id < GROUPS, group_sums, 0.0)
    group_mean = group_mean * (1.0 / (pixels * (chans // GROUPS)))
    chan_mean = member_dot(group_mean, group_members(chans, 1))[:1]
    spread = jnp.sum(jnp.square(joined_ref[...] - chan_mean), axis=0, keepdims=True)
    group_spread = member_dot(jnp.broadcast_to(spread, (8, chans)), members)
    stats = jnp.where(lane_id < GROUPS, group_sums, group_spread)
    stats = jnp.where(lane_id < 2 * GROUPS, stats, 0.0)
    stats_ref[...] = jnp.broadcast_to(stats[:1], stats_ref.shape)
    copy.wait()


def conv_kernel(
    clip_ref, joined_ref, stats_ref, gains_ref, early_ref, weight_hbm, resid_ref, sent_ref,
    window_ref, weight_ref, sems,
):
    copies = [
        pltpu.make_async_copy(weight_hbm.at[tap + 3], weight_ref.at[tap], sems.at[tap])
        for tap in range(6)
    ]
    for copy in copies:
        copy.start()
    pixels, chans = joined_ref.shape
    frames = stats_ref.shape[0]
    per_frame = float(pixels * (chans // GROUPS))
    stats = stats_ref[...]
    if frames > CLIP:
        row = lax.broadcasted_iota(jnp.int32, (frames, LANES), 0)
        first = clip_ref[0] * CLIP
        member = (row >= first) & (row < first + CLIP)
    else:
        member = jnp.full((frames, LANES), True)
    stats = jnp.where(member, stats, 0.0)
    mean_rows = stats * (1.0 / per_frame)
    lane_mean = jnp.sum(mean_rows, axis=0, keepdims=True) * (1.0 / CLIP)
    between = jnp.where(member, jnp.square(mean_rows - lane_mean), 0.0)
    lane_between = jnp.sum(between, axis=0, keepdims=True) * (1.0 / CLIP)
    lane_id = lax.broadcasted_iota(jnp.int32, (8, LANES), 1)
    row_id = lax.broadcasted_iota(jnp.int32, (8, LANES), 0)
    lane_var = jnp.where(lane_id < GROUPS, lane_between, lane_mean)
    lane_mean = jnp.where(lane_id < GROUPS, lane_mean, 0.0)
    chan_stats = member_dot(
        jnp.where(row_id == 0, lane_mean, lane_var), group_members(chans, 1)
    )
    chan_mean, chan_var = chan_stats[:1], chan_stats[1:2]
    edge = jnp.zeros((W, 3 * chans), BF16)
    window_ref[:W] = edge
    window_ref[W + pixels :] = edge
    factor = lax.rsqrt(chan_var + norm_epsilon)
    gain, bias = gains_ref[:1], gains_ref[1:2]
    col = lax.broadcasted_iota(jnp.int32, (W, chans), 0)

    @pl.loop(0, pixels // W)
    def _(line):
        here = pl.ds(pl.multiple_of(line * W, W), W)
        there = pl.ds(pl.multiple_of(line * W + W, W), W)
        activated = jax.nn.silu((joined_ref[here] - chan_mean) * factor * gain + bias)
        left = jnp.where(col == 0, 0.0, pltpu.roll(activated, 1, 0))
        right = jnp.where(col == W - 1, 0.0, pltpu.roll(activated, W - 1, 0))
        window_ref[there, :chans] = left.astype(BF16)
        window_ref[there, chans : 2 * chans] = activated.astype(BF16)
        window_ref[there, 2 * chans :] = right.astype(BF16)

    total = joined_ref[...]
    for shift in range(3):
        if shift == 0:
            weights = early_ref[...]
        else:
            taps = slice(3 * shift - 3, 3 * shift)
            for copy in copies[taps]:
                copy.wait()
            weights = weight_ref[taps]
        total = total + jnp.dot(
            window_ref[shift * W : shift * W + pixels],
            weights.reshape(3 * chans, chans),
            preferred_element_type=F32,
        )
    resid_ref[...] = total
    sent_ref[...] = total.astype(BF16)


def attend_kernel(per_dev, resid_ref, gains_ref, qkv_ref, out_ref, result_ref, rows_ref, mixed_ref):
    rows, chans = resid_ref.shape
    resid = resid_ref[...].astype(F32)
    mean = jnp.mean(resid, axis=-1, keepdims=True)
    centred = resid - mean
    var = jnp.mean(jnp.square(centred), axis=-1, keepdims=True)
    normed = (centred * lax.rsqrt(var + norm_epsilon) * gains_ref[2:3]).astype(BF16)
    rows_ref[...] = jnp.dot(normed, qkv_ref[...], preferred_element_type=F32).astype(BF16)
    scale = math.log2(math.e) / math.sqrt(HD)
    clip_rows = per_dev * CLIP
    period = max(per_dev, 8)
    pixel = lax.rem(lax.broadcasted_iota(jnp.int32, (1, period, clip_rows), 1), per_dev)
    other = lax.rem(lax.broadcasted_iota(jnp.int32, (1, period, clip_rows), 2), per_dev)
    paired = pixel == other
    low_lanes = lax.broadcasted_iota(jnp.int32, (clip_rows, LANES), 1) < HD
    one = jnp.ones((clip_rows, LANES), BF16)
    zero = jnp.zeros((clip_rows, LANES), BF16)
    for first_row in range(0, rows, clip_rows):
        clip = slice(first_row, first_row + clip_rows)

        for block in range(chans // LANES):
            lanes = [
                slice(block * LANES + part * chans, (block + 1) * LANES + part * chans)
                for part in range(3)
            ]
            queries, keys, values = [rows_ref[clip, part] for part in lanes]
            pair_queries = jnp.concatenate(
                [jnp.where(low_lanes, queries, zero), jnp.where(low_lanes, zero, queries)]
            )
            scores = lax.dot_general(
                pair_queries, keys, (((1,), (1,)), ((), ())), preferred_element_type=F32
            ).reshape(2 * clip_rows // period, period, clip_rows)
            scores = jnp.where(paired, scores, -1e30)
            top = jnp.max(scores, axis=-1, keepdims=True)
            expon = jnp.exp2((scores - top) * scale)
            expon = expon.reshape(2 * clip_rows, clip_rows).astype(BF16)
            low = jnp.dot(
                expon[:clip_rows], jnp.where(low_lanes, values, one), preferred_element_type=F32
            )
            high = jnp.dot(
                expon[clip_rows:], jnp.where(low_lanes, one, values), preferred_element_type=F32
            )
            total = pltpu.roll(jnp.where(low_lanes, high, low), HD, 1)
            mixed = jnp.where(low_lanes, low, high) / total
            mixed_ref[clip, lanes[0]] = mixed.astype(BF16)
    result = jnp.dot(mixed_ref[...], out_ref[...], preferred_element_type=F32)
    result_ref[...] = result.astype(BF16)


def fetch_kernel(*refs):
    count = len(refs) // 2
    for i in range(count):
        refs[count + i][...] = refs[i][...]


def fetch(*arrays):
    size = sum(a.size * a.dtype.itemsize for a in arrays)
    return pl.pallas_call(
        fetch_kernel,
        out_shape=tuple(jax.ShapeDtypeStruct(a.shape, a.dtype) for a in arrays),
        in_specs=[VMEM] * len(arrays),
        out_specs=(VMEM,) * len(arrays),
        compiler_params=params(1),
        cost_estimate=cost(0, 2 * size),
        name="fetch",
    )(*arrays)


def cost(flops, moved):
    return pl.CostEstimate(flops=int(flops), bytes_accessed=int(moved), transcendentals=0)


def exchange(blocks):
    return lax.all_to_all(blocks, "frames", split_axis=0, concat_axis=0, tiled=True)


def body(
    skip, control, zero_weight, gn_gain, gn_bias, conv_weight, ln_gain, qkv_weight, out_weight
):
    f_dev, pixels, chans = skip.shape
    devices = lax.axis_size("frames")
    frame_count, per_dev, _ = control.shape
    rows = frame_count * per_dev
    own_control = exchange(control.reshape(rows, chans)).reshape(devices, f_dev, per_dev, chans)
    gains = jnp.stack((gn_gain, gn_bias, ln_gain))
    skip, zero_weight, gains = fetch(skip, zero_weight, gains)
    first_frame = lax.axis_index("frames") * f_dev if frame_count > CLIP else jnp.int32(0)
    joined, stats, early = [], [], []
    for f in range(f_dev):
        frame_joined, frame_stats, frame_early = pl.pallas_call(
            join_kernel,
            out_shape=(
                jax.ShapeDtypeStruct((pixels, chans), F32),
                jax.ShapeDtypeStruct((devices, LANES), F32),
                jax.ShapeDtypeStruct((3, chans, chans), BF16),
            ),
            in_specs=[VMEM] * 3 + [pl.BlockSpec(memory_space=pl.ANY)],
            out_specs=(VMEM,) * 3,
            scratch_shapes=[pltpu.SemaphoreType.DMA],
            compiler_params=params(44),
            cost_estimate=cost(2 * pixels * chans * chans, 32e6),
            name="join",
        )(skip[f], own_control[:, f].reshape(pixels, chans), zero_weight, conv_weight)
        joined.append(frame_joined)
        stats.append(frame_stats)
        early.append(frame_early)
    all_stats = exchange(jnp.stack(stats, axis=1).reshape(devices * f_dev, LANES))
    resid, sent = [], []
    for f in range(f_dev):
        frame_resid, frame_sent = pl.pallas_call(
            conv_kernel,
            out_shape=(
                jax.ShapeDtypeStruct((pixels, chans), F32),
                jax.ShapeDtypeStruct((pixels, chans), BF16),
            ),
            in_specs=[SMEM] + [VMEM] * 4 + [pl.BlockSpec(memory_space=pl.ANY)],
            out_specs=(VMEM, VMEM),
            scratch_shapes=[
                pltpu.VMEM((pixels + 2 * W, 3 * chans), BF16),
                pltpu.VMEM((6, chans, chans), BF16),
                pltpu.SemaphoreType.DMA((6,)),
            ],
            compiler_params=params(50),
            cost_estimate=cost(18 * pixels * chans * chans, 9e6),
            name="conv",
        )(
            ((first_frame + f) // CLIP).reshape(1),
            joined[f],
            all_stats,
            gains,
            early[f],
            conv_weight,
        )
        resid.append(frame_resid)
        sent.append(frame_sent)
    by_pixel = jnp.stack(sent).reshape(f_dev, devices, per_dev, chans)
    by_pixel = exchange(by_pixel.transpose(1, 0, 2, 3).reshape(rows, chans))
    result = pl.pallas_call(
        functools.partial(attend_kernel, per_dev),
        out_shape=jax.ShapeDtypeStruct((rows, chans), BF16),
        in_specs=[VMEM] * 4,
        out_specs=VMEM,
        scratch_shapes=[pltpu.VMEM((rows, 3 * chans), BF16), pltpu.VMEM((rows, chans), BF16)],
        compiler_params=params(14),
        cost_estimate=cost(8 * rows * chans * chans, 4e6),
        name="attend",
    )(by_pixel, gains, qkv_weight, out_weight)
    mixed = exchange(result).reshape(devices, f_dev, per_dev, chans)
    mixed = mixed.transpose(1, 0, 2, 3).reshape(f_dev, pixels, chans)
    return (jnp.stack(resid) + mixed.astype(F32)).astype(BF16)


def solution(mesh):
    in_specs = (
        P(("groups", "frames"), None, None),
        P("groups", "frames", None),
        P(),
        P(),
        P(),
        P(),
        P(),
        P(),
        P(),
    )
    out_specs = P(("groups", "frames"), None, None)
    return jax.shard_map(body, mesh=mesh, in_specs=in_specs, out_specs=out_specs, check_vma=False)
```

time: 68.9 us -> 66.6 us (0.967)
  waiting for transfers between devices: 8.95 us -> 7.74 us
  Pallas kernels: 9.92 us -> 8.93 us
    all_to_all x1, waiting for transfers between devices: 8.95 us -> 7.74 us  [exchange(): lax.all_to_all(blocks, 'frames', split_axis=0, concat_axis=0, tiled=True)]
    pallas_call x1, Pallas kernels: 4.7 us -> 3.82 us  [body(): pl.pallas_call(conv_kernel, out_shape=(jax.ShapeDtypeStruct((pixels, chan...]
    pallas_call x1, Pallas kernels: 3.7 us -> 2.95 us  [body(): pl.pallas_call(functools.partial(attend_kernel, per_dev), out_shape=jax.S...]
where the time goes in v4:
time: 66.6 us; the launch traced here: 66.2 us
  blocking collectives  37.2 us (56%)
  Pallas kernels  8.93 us (13%)
  waiting for transfers between devices  7.74 us (12%)
  starting transfers between devices  7.33 us (11%)
  local copies, waits for them, and re-layouts  4.19 us (6%)
  other arithmetic  0.8 us (1%)
    all_to_all x3, blocking collectives, exchange(): lax.all_to_all(blocks, 'frames', split_axis=0, concat_axis=0, tiled=True)  37.2 us
    all_to_all x1, waiting for transfers between devices, exchange(): lax.all_to_all(blocks, 'frames', split_axis=0, concat_axis=0, tiled=True)  7.74 us
    all_to_all x1, starting transfers between devices, exchange(): lax.all_to_all(blocks, 'frames', split_axis=0, concat_axis=0, tiled=True)  7.33 us
    pallas_call x1, Pallas kernels, body(): pl.pallas_call(conv_kernel, out_shape=(jax.ShapeDtypeStruct((pixels, chan...  3.82 us
    pallas_call x1, Pallas kernels, body(): pl.pallas_call(functools.partial(attend_kernel, per_dev), out_shape=jax.S...  2.95 us
    unnamed x8, local copies, waits for them, and re-layouts  2.12 us
    pallas_call x1, Pallas kernels, body(): pl.pallas_call(join_kernel, out_shape=(jax.ShapeDtypeStruct((pixels, chan...  2.07 us
    another operation x3, local copies, waits for them, and re-layouts, body(): gains = jnp.stack((gn_gain, gn_bias, ln_gain))  2.07 us
  transfers between devices with their start and end apart: 1, of which 1 were waited for; matrix products, arithmetic and copies ran while one was open for 3% of the time, Pallas kernels for 0%

profile of v4, /device:TPU:0, one launch (start us, length us, event | category | flops | bytes accessed | tf_op | source)
XLA Modules:
  0.0 66.2 jit_solution(13762165773970920453)
XLA Ops:
  0.0 7.3 %all-to-all-start = ((bf16[32,8,640]{2,1,0:T(8,128)(2,1)}), bf16[32,8,640]{2,1,0:T(8,128)(2,1)S(1)}, u32[]{:S(2)}, u32[]{:S(2)}) async-start(bf16[32,8,640]{2,1,0:T(8,128)(2,1)} %param.10), calls=%async_computation | async-start | bytes 655360 | tf_op jit(solution)/shard_map/all_to_all | solution.py:218
  7.3 0.7 %stack.13 = f32[1,640]{1,0:T(1,128)S(1)} reshape(f32[640]{0:T(1024)} %param.12) | data formatting | bytes 5120 | tf_op jit(solution)/shard_map/stack | solution.py:229
  8.0 0.7 %stack.14 = f32[1,640]{1,0:T(1,128)S(1)} reshape(f32[640]{0:T(1024)} %param.13) | data formatting | bytes 5120 | tf_op jit(solution)/shard_map/stack | solution.py:229
  8.7 0.7 %stack.15 = f32[1,640]{1,0:T(1,128)S(1)} reshape(f32[640]{0:T(1024)} %param.15) | data formatting | bytes 5120 | tf_op jit(solution)/shard_map/stack | solution.py:229
  9.4 0.0 copy-start.2
  9.4 1.1 %copy-done.2 = bf16[640,640]{1,0:T(8,128)(2,1)S(1)} copy-done((bf16[640,640]{1,0:T(8,128)(2,1)S(1)}, bf16[640,640]{1,0:T(8,128)(2,1)}, u32[]{:S(2)}) %copy-start.2) | copy-done | bytes 819224
  10.6 0.0 copy-start.3
  10.6 1.0 %copy-done.3 = bf16[1,256,640]{2,1,0:T(8,128)(2,1)S(1)} copy-done((bf16[1,256,640]{2,1,0:T(8,128)(2,1)S(1)}, bf16[1,256,640]{2,1,0:T(8,128)(2,1)}, u32[]{:S(2)}) %copy-start.3) | copy-done | bytes 327704
  11.5 0.1 fetch.1
  11.6 7.7 %all-to-all-done = bf16[32,8,640]{2,1,0:T(8,128)(2,1)S(1)} async-done(((bf16[32,8,640]{2,1,0:T(8,128)(2,1)}), bf16[32,8,640]{2,1,0:T(8,128)(2,1)S(1)}, u32[]{:S(2)}, u32[]{:S(2)}) %all-to-all-start) | async-done | bytes 327712 | tf_op jit(solution)/shard_map/all_to_all | solution.py:218
  19.4 2.1 %join.1 = (f32[256,640]{1,0:T(8,128)S(1)}, f32[32,128]{1,0:T(8,128)S(1)}, bf16[3,640,640]{2,1,0:T(8,128)(2,1)S(1)}) custom-call(bf16[256,640]{1,0:T(8,128)(2,1)S(1)} %bitcast.17, bf16[256,640]{1,0:T(8,128)(2,1)S(1)} %bitcast.14, bf16[640,640]{1,0:T(8,128)(2,1)S(1)} %get-tuple-element.14.weight_ref, bf16[9,640,640]{2,1,0:T(8,128)(2,1)} %weight_hbm.1), custom_call_target="tpu_custom_call" | custom-call | flops 209715200 | bytes 32000000 | tf_op jit(solution)/shard_map/join/pallas_call | solution.py:234
  21.5 9.3 %all_to_all.39 = f32[32,1,128]{2,1,0:T(1,128)S(1)} all-to-all(f32[32,1,128]{2,1,0:T(1,128)S(1)} %bitcast.20), channel_id=1, replica_groups=mesh['groups'=1,'frames'=32] {'frames'}, dimensions={0} | all-to-all | bytes 32768 | tf_op jit(solution)/shard_map/all_to_all | solution.py:218
  30.8 0.0 copy-start
  30.8 0.0 copy-start.1
  30.8 3.8 %conv.1 = (f32[256,640]{1,0:T(8,128)S(1)}, bf16[256,640]{1,0:T(8,128)(2,1)S(1)}) custom-call(s32[1]{0:T(128)} %constant.15.clone.1.clip_ref, f32[256,640]{1,0:T(8,128)S(1)} %get-tuple-element.15.joined_ref, f32[32,128]{1,0:T(8,128)S(1)} %bitcast.19, f32[3,640]{1,0:T(4,128)S(1)} %get-tuple-element.17.gains_ref, ...), custom_call_target="tpu_custom_call" | custom-call | flops 1887436800 | bytes 9000000 | tf_op jit(solution)/shard_map/conv/pallas_call | solution.py:254
  34.6 13.8 %all_to_all.40 = bf16[32,8,640]{2,1,0:T(8,128)(2,1)S(1)} all-to-all(bf16[32,8,640]{2,1,0:T(8,128)(2,1)S(1)} %bitcast.18), channel_id=1, replica_groups=mesh['groups'=1,'frames'=32] {'frames'}, dimensions={0} | all-to-all | bytes 655360 | tf_op jit(solution)/shard_map/all_to_all | solution.py:218
  48.4 0.0 copy-done
  48.4 0.0 copy-done.1
  48.4 2.9 %attend.1 = bf16[256,640]{1,0:T(8,128)(2,1)S(1)} custom-call(bf16[256,640]{1,0:T(8,128)(2,1)S(1)} %bitcast.15, f32[3,640]{1,0:T(4,128)S(1)} %get-tuple-element.17.gains_ref, bf16[640,1920]{1,0:T(8,128)(2,1)S(1)} %copy-done, bf16[640,640]{1,0:T(8,128)(2,1)S(1)} %copy-done.1), custom_call_target="tpu_custom_call" | custom-call | flops 838860800 | bytes 4000000 | tf_op jit(solution)/shard_map/attend/pallas_call | solution.py:282
  51.3 14.1 %all_to_all.41 = bf16[32,8,640]{2,1,0:T(8,128)(2,1)S(1)} all-to-all(bf16[32,8,640]{2,1,0:T(8,128)(2,1)S(1)} %bitcast.16), channel_id=1, replica_groups=mesh['groups'=1,'frames'=32] {'frames'}, dimensions={0} | all-to-all | bytes 655360 | tf_op jit(solution)/shard_map/all_to_all | solution.py:218
  65.4 0.8 %fusion.1 = bf16[1,256,640]{2,1,0:T(8,128)(2,1)} fusion(f32[256,640]{1,0:T(8,128)S(1)} %get-tuple-element.19, bf16[32,8,640]{2,1,0:T(8,128)(2,1)S(1)} %all_to_all.41), kind=kLoop, calls=%fused_computation.2 | loop fusion | flops 491520 | bytes 1310720 | tf_op jit(solution)/shard_map/convert_element_type | solution.py:294
  (1 shorter events, 0.0 us)
Async XLA Ops:
  0.0 19.4 %all-to-all-start = ((bf16[32,8,640]{2,1,0:T(8,128)(2,1)}), bf16[32,8,640]{2,1,0:T(8,128)(2,1)S(1)}, u32[]{:S(2)}, u32[]{:S(2)}) async-start(bf16[32,8,640]{2,1,0:T(8,128)(2,1)} %param.10), calls=%async_computation | async-start | bytes 655360 | tf_op jit(solution)/shard_map/all_to_all | solution.py:218
  9.4 1.1 %copy-start.2 = (bf16[640,640]{1,0:T(8,128)(2,1)S(1)}, bf16[640,640]{1,0:T(8,128)(2,1)}, u32[]{:S(2)}) copy-start(bf16[640,640]{1,0:T(8,128)(2,1)} %refs_1_.1) | copy-start | bytes 2457604
  10.6 1.0 %copy-start.3 = (bf16[1,256,640]{2,1,0:T(8,128)(2,1)S(1)}, bf16[1,256,640]{2,1,0:T(8,128)(2,1)}, u32[]{:S(2)}) copy-start(bf16[1,256,640]{2,1,0:T(8,128)(2,1)} %refs_0_.1) | copy-start | bytes 983044
  30.8 17.6 %copy-start = (bf16[640,1920]{1,0:T(8,128)(2,1)S(1)}, bf16[640,1920]{1,0:T(8,128)(2,1)}, u32[]{:S(2)}) copy-start(bf16[640,1920]{1,0:T(8,128)(2,1)} %qkv_ref.1) | copy-start | bytes 7372804
  30.8 17.6 %copy-start.1 = (bf16[640,640]{1,0:T(8,128)(2,1)S(1)}, bf16[640,640]{1,0:T(8,128)(2,1)}, u32[]{:S(2)}) copy-start(bf16[640,640]{1,0:T(8,128)(2,1)} %out_ref.1) | copy-start | bytes 2457604

commit v5 on v4

--- a/solution.py
+++ b/solution.py
@@ -14,6 +14,7 @@
 CLIP = 32
 W = 32
 LANES = 128
+EARLY = 2
 
 norm_epsilon = 1e-05
 F32 = jnp.float32
@@ -52,7 +53,7 @@
 def join_kernel(
     skip_ref, control_ref, weight_ref, conv_hbm, joined_ref, stats_ref, conv_ref, sem
 ):
-    copy = pltpu.make_async_copy(conv_hbm.at[pl.ds(0, 3)], conv_ref, sem)
+    copy = pltpu.make_async_copy(conv_hbm.at[pl.ds(EARLY, 1)], conv_ref, sem)
     copy.start()
     pixels, chans = skip_ref.shape
     zero_out = jnp.dot(control_ref[...], weight_ref[...], preferred_element_type=F32).astype(BF16)
@@ -74,8 +75,8 @@
 
 
 def conv_kernel(
-    clip_ref, joined_ref, stats_ref, gains_ref, early_ref, weight_hbm, resid_ref, sent_ref,
-    window_ref, weight_ref, sems,
+    clip_ref, joined_ref, stats_ref, gains_ref, first_ref, early_ref, weight_hbm, resid_ref,
+    sent_ref, window_ref, weight_ref, sems,
 ):
     copies = [
         pltpu.make_async_copy(weight_hbm.at[tap + 3], weight_ref.at[tap], sems.at[tap])
@@ -125,24 +126,33 @@
         window_ref[there, 2 * chans :] = right.astype(BF16)
 
     total = joined_ref[...]
-    for shift in range(3):
-        if shift == 0:
+    tap = 0
+    for count in (EARLY, 1, 3, 3):
+        if tap == 0:
+            weights = first_ref[...]
+        elif tap == EARLY:
             weights = early_ref[...]
         else:
-            taps = slice(3 * shift - 3, 3 * shift)
+            taps = slice(tap - 3, tap - 3 + count)
             for copy in copies[taps]:
                 copy.wait()
             weights = weight_ref[taps]
+        row = tap // 3 * W
+        start = tap % 3 * chans
         total = total + jnp.dot(
-            window_ref[shift * W : shift * W + pixels],
-            weights.reshape(3 * chans, chans),
+            window_ref[row : row + pixels, start : start + count * chans],
+            weights.reshape(count * chans, chans),
             preferred_element_type=F32,
         )
+        tap += count
     resid_ref[...] = total
     sent_ref[...] = total.astype(BF16)
 
 
-def attend_kernel(per_dev, resid_ref, gains_ref, qkv_ref, out_ref, result_ref, rows_ref, mixed_ref):
+def attend_kernel(
+    per_dev, resid_ref, gains_ref, qkv_ref, out_ref, result_ref, rows_ref, mixed_ref, scores_ref,
+    weights_ref,
+):
     rows, chans = resid_ref.shape
     resid = resid_ref[...].astype(F32)
     mean = jnp.mean(resid, axis=-1, keepdims=True)
@@ -162,52 +172,81 @@
     for first_row in range(0, rows, clip_rows):
         clip = slice(first_row, first_row + clip_rows)
 
-        for block in range(chans // LANES):
-            lanes = [
-                slice(block * LANES + part * chans, (block + 1) * LANES + part * chans)
-                for part in range(3)
-            ]
-            queries, keys, values = [rows_ref[clip, part] for part in lanes]
+        blocks = chans // LANES
+
+        def lanes_of(block, part):
+            start = block * LANES + part * chans
+            return rows_ref[clip, start : start + LANES]
+
+        def scores_of(block):
+            queries = lanes_of(block, 0)
             pair_queries = jnp.concatenate(
                 [jnp.where(low_lanes, queries, zero), jnp.where(low_lanes, zero, queries)]
             )
-            scores = lax.dot_general(
-                pair_queries, keys, (((1,), (1,)), ((), ())), preferred_element_type=F32
-            ).reshape(2 * clip_rows // period, period, clip_rows)
+            scores_ref[block % 2] = lax.dot_general(
+                pair_queries,
+                lanes_of(block, 1),
+                (((1,), (1,)), ((), ())),
+                preferred_element_type=F32,
+            )
+
+        def weights_of(block):
+            scores = scores_ref[block % 2].reshape(2 * clip_rows // period, period, clip_rows)
             scores = jnp.where(paired, scores, -1e30)
             top = jnp.max(scores, axis=-1, keepdims=True)
             expon = jnp.exp2((scores - top) * scale)
-            expon = expon.reshape(2 * clip_rows, clip_rows).astype(BF16)
+            weights_ref[block % 2] = expon.reshape(2 * clip_rows, clip_rows).astype(BF16)
+
+        def mix(block):
+            values = lanes_of(block, 2)
+            weights = weights_ref[block % 2]
             low = jnp.dot(
-                expon[:clip_rows], jnp.where(low_lanes, values, one), preferred_element_type=F32
+                weights[:clip_rows], jnp.where(low_lanes, values, one), preferred_element_type=F32
             )
             high = jnp.dot(
-                expon[clip_rows:], jnp.where(low_lanes, one, values), preferred_element_type=F32
+                weights[clip_rows:], jnp.where(low_lanes, one, values), preferred_element_type=F32
             )
             total = pltpu.roll(jnp.where(low_lanes, high, low), HD, 1)
             mixed = jnp.where(low_lanes, low, high) / total
-            mixed_ref[clip, lanes[0]] = mixed.astype(BF16)
+            mixed_ref[clip, block * LANES : (block + 1) * LANES] = mixed.astype(BF16)
+
+        scores_of(0)
+        for block in range(blocks):
+            if block + 1 < blocks:
+                scores_of(block + 1)
+            weights_of(block)
+            if block:
+                mix(block - 1)
+        mix(blocks - 1)
     result = jnp.dot(mixed_ref[...], out_ref[...], preferred_element_type=F32)
     result_ref[...] = result.astype(BF16)
 
 
-def fetch_kernel(*refs):
-    count = len(refs) // 2
+def fetch_kernel(count, *refs):
+    sem = refs[-1]
+    taps_hbm, taps_ref = refs[count], refs[-2]
+    copy = pltpu.make_async_copy(taps_hbm.at[pl.ds(0, EARLY)], taps_ref, sem)
+    copy.start()
     for i in range(count):
-        refs[count + i][...] = refs[i][...]
-
-
-def fetch(*arrays):
+        refs[count + 1 + i][...] = refs[i][...]
+    copy.wait()
+
+
+def fetch(conv_weight, *arrays):
+    count = len(arrays)
     size = sum(a.size * a.dtype.itemsize for a in arrays)
+    shapes = [jax.ShapeDtypeStruct(a.shape, a.dtype) for a in arrays]
+    shapes.append(jax.ShapeDtypeStruct((EARLY,) + conv_weight.shape[1:], conv_weight.dtype))
     return pl.pallas_call(
-        fetch_kernel,
-        out_shape=tuple(jax.ShapeDtypeStruct(a.shape, a.dtype) for a in arrays),
-        in_specs=[VMEM] * len(arrays),
-        out_specs=(VMEM,) * len(arrays),
-        compiler_params=params(1),
+        functools.partial(fetch_kernel, count),
+        out_shape=tuple(shapes),
+        in_specs=[VMEM] * count + [pl.BlockSpec(memory_space=pl.ANY)],
+        out_specs=(VMEM,) * (count + 1),
+        scratch_shapes=[pltpu.SemaphoreType.DMA],
+        compiler_params=params(44),
         cost_estimate=cost(0, 2 * size),
         name="fetch",
-    )(*arrays)
+    )(*arrays, conv_weight)
 
 
 def cost(flops, moved):
@@ -227,7 +266,7 @@
     rows = frame_count * per_dev
     own_control = exchange(control.reshape(rows, chans)).reshape(devices, f_dev, per_dev, chans)
     gains = jnp.stack((gn_gain, gn_bias, ln_gain))
-    skip, zero_weight, gains = fetch(skip, zero_weight, gains)
+    skip, zero_weight, gains, first_taps = fetch(conv_weight, skip, zero_weight, gains)
     first_frame = lax.axis_index("frames") * f_dev if frame_count > CLIP else jnp.int32(0)
     joined, stats, early = [], [], []
     for f in range(f_dev):
@@ -236,12 +275,12 @@
             out_shape=(
                 jax.ShapeDtypeStruct((pixels, chans), F32),
                 jax.ShapeDtypeStruct((devices, LANES), F32),
-                jax.ShapeDtypeStruct((3, chans, chans), BF16),
+                jax.ShapeDtypeStruct((1, chans, chans), BF16),
             ),
             in_specs=[VMEM] * 3 + [pl.BlockSpec(memory_space=pl.ANY)],
             out_specs=(VMEM,) * 3,
             scratch_shapes=[pltpu.SemaphoreType.DMA],
-            compiler_params=params(44),
+            compiler_params=params(48),
             cost_estimate=cost(2 * pixels * chans * chans, 32e6),
             name="join",
         )(skip[f], own_control[:, f].reshape(pixels, chans), zero_weight, conv_weight)
@@ -257,7 +296,7 @@
                 jax.ShapeDtypeStruct((pixels, chans), F32),
                 jax.ShapeDtypeStruct((pixels, chans), BF16),
             ),
-            in_specs=[SMEM] + [VMEM] * 4 + [pl.BlockSpec(memory_space=pl.ANY)],
+            in_specs=[SMEM] + [VMEM] * 5 + [pl.BlockSpec(memory_space=pl.ANY)],
             out_specs=(VMEM, VMEM),
             scratch_shapes=[
                 pltpu.VMEM((pixels + 2 * W, 3 * chans), BF16),
@@ -272,6 +311,7 @@
             joined[f],
             all_stats,
             gains,
+            first_taps,
             early[f],
             conv_weight,
         )
@@ -284,7 +324,12 @@
         out_shape=jax.ShapeDtypeStruct((rows, chans), BF16),
         in_specs=[VMEM] * 4,
         out_specs=VMEM,
-        scratch_shapes=[pltpu.VMEM((rows, 3 * chans), BF16), pltpu.VMEM((rows, chans), BF16)],
+        scratch_shapes=[
+            pltpu.VMEM((rows, 3 * chans), BF16),
+            pltpu.VMEM((rows, chans), BF16),
+            pltpu.VMEM((2, 2 * per_dev * CLIP, per_dev * CLIP), F32),
+            pltpu.VMEM((2, 2 * per_dev * CLIP, per_dev * CLIP), BF16),
+        ],
         compiler_params=params(14),
         cost_estimate=cost(8 * rows * chans * chans, 4e6),
         name="attend",

time: 66.6 us -> 66 us (level)
  waiting for transfers between devices: 7.74 us -> 6.39 us
  Pallas kernels: 8.93 us -> 9.61 us
    all_to_all x1, waiting for transfers between devices: 7.74 us -> 6.39 us  [exchange(): lax.all_to_all(blocks, 'frames', split_axis=0, concat_axis=0, tiled=True)]
    pallas_call x1, Pallas kernels: 0.09 us -> 1.44 us  [fetch(): pl.pallas_call(functools.partial(fetch_kernel, count), out_shape=tuple(sh...]
  transfers between devices with their start and end apart: 1 -> 1, of which waited for: 1 -> 1; matrix products, arithmetic and copies ran while one was open for 3% -> 3% of each run, Pallas kernels for 0% -> 2%
where the time goes in v5:
time: 66 us; the launch traced here: 65.5 us
  blocking collectives  37.2 us (56%)
  Pallas kernels  9.61 us (15%)
  starting transfers between devices  7.33 us (11%)
  waiting for transfers between devices  6.39 us (10%)
  local copies, waits for them, and re-layouts  4.19 us (6%)
  other arithmetic  0.8 us (1%)
    all_to_all x3, blocking collectives, exchange(): lax.all_to_all(blocks, 'frames', split_axis=0, concat_axis=0, tiled=True)  37.2 us
    all_to_all x1, starting transfers between devices, exchange(): lax.all_to_all(blocks, 'frames', split_axis=0, concat_axis=0, tiled=True)  7.33 us
    all_to_all x1, waiting for transfers between devices, exchange(): lax.all_to_all(blocks, 'frames', split_axis=0, concat_axis=0, tiled=True)  6.39 us
    pallas_call x1, Pallas kernels, body(): pl.pallas_call(conv_kernel, out_shape=(jax.ShapeDtypeStruct((pixels, chan...  3.82 us
    pallas_call x1, Pallas kernels, body(): pl.pallas_call(functools.partial(attend_kernel, per_dev), out_shape=jax.S...  2.83 us
    unnamed x8, local copies, waits for them, and re-layouts  2.12 us
    another operation x3, local copies, waits for them, and re-layouts, body(): gains = jnp.stack((gn_gain, gn_bias, ln_gain))  2.07 us
    pallas_call x1, Pallas kernels, body(): pl.pallas_call(join_kernel, out_shape=(jax.ShapeDtypeStruct((pixels, chan...  1.53 us
  transfers between devices with their start and end apart: 1, of which 1 were waited for; matrix products, arithmetic and copies ran while one was open for 3% of the time, Pallas kernels for 2%

profile of v5, /device:TPU:0, one launch (start us, length us, event | category | flops | bytes accessed | tf_op | source)
XLA Modules:
  0.0 65.5 jit_solution(1354781116707836842)
XLA Ops:
  0.0 7.3 %all-to-all-start = ((bf16[32,8,640]{2,1,0:T(8,128)(2,1)}), bf16[32,8,640]{2,1,0:T(8,128)(2,1)S(1)}, u32[]{:S(2)}, u32[]{:S(2)}) async-start(bf16[32,8,640]{2,1,0:T(8,128)(2,1)} %param.10), calls=%async_computation | async-start | bytes 655360 | tf_op jit(solution)/shard_map/all_to_all | solution.py:257
  7.3 0.7 %stack.13 = f32[1,640]{1,0:T(1,128)S(1)} reshape(f32[640]{0:T(1024)} %param.12) | data formatting | bytes 5120 | tf_op jit(solution)/shard_map/stack | solution.py:268
  8.0 0.7 %stack.14 = f32[1,640]{1,0:T(1,128)S(1)} reshape(f32[640]{0:T(1024)} %param.13) | data formatting | bytes 5120 | tf_op jit(solution)/shard_map/stack | solution.py:268
  8.7 0.7 %stack.15 = f32[1,640]{1,0:T(1,128)S(1)} reshape(f32[640]{0:T(1024)} %param.15) | data formatting | bytes 5120 | tf_op jit(solution)/shard_map/stack | solution.py:268
  9.4 0.0 copy-start.2
  9.4 1.1 %copy-done.2 = bf16[640,640]{1,0:T(8,128)(2,1)S(1)} copy-done((bf16[640,640]{1,0:T(8,128)(2,1)S(1)}, bf16[640,640]{1,0:T(8,128)(2,1)}, u32[]{:S(2)}) %copy-start.2) | copy-done | bytes 819224
  10.6 0.0 copy-start.3
  10.6 1.0 %copy-done.3 = bf16[1,256,640]{2,1,0:T(8,128)(2,1)S(1)} copy-done((bf16[1,256,640]{2,1,0:T(8,128)(2,1)S(1)}, bf16[1,256,640]{2,1,0:T(8,128)(2,1)}, u32[]{:S(2)}) %copy-start.3) | copy-done | bytes 327704
  11.5 1.4 %fetch.1 = (bf16[1,256,640]{2,1,0:T(8,128)(2,1)S(1)}, bf16[640,640]{1,0:T(8,128)(2,1)S(1)}, f32[3,640]{1,0:T(4,128)S(1)}, bf16[2,640,640]{2,1,0:T(8,128)(2,1)S(1)}) custom-call(bf16[1,256,640]{2,1,0:T(8,128)(2,1)S(1)} %copy-done.3, bf16[640,640]{1,0:T(8,128)(2,1)S(1)} %copy-done.2, f32[3,640]{1,0:T(4,128)S(1)} %pad_maximum_fusion.refs_2_, ...), custom_call_target="tpu_custom_call" | custom-call | bytes 2309120 | tf_op jit(solution)/shard_map/fetch/pallas_call | solution.py:240
  13.0 6.4 %all-to-all-done = bf16[32,8,640]{2,1,0:T(8,128)(2,1)S(1)} async-done(((bf16[32,8,640]{2,1,0:T(8,128)(2,1)}), bf16[32,8,640]{2,1,0:T(8,128)(2,1)S(1)}, u32[]{:S(2)}, u32[]{:S(2)}) %all-to-all-start) | async-done | bytes 327712 | tf_op jit(solution)/shard_map/all_to_all | solution.py:257
  19.4 1.5 %join.1 = (f32[256,640]{1,0:T(8,128)S(1)}, f32[32,128]{1,0:T(8,128)S(1)}, bf16[1,640,640]{2,1,0:T(8,128)(2,1)S(1)}) custom-call(bf16[256,640]{1,0:T(8,128)(2,1)S(1)} %bitcast.17, bf16[256,640]{1,0:T(8,128)(2,1)S(1)} %bitcast.14, bf16[640,640]{1,0:T(8,128)(2,1)S(1)} %get-tuple-element.15.weight_ref, bf16[9,640,640]{2,1,0:T(8,128)(2,1)} %weight_hbm.1), custom_call_target="tpu_custom_call" | custom-call | flops 209715200 | bytes 32000000 | tf_op jit(solution)/shard_map/join/pallas_call | solution.py:273
  20.9 9.3 %all_to_all.39 = f32[32,1,128]{2,1,0:T(1,128)S(1)} all-to-all(f32[32,1,128]{2,1,0:T(1,128)S(1)} %bitcast.20), channel_id=1, replica_groups=mesh['groups'=1,'frames'=32] {'frames'}, dimensions={0} | all-to-all | bytes 32768 | tf_op jit(solution)/shard_map/all_to_all | solution.py:257
  30.2 0.0 copy-start
  30.2 0.0 copy-start.1
  30.2 3.8 %conv.1 = (f32[256,640]{1,0:T(8,128)S(1)}, bf16[256,640]{1,0:T(8,128)(2,1)S(1)}) custom-call(s32[1]{0:T(128)} %constant.15.clone.1.clip_ref, f32[256,640]{1,0:T(8,128)S(1)} %get-tuple-element.16.joined_ref, f32[32,128]{1,0:T(8,128)S(1)} %bitcast.19, f32[3,640]{1,0:T(4,128)S(1)} %get-tuple-element.18.gains_ref, ...), custom_call_target="tpu_custom_call" | custom-call | flops 1887436800 | bytes 9000000 | tf_op jit(solution)/shard_map/conv/pallas_call | solution.py:293
  34.1 13.8 %all_to_all.40 = bf16[32,8,640]{2,1,0:T(8,128)(2,1)S(1)} all-to-all(bf16[32,8,640]{2,1,0:T(8,128)(2,1)S(1)} %bitcast.18), channel_id=1, replica_groups=mesh['groups'=1,'frames'=32] {'frames'}, dimensions={0} | all-to-all | bytes 655360 | tf_op jit(solution)/shard_map/all_to_all | solution.py:257
  47.8 0.0 copy-done
  47.8 0.0 copy-done.1
  47.8 2.8 %attend.1 = bf16[256,640]{1,0:T(8,128)(2,1)S(1)} custom-call(bf16[256,640]{1,0:T(8,128)(2,1)S(1)} %bitcast.15, f32[3,640]{1,0:T(4,128)S(1)} %get-tuple-element.18.gains_ref, bf16[640,1920]{1,0:T(8,128)(2,1)S(1)} %copy-done, bf16[640,640]{1,0:T(8,128)(2,1)S(1)} %copy-done.1), custom_call_target="tpu_custom_call" | custom-call | flops 838860800 | bytes 4000000 | tf_op jit(solution)/shard_map/attend/pallas_call | solution.py:322
  50.7 14.1 %all_to_all.41 = bf16[32,8,640]{2,1,0:T(8,128)(2,1)S(1)} all-to-all(bf16[32,8,640]{2,1,0:T(8,128)(2,1)S(1)} %bitcast.16), channel_id=1, replica_groups=mesh['groups'=1,'frames'=32] {'frames'}, dimensions={0} | all-to-all | bytes 655360 | tf_op jit(solution)/shard_map/all_to_all | solution.py:257
  64.7 0.8 %fusion.1 = bf16[1,256,640]{2,1,0:T(8,128)(2,1)} fusion(f32[256,640]{1,0:T(8,128)S(1)} %get-tuple-element.21, bf16[32,8,640]{2,1,0:T(8,128)(2,1)S(1)} %all_to_all.41), kind=kLoop, calls=%fused_computation.2 | loop fusion | flops 491520 | bytes 1310720 | tf_op jit(solution)/shard_map/convert_element_type | solution.py:339
  (1 shorter events, 0.0 us)
Async XLA Ops:
  0.0 19.4 %all-to-all-start = ((bf16[32,8,640]{2,1,0:T(8,128)(2,1)}), bf16[32,8,640]{2,1,0:T(8,128)(2,1)S(1)}, u32[]{:S(2)}, u32[]{:S(2)}) async-start(bf16[32,8,640]{2,1,0:T(8,128)(2,1)} %param.10), calls=%async_computation | async-start | bytes 655360 | tf_op jit(solution)/shard_map/all_to_all | solution.py:257
  9.4 1.1 %copy-start.2 = (bf16[640,640]{1,0:T(8,128)(2,1)S(1)}, bf16[640,640]{1,0:T(8,128)(2,1)}, u32[]{:S(2)}) copy-start(bf16[640,640]{1,0:T(8,128)(2,1)} %refs_1_.1) | copy-start | bytes 2457604
  10.6 1.0 %copy-start.3 = (bf16[1,256,640]{2,1,0:T(8,128)(2,1)S(1)}, bf16[1,256,640]{2,1,0:T(8,128)(2,1)}, u32[]{:S(2)}) copy-start(bf16[1,256,640]{2,1,0:T(8,128)(2,1)} %refs_0_.1) | copy-start | bytes 983044
  30.2 17.6 %copy-start = (bf16[640,1920]{1,0:T(8,128)(2,1)S(1)}, bf16[640,1920]{1,0:T(8,128)(2,1)}, u32[]{:S(2)}) copy-start(bf16[640,1920]{1,0:T(8,128)(2,1)} %qkv_ref.1) | copy-start | bytes 7372804
  30.2 17.6 %copy-start.1 = (bf16[640,640]{1,0:T(8,128)(2,1)S(1)}, bf16[640,640]{1,0:T(8,128)(2,1)}, u32[]{:S(2)}) copy-start(bf16[640,640]{1,0:T(8,128)(2,1)} %out_ref.1) | copy-start | bytes 2457604

commit v6 on v5

--- a/solution.py
+++ b/solution.py
@@ -15,6 +15,7 @@
 W = 32
 LANES = 128
 EARLY = 2
+COUNTS = (2, 1, 3, 3)
 
 norm_epsilon = 1e-05
 F32 = jnp.float32
@@ -50,11 +51,7 @@
     return jnp.concatenate(blocks, axis=axis)
 
 
-def join_kernel(
-    skip_ref, control_ref, weight_ref, conv_hbm, joined_ref, stats_ref, conv_ref, sem
-):
-    copy = pltpu.make_async_copy(conv_hbm.at[pl.ds(EARLY, 1)], conv_ref, sem)
-    copy.start()
+def join_kernel(skip_ref, control_ref, weight_ref, joined_ref, stats_ref):
     pixels, chans = skip_ref.shape
     zero_out = jnp.dot(control_ref[...], weight_ref[...], preferred_element_type=F32).astype(BF16)
     joined = skip_ref[...].astype(F32) + zero_out.astype(F32)
@@ -71,16 +68,15 @@
     stats = jnp.where(lane_id < GROUPS, group_sums, group_spread)
     stats = jnp.where(lane_id < 2 * GROUPS, stats, 0.0)
     stats_ref[...] = jnp.broadcast_to(stats[:1], stats_ref.shape)
-    copy.wait()
 
 
 def conv_kernel(
-    clip_ref, joined_ref, stats_ref, gains_ref, first_ref, early_ref, weight_hbm, resid_ref,
-    sent_ref, window_ref, weight_ref, sems,
+    clip_ref, joined_ref, stats_ref, gains_ref, first_ref, weight_hbm, resid_ref, sent_ref,
+    window_ref, weight_ref, sems,
 ):
     copies = [
-        pltpu.make_async_copy(weight_hbm.at[tap + 3], weight_ref.at[tap], sems.at[tap])
-        for tap in range(6)
+        pltpu.make_async_copy(weight_hbm.at[tap + EARLY], weight_ref.at[tap], sems.at[tap])
+        for tap in range(9 - EARLY)
     ]
     for copy in copies:
         copy.start()
@@ -127,13 +123,11 @@
 
     total = joined_ref[...]
     tap = 0
-    for count in (EARLY, 1, 3, 3):
+    for count in COUNTS:
         if tap == 0:
             weights = first_ref[...]
-        elif tap == EARLY:
-            weights = early_ref[...]
         else:
-            taps = slice(tap - 3, tap - 3 + count)
+            taps = slice(tap - EARLY, tap - EARLY + count)
             for copy in copies[taps]:
                 copy.wait()
             weights = weight_ref[taps]
@@ -268,25 +262,22 @@
     gains = jnp.stack((gn_gain, gn_bias, ln_gain))
     skip, zero_weight, gains, first_taps = fetch(conv_weight, skip, zero_weight, gains)
     first_frame = lax.axis_index("frames") * f_dev if frame_count > CLIP else jnp.int32(0)
-    joined, stats, early = [], [], []
+    joined, stats = [], []
     for f in range(f_dev):
-        frame_joined, frame_stats, frame_early = pl.pallas_call(
+        frame_joined, frame_stats = pl.pallas_call(
             join_kernel,
             out_shape=(
                 jax.ShapeDtypeStruct((pixels, chans), F32),
                 jax.ShapeDtypeStruct((devices, LANES), F32),
-                jax.ShapeDtypeStruct((1, chans, chans), BF16),
             ),
-            in_specs=[VMEM] * 3 + [pl.BlockSpec(memory_space=pl.ANY)],
-            out_specs=(VMEM,) * 3,
-            scratch_shapes=[pltpu.SemaphoreType.DMA],
-            compiler_params=params(48),
+            in_specs=[VMEM] * 3,
+            out_specs=(VMEM, VMEM),
+            compiler_params=params(8),
             cost_estimate=cost(2 * pixels * chans * chans, 32e6),
             name="join",
-        )(skip[f], own_control[:, f].reshape(pixels, chans), zero_weight, conv_weight)
+        )(skip[f], own_control[:, f].reshape(pixels, chans), zero_weight)
         joined.append(frame_joined)
         stats.append(frame_stats)
-        early.append(frame_early)
     all_stats = exchange(jnp.stack(stats, axis=1).reshape(devices * f_dev, LANES))
     resid, sent = [], []
     for f in range(f_dev):
@@ -296,12 +287,12 @@
                 jax.ShapeDtypeStruct((pixels, chans), F32),
                 jax.ShapeDtypeStruct((pixels, chans), BF16),
             ),
-            in_specs=[SMEM] + [VMEM] * 5 + [pl.BlockSpec(memory_space=pl.ANY)],
+            in_specs=[SMEM] + [VMEM] * 4 + [pl.BlockSpec(memory_space=pl.ANY)],
             out_specs=(VMEM, VMEM),
             scratch_shapes=[
                 pltpu.VMEM((pixels + 2 * W, 3 * chans), BF16),
-                pltpu.VMEM((6, chans, chans), BF16),
-                pltpu.SemaphoreType.DMA((6,)),
+                pltpu.VMEM((9 - EARLY, chans, chans), BF16),
+                pltpu.SemaphoreType.DMA((9 - EARLY,)),
             ],
             compiler_params=params(50),
             cost_estimate=cost(18 * pixels * chans * chans, 9e6),
@@ -312,7 +303,6 @@
             all_stats,
             gains,
             first_taps,
-            early[f],
             conv_weight,
         )
         resid.append(frame_resid)

time: 66 us -> 65.7 us (level)
  no operation moved by 1% of the time
where the time goes in v6:
time: 65.7 us; the launch traced here: 65.2 us
  blocking collectives  37.2 us (57%)
  Pallas kernels  9.32 us (14%)
  starting transfers between devices  7.33 us (11%)
  waiting for transfers between devices  6.39 us (10%)
  local copies, waits for them, and re-layouts  4.19 us (6%)
  other arithmetic  0.8 us (1%)
    all_to_all x3, blocking collectives, exchange(): lax.all_to_all(blocks, 'frames', split_axis=0, concat_axis=0, tiled=True)  37.2 us
    all_to_all x1, starting transfers between devices, exchange(): lax.all_to_all(blocks, 'frames', split_axis=0, concat_axis=0, tiled=True)  7.33 us
    all_to_all x1, waiting for transfers between devices, exchange(): lax.all_to_all(blocks, 'frames', split_axis=0, concat_axis=0, tiled=True)  6.39 us
    pallas_call x1, Pallas kernels, body(): pl.pallas_call(conv_kernel, out_shape=(jax.ShapeDtypeStruct((pixels, chan...  4.07 us
    pallas_call x1, Pallas kernels, body(): pl.pallas_call(functools.partial(attend_kernel, per_dev), out_shape=jax.S...  2.83 us
    unnamed x8, local copies, waits for them, and re-layouts  2.12 us
    another operation x3, local copies, waits for them, and re-layouts, body(): gains = jnp.stack((gn_gain, gn_bias, ln_gain))  2.07 us
    pallas_call x1, Pallas kernels, fetch(): pl.pallas_call(functools.partial(fetch_kernel, count), out_shape=tuple(sh...  1.44 us
  transfers between devices with their start and end apart: 1, of which 1 were waited for; matrix products, arithmetic and copies ran while one was open for 3% of the time, Pallas kernels for 2%

profile of v6, /device:TPU:0, one launch (start us, length us, event | category | flops | bytes accessed | tf_op | source)
XLA Modules:
  0.0 65.2 jit_solution(139064340830598373)
XLA Ops:
  0.0 7.3 %all-to-all-start = ((bf16[32,8,640]{2,1,0:T(8,128)(2,1)}), bf16[32,8,640]{2,1,0:T(8,128)(2,1)S(1)}, u32[]{:S(2)}, u32[]{:S(2)}) async-start(bf16[32,8,640]{2,1,0:T(8,128)(2,1)} %param.10), calls=%async_computation | async-start | bytes 655360 | tf_op jit(solution)/shard_map/all_to_all | solution.py:251
  7.3 0.7 %stack.13 = f32[1,640]{1,0:T(1,128)S(1)} reshape(f32[640]{0:T(1024)} %param.12) | data formatting | bytes 5120 | tf_op jit(solution)/shard_map/stack | solution.py:262
  8.0 0.7 %stack.14 = f32[1,640]{1,0:T(1,128)S(1)} reshape(f32[640]{0:T(1024)} %param.13) | data formatting | bytes 5120 | tf_op jit(solution)/shard_map/stack | solution.py:262
  8.7 0.7 %stack.15 = f32[1,640]{1,0:T(1,128)S(1)} reshape(f32[640]{0:T(1024)} %param.15) | data formatting | bytes 5120 | tf_op jit(solution)/shard_map/stack | solution.py:262
  9.4 0.0 copy-start.2
  9.4 1.1 %copy-done.2 = bf16[640,640]{1,0:T(8,128)(2,1)S(1)} copy-done((bf16[640,640]{1,0:T(8,128)(2,1)S(1)}, bf16[640,640]{1,0:T(8,128)(2,1)}, u32[]{:S(2)}) %copy-start.2) | copy-done | bytes 819224
  10.6 0.0 copy-start.3
  10.6 1.0 %copy-done.3 = bf16[1,256,640]{2,1,0:T(8,128)(2,1)S(1)} copy-done((bf16[1,256,640]{2,1,0:T(8,128)(2,1)S(1)}, bf16[1,256,640]{2,1,0:T(8,128)(2,1)}, u32[]{:S(2)}) %copy-start.3) | copy-done | bytes 327704
  11.5 1.4 %fetch.1 = (bf16[1,256,640]{2,1,0:T(8,128)(2,1)S(1)}, bf16[640,640]{1,0:T(8,128)(2,1)S(1)}, f32[3,640]{1,0:T(4,128)S(1)}, bf16[2,640,640]{2,1,0:T(8,128)(2,1)S(1)}) custom-call(bf16[1,256,640]{2,1,0:T(8,128)(2,1)S(1)} %copy-done.3, bf16[640,640]{1,0:T(8,128)(2,1)S(1)} %copy-done.2, f32[3,640]{1,0:T(4,128)S(1)} %pad_maximum_fusion.refs_2_, ...), custom_call_target="tpu_custom_call" | custom-call | bytes 2309120 | tf_op jit(solution)/shard_map/fetch/pallas_call | solution.py:234
  13.0 6.4 %all-to-all-done = bf16[32,8,640]{2,1,0:T(8,128)(2,1)S(1)} async-done(((bf16[32,8,640]{2,1,0:T(8,128)(2,1)}), bf16[32,8,640]{2,1,0:T(8,128)(2,1)S(1)}, u32[]{:S(2)}, u32[]{:S(2)}) %all-to-all-start) | async-done | bytes 327712 | tf_op jit(solution)/shard_map/all_to_all | solution.py:251
  19.4 1.0 %join.1 = (f32[256,640]{1,0:T(8,128)S(1)}, f32[32,128]{1,0:T(8,128)S(1)}) custom-call(bf16[256,640]{1,0:T(8,128)(2,1)S(1)} %bitcast.18, bf16[256,640]{1,0:T(8,128)(2,1)S(1)} %bitcast.16, bf16[640,640]{1,0:T(8,128)(2,1)S(1)} %get-tuple-element.14.weight_ref), custom_call_target="tpu_custom_call" | custom-call | flops 209715200 | bytes 32000000 | tf_op jit(solution)/shard_map/join/pallas_call | solution.py:267
  20.4 9.3 %all_to_all.39 = f32[32,1,128]{2,1,0:T(1,128)S(1)} all-to-all(f32[32,1,128]{2,1,0:T(1,128)S(1)} %bitcast.20), channel_id=1, replica_groups=mesh['groups'=1,'frames'=32] {'frames'}, dimensions={0} | all-to-all | bytes 32768 | tf_op jit(solution)/shard_map/all_to_all | solution.py:251
  29.7 0.0 copy-start
  29.7 0.0 copy-start.1
  29.7 4.1 %conv.1 = (f32[256,640]{1,0:T(8,128)S(1)}, bf16[256,640]{1,0:T(8,128)(2,1)S(1)}) custom-call(s32[1]{0:T(128)} %constant.15.clone.1.clip_ref, f32[256,640]{1,0:T(8,128)S(1)} %get-tuple-element.15.joined_ref, f32[32,128]{1,0:T(8,128)S(1)} %bitcast.19, f32[3,640]{1,0:T(4,128)S(1)} %get-tuple-element.17.gains_ref, ...), custom_call_target="tpu_custom_call" | custom-call | flops 1887436800 | bytes 9000000 | tf_op jit(solution)/shard_map/conv/pallas_call | solution.py:284
  33.8 13.8 %all_to_all.40 = bf16[32,8,640]{2,1,0:T(8,128)(2,1)S(1)} all-to-all(bf16[32,8,640]{2,1,0:T(8,128)(2,1)S(1)} %bitcast.17), channel_id=1, replica_groups=mesh['groups'=1,'frames'=32] {'frames'}, dimensions={0} | all-to-all | bytes 655360 | tf_op jit(solution)/shard_map/all_to_all | solution.py:251
  47.5 0.0 copy-done
  47.5 0.0 copy-done.1
  47.5 2.8 %attend.1 = bf16[256,640]{1,0:T(8,128)(2,1)S(1)} custom-call(bf16[256,640]{1,0:T(8,128)(2,1)S(1)} %bitcast.14, f32[3,640]{1,0:T(4,128)S(1)} %get-tuple-element.17.gains_ref, bf16[640,1920]{1,0:T(8,128)(2,1)S(1)} %copy-done, bf16[640,640]{1,0:T(8,128)(2,1)S(1)} %copy-done.1), custom_call_target="tpu_custom_call" | custom-call | flops 838860800 | bytes 4000000 | tf_op jit(solution)/shard_map/attend/pallas_call | solution.py:312
  50.4 14.1 %all_to_all.41 = bf16[32,8,640]{2,1,0:T(8,128)(2,1)S(1)} all-to-all(bf16[32,8,640]{2,1,0:T(8,128)(2,1)S(1)} %bitcast.15), channel_id=1, replica_groups=mesh['groups'=1,'frames'=32] {'frames'}, dimensions={0} | all-to-all | bytes 655360 | tf_op jit(solution)/shard_map/all_to_all | solution.py:251
  64.4 0.8 %fusion.1 = bf16[1,256,640]{2,1,0:T(8,128)(2,1)} fusion(f32[256,640]{1,0:T(8,128)S(1)} %get-tuple-element.19, bf16[32,8,640]{2,1,0:T(8,128)(2,1)S(1)} %all_to_all.41), kind=kLoop, calls=%fused_computation.2 | loop fusion | flops 491520 | bytes 1310720 | tf_op jit(solution)/shard_map/convert_element_type | solution.py:329
  (1 shorter events, 0.0 us)
Async XLA Ops:
  0.0 19.4 %all-to-all-start = ((bf16[32,8,640]{2,1,0:T(8,128)(2,1)}), bf16[32,8,640]{2,1,0:T(8,128)(2,1)S(1)}, u32[]{:S(2)}, u32[]{:S(2)}) async-start(bf16[32,8,640]{2,1,0:T(8,128)(2,1)} %param.10), calls=%async_computation | async-start | bytes 655360 | tf_op jit(solution)/shard_map/all_to_all | solution.py:251
  9.4 1.1 %copy-start.2 = (bf16[640,640]{1,0:T(8,128)(2,1)S(1)}, bf16[640,640]{1,0:T(8,128)(2,1)}, u32[]{:S(2)}) copy-start(bf16[640,640]{1,0:T(8,128)(2,1)} %refs_1_.1) | copy-start | bytes 2457604
  10.6 1.0 %copy-start.3 = (bf16[1,256,640]{2,1,0:T(8,128)(2,1)S(1)}, bf16[1,256,640]{2,1,0:T(8,128)(2,1)}, u32[]{:S(2)}) copy-start(bf16[1,256,640]{2,1,0:T(8,128)(2,1)} %refs_0_.1) | copy-start | bytes 983044
  29.7 17.8 %copy-start = (bf16[640,1920]{1,0:T(8,128)(2,1)S(1)}, bf16[640,1920]{1,0:T(8,128)(2,1)}, u32[]{:S(2)}) copy-start(bf16[640,1920]{1,0:T(8,128)(2,1)} %qkv_ref.1) | copy-start | bytes 7372804
  29.7 17.8 %copy-start.1 = (bf16[640,640]{1,0:T(8,128)(2,1)S(1)}, bf16[640,640]{1,0:T(8,128)(2,1)}, u32[]{:S(2)}) copy-start(bf16[640,640]{1,0:T(8,128)(2,1)} %out_ref.1) | copy-start | bytes 2457604

commit v7 on v6

--- a/solution.py
+++ b/solution.py
@@ -14,8 +14,8 @@
 CLIP = 32
 W = 32
 LANES = 128
-EARLY = 2
-COUNTS = (2, 1, 3, 3)
+EARLY = 3
+COUNTS = (3, 3, 3)
 
 norm_epsilon = 1e-05
 F32 = jnp.float32
@@ -217,30 +217,41 @@
 
 
 def fetch_kernel(count, *refs):
-    sem = refs[-1]
-    taps_hbm, taps_ref = refs[count], refs[-2]
+    for i in range(count):
+        refs[count + i][...] = refs[i][...]
+
+
+def fetch(*arrays):
+    size = sum(a.size * a.dtype.itemsize for a in arrays)
+    return pl.pallas_call(
+        functools.partial(fetch_kernel, len(arrays)),
+        out_shape=tuple(jax.ShapeDtypeStruct(a.shape, a.dtype) for a in arrays),
+        in_specs=[VMEM] * len(arrays),
+        out_specs=(VMEM,) * len(arrays),
+        compiler_params=params(1),
+        cost_estimate=cost(0, 2 * size),
+        name="fetch",
+    )(*arrays)
+
+
+def taps_kernel(taps_hbm, after_ref, taps_ref, sem):
     copy = pltpu.make_async_copy(taps_hbm.at[pl.ds(0, EARLY)], taps_ref, sem)
     copy.start()
-    for i in range(count):
-        refs[count + 1 + i][...] = refs[i][...]
     copy.wait()
 
 
-def fetch(conv_weight, *arrays):
-    count = len(arrays)
-    size = sum(a.size * a.dtype.itemsize for a in arrays)
-    shapes = [jax.ShapeDtypeStruct(a.shape, a.dtype) for a in arrays]
-    shapes.append(jax.ShapeDtypeStruct((EARLY,) + conv_weight.shape[1:], conv_weight.dtype))
+def fetch_taps(conv_weight, after):
+    shape = (EARLY,) + conv_weight.shape[1:]
     return pl.pallas_call(
-        functools.partial(fetch_kernel, count),
-        out_shape=tuple(shapes),
-        in_specs=[VMEM] * count + [pl.BlockSpec(memory_space=pl.ANY)],
-        out_specs=(VMEM,) * (count + 1),
+        taps_kernel,
+        out_shape=jax.ShapeDtypeStruct(shape, conv_weight.dtype),
+        in_specs=[pl.BlockSpec(memory_space=pl.ANY), VMEM],
+        out_specs=VMEM,
         scratch_shapes=[pltpu.SemaphoreType.DMA],
-        compiler_params=params(44),
-        cost_estimate=cost(0, 2 * size),
-        name="fetch",
-    )(*arrays, conv_weight)
+        compiler_params=params(48),
+        cost_estimate=cost(0, 6e6),
+        name="taps",
+    )(conv_weight, after)
 
 
 def cost(flops, moved):
@@ -260,7 +271,7 @@
     rows = frame_count * per_dev
     own_control = exchange(control.reshape(rows, chans)).reshape(devices, f_dev, per_dev, chans)
     gains = jnp.stack((gn_gain, gn_bias, ln_gain))
-    skip, zero_weight, gains, first_taps = fetch(conv_weight, skip, zero_weight, gains)
+    skip, zero_weight, gains = fetch(skip, zero_weight, gains)
     first_frame = lax.axis_index("frames") * f_dev if frame_count > CLIP else jnp.int32(0)
     joined, stats = [], []
     for f in range(f_dev):
@@ -278,6 +289,7 @@
         )(skip[f], own_control[:, f].reshape(pixels, chans), zero_weight)
         joined.append(frame_joined)
         stats.append(frame_stats)
+    first_taps = fetch_taps(conv_weight, stats[0])
     all_stats = exchange(jnp.stack(stats, axis=1).reshape(devices * f_dev, LANES))
     resid, sent = [], []
     for f in range(f_dev):

time: 65.7 us -> 66.4 us (1.011)
  blocking collectives: 37.2 us -> 27.8 us
  waiting for transfers between devices: 6.39 us -> 12.4 us
  starting transfers between devices: 7.33 us -> 9.87 us
  Pallas kernels: 9.32 us -> 10.8 us
    all_to_all x3 -> x2, blocking collectives: 37.2 us -> 27.8 us  [exchange(): lax.all_to_all(blocks, 'frames', split_axis=0, concat_axis=0, tiled=True)]
    all_to_all x1 -> x2, waiting for transfers between devices: 6.39 us -> 12.4 us  [exchange(): lax.all_to_all(blocks, 'frames', split_axis=0, concat_axis=0, tiled=True)]
    all_to_all x1 -> x2, starting transfers between devices: 7.33 us -> 9.87 us  [exchange(): lax.all_to_all(blocks, 'frames', split_axis=0, concat_axis=0, tiled=True)]
    pallas_call x1 -> x2, Pallas kernels: 1.44 us -> 2.54 us  [the longest x1 2.45 us: fetch_taps(): pl.pallas_call(taps_kernel, out_shape=jax.ShapeDtypeStruct(shape, conv_we...]
  transfers between devices with their start and end apart: 1 -> 2, of which waited for: 1 -> 2; matrix products, arithmetic and copies ran while one was open for 3% -> 3% of each run, Pallas kernels for 2% -> 4%
where the time goes in v7:
time: 66.4 us; the launch traced here: 65.9 us
  blocking collectives  27.8 us (42%)
  waiting for transfers between devices  12.4 us (19%)
  Pallas kernels  10.8 us (16%)
  starting transfers between devices  9.87 us (15%)
  local copies, waits for them, and re-layouts  4.19 us (6%)
  other arithmetic  0.8 us (1%)
    all_to_all x2, blocking collectives, exchange(): lax.all_to_all(blocks, 'frames', split_axis=0, concat_axis=0, tiled=True)  27.8 us
    all_to_all x2, waiting for transfers between devices, exchange(): lax.all_to_all(blocks, 'frames', split_axis=0, concat_axis=0, tiled=True)  12.4 us
    all_to_all x2, starting transfers between devices, exchange(): lax.all_to_all(blocks, 'frames', split_axis=0, concat_axis=0, tiled=True)  9.87 us
    pallas_call x1, Pallas kernels, body(): pl.pallas_call(conv_kernel, out_shape=(jax.ShapeDtypeStruct((pixels, chan...  3.82 us
    pallas_call x1, Pallas kernels, body(): pl.pallas_call(functools.partial(attend_kernel, per_dev), out_shape=jax.S...  2.83 us
    pallas_call x1, Pallas kernels, fetch_taps(): pl.pallas_call(taps_kernel, out_shape=jax.ShapeDtypeStruct(shape, conv_we...  2.45 us
    unnamed x8, local copies, waits for them, and re-layouts  2.12 us
    another operation x3, local copies, waits for them, and re-layouts, body(): gains = jnp.stack((gn_gain, gn_bias, ln_gain))  2.07 us
  transfers between devices with their start and end apart: 2, of which 2 were waited for; matrix products, arithmetic and copies ran while one was open for 3% of the time, Pallas kernels for 4%

profile of v7, /device:TPU:0, one launch (start us, length us, event | category | flops | bytes accessed | tf_op | source)
XLA Modules:
  0.0 65.9 jit_solution(937739509236504411)
XLA Ops:
  0.0 7.3 %all-to-all-start = ((bf16[32,8,640]{2,1,0:T(8,128)(2,1)}), bf16[32,8,640]{2,1,0:T(8,128)(2,1)S(1)}, u32[]{:S(2)}, u32[]{:S(2)}) async-start(bf16[32,8,640]{2,1,0:T(8,128)(2,1)} %param.10), calls=%async_computation | async-start | bytes 655360 | tf_op jit(solution)/shard_map/all_to_all | solution.py:262
  7.3 0.7 %stack.13 = f32[1,640]{1,0:T(1,128)S(1)} reshape(f32[640]{0:T(1024)} %param.12) | data formatting | bytes 5120 | tf_op jit(solution)/shard_map/stack | solution.py:273
  8.0 0.7 %stack.14 = f32[1,640]{1,0:T(1,128)S(1)} reshape(f32[640]{0:T(1024)} %param.13) | data formatting | bytes 5120 | tf_op jit(solution)/shard_map/stack | solution.py:273
  8.7 0.7 %stack.15 = f32[1,640]{1,0:T(1,128)S(1)} reshape(f32[640]{0:T(1024)} %param.15) | data formatting | bytes 5120 | tf_op jit(solution)/shard_map/stack | solution.py:273
  9.4 0.0 copy-start.2
  9.4 1.1 %copy-done.2 = bf16[640,640]{1,0:T(8,128)(2,1)S(1)} copy-done((bf16[640,640]{1,0:T(8,128)(2,1)S(1)}, bf16[640,640]{1,0:T(8,128)(2,1)}, u32[]{:S(2)}) %copy-start.2) | copy-done | bytes 819224
  10.6 0.0 copy-start.3
  10.6 1.0 %copy-done.3 = bf16[1,256,640]{2,1,0:T(8,128)(2,1)S(1)} copy-done((bf16[1,256,640]{2,1,0:T(8,128)(2,1)S(1)}, bf16[1,256,640]{2,1,0:T(8,128)(2,1)}, u32[]{:S(2)}) %copy-start.3) | copy-done | bytes 327704
  11.5 0.1 fetch.1
  11.6 7.7 %all-to-all-done = bf16[32,8,640]{2,1,0:T(8,128)(2,1)S(1)} async-done(((bf16[32,8,640]{2,1,0:T(8,128)(2,1)}), bf16[32,8,640]{2,1,0:T(8,128)(2,1)S(1)}, u32[]{:S(2)}, u32[]{:S(2)}) %all-to-all-start) | async-done | bytes 327712 | tf_op jit(solution)/shard_map/all_to_all | solution.py:262
  19.4 1.6 %join.1 = (f32[256,640]{1,0:T(8,128)S(1)}, f32[32,128]{1,0:T(8,128)}) custom-call(bf16[256,640]{1,0:T(8,128)(2,1)S(1)} %bitcast.18, bf16[256,640]{1,0:T(8,128)(2,1)S(1)} %bitcast.16, bf16[640,640]{1,0:T(8,128)(2,1)S(1)} %get-tuple-element.13.weight_ref), custom_call_target="tpu_custom_call" | custom-call | flops 209715200 | bytes 32000000 | tf_op jit(solution)/shard_map/join/pallas_call | solution.py:278
  21.0 2.5 %all-to-all-start.1 = ((f32[32,1,128]{2,1,0:T(1,128)}), f32[32,1,128]{2,1,0:T(1,128)S(1)}, u32[]{:S(2)}, u32[]{:S(2)}) async-start(f32[32,1,128]{2,1,0:T(1,128)} %bitcast.3), calls=%async_computation.1 | async-start | bytes 32768 | tf_op jit(solution)/shard_map/all_to_all | solution.py:262
  23.5 2.5 %taps.1.first_ref = bf16[3,640,640]{2,1,0:T(8,128)(2,1)S(1)} custom-call(bf16[9,640,640]{2,1,0:T(8,128)(2,1)} %weight_hbm.1, f32[32,128]{1,0:T(8,128)} %get-tuple-element.15.after_ref), custom_call_target="tpu_custom_call" | custom-call | bytes 6000000 | tf_op jit(solution)/shard_map/taps/pallas_call | solution.py:245
  26.0 4.6 %all-to-all-done.1 = f32[32,1,128]{2,1,0:T(1,128)S(1)} async-done(((f32[32,1,128]{2,1,0:T(1,128)}), f32[32,1,128]{2,1,0:T(1,128)S(1)}, u32[]{:S(2)}, u32[]{:S(2)}) %all-to-all-start.1) | async-done | bytes 16416 | tf_op jit(solution)/shard_map/all_to_all | solution.py:262
  30.6 0.0 copy-start
  30.6 0.0 copy-start.1
  30.6 3.8 %conv.1 = (f32[256,640]{1,0:T(8,128)S(1)}, bf16[256,640]{1,0:T(8,128)(2,1)S(1)}) custom-call(s32[1]{0:T(128)} %constant.15.clone.1.clip_ref, f32[256,640]{1,0:T(8,128)S(1)} %get-tuple-element.14.joined_ref, f32[32,128]{1,0:T(8,128)S(1)} %bitcast.19, f32[3,640]{1,0:T(4,128)S(1)} %get-tuple-element.16.gains_ref, bf16[3,640,640]{2,1,0:T(8,128)(2,1)S(1)} %taps.1.first_ref, ...), custom_call_target="tpu_custom_call" | custom-call | flops 1887436800 | bytes 9000000 | tf_op jit(solution)/shard_map/conv/pallas_call | solution.py:296
  34.5 13.8 %all_to_all.39 = bf16[32,8,640]{2,1,0:T(8,128)(2,1)S(1)} all-to-all(bf16[32,8,640]{2,1,0:T(8,128)(2,1)S(1)} %bitcast.17), channel_id=1, replica_groups=mesh['groups'=1,'frames'=32] {'frames'}, dimensions={0} | all-to-all | bytes 655360 | tf_op jit(solution)/shard_map/all_to_all | solution.py:262
  48.2 0.0 copy-done
  48.2 0.0 copy-done.1
  48.2 2.8 %attend.1 = bf16[256,640]{1,0:T(8,128)(2,1)S(1)} custom-call(bf16[256,640]{1,0:T(8,128)(2,1)S(1)} %bitcast.14, f32[3,640]{1,0:T(4,128)S(1)} %get-tuple-element.16.gains_ref, bf16[640,1920]{1,0:T(8,128)(2,1)S(1)} %copy-done, bf16[640,640]{1,0:T(8,128)(2,1)S(1)} %copy-done.1), custom_call_target="tpu_custom_call" | custom-call | flops 838860800 | bytes 4000000 | tf_op jit(solution)/shard_map/attend/pallas_call | solution.py:324
  51.1 14.1 %all_to_all.40 = bf16[32,8,640]{2,1,0:T(8,128)(2,1)S(1)} all-to-all(bf16[32,8,640]{2,1,0:T(8,128)(2,1)S(1)} %bitcast.15), channel_id=1, replica_groups=mesh['groups'=1,'frames'=32] {'frames'}, dimensions={0} | all-to-all | bytes 655360 | tf_op jit(solution)/shard_map/all_to_all | solution.py:262
  65.1 0.8 %fusion.1 = bf16[1,256,640]{2,1,0:T(8,128)(2,1)} fusion(f32[256,640]{1,0:T(8,128)S(1)} %get-tuple-element.17, bf16[32,8,640]{2,1,0:T(8,128)(2,1)S(1)} %all_to_all.40), kind=kLoop, calls=%fused_computation.2 | loop fusion | flops 491520 | bytes 1310720 | tf_op jit(solution)/shard_map/convert_element_type | solution.py:341
  (1 shorter events, 0.0 us)
Async XLA Ops:
  0.0 19.4 %all-to-all-start = ((bf16[32,8,640]{2,1,0:T(8,128)(2,1)}), bf16[32,8,640]{2,1,0:T(8,128)(2,1)S(1)}, u32[]{:S(2)}, u32[]{:S(2)}) async-start(bf16[32,8,640]{2,1,0:T(8,128)(2,1)} %param.10), calls=%async_computation | async-start | bytes 655360 | tf_op jit(solution)/shard_map/all_to_all | solution.py:262
  9.4 1.1 %copy-start.2 = (bf16[640,640]{1,0:T(8,128)(2,1)S(1)}, bf16[640,640]{1,0:T(8,128)(2,1)}, u32[]{:S(2)}) copy-start(bf16[640,640]{1,0:T(8,128)(2,1)} %refs_1_.1) | copy-start | bytes 2457604
  10.6 1.0 %copy-start.3 = (bf16[1,256,640]{2,1,0:T(8,128)(2,1)S(1)}, bf16[1,256,640]{2,1,0:T(8,128)(2,1)}, u32[]{:S(2)}) copy-start(bf16[1,256,640]{2,1,0:T(8,128)(2,1)} %refs_0_.1) | copy-start | bytes 983044
  21.0 9.7 %all-to-all-start.1 = ((f32[32,1,128]{2,1,0:T(1,128)}), f32[32,1,128]{2,1,0:T(1,128)S(1)}, u32[]{:S(2)}, u32[]{:S(2)}) async-start(f32[32,1,128]{2,1,0:T(1,128)} %bitcast.3), calls=%async_computation.1 | async-start | bytes 32768 | tf_op jit(solution)/shard_map/all_to_all | solution.py:262
  30.6 17.6 %copy-start = (bf16[640,1920]{1,0:T(8,128)(2,1)S(1)}, bf16[640,1920]{1,0:T(8,128)(2,1)}, u32[]{:S(2)}) copy-start(bf16[640,1920]{1,0:T(8,128)(2,1)} %qkv_ref.1) | copy-start | bytes 7372804
  30.6 17.6 %copy-start.1 = (bf16[640,640]{1,0:T(8,128)(2,1)S(1)}, bf16[640,640]{1,0:T(8,128)(2,1)}, u32[]{:S(2)}) copy-start(bf16[640,640]{1,0:T(8,128)(2,1)} %out_ref.1) | copy-start | bytes 2457604

commit v8 on v6

--- a/solution.py
+++ b/solution.py
@@ -14,8 +14,7 @@
 CLIP = 32
 W = 32
 LANES = 128
-EARLY = 2
-COUNTS = (2, 1, 3, 3)
+EARLY_BYTES = 2 * 1024 * 1024
 
 norm_epsilon = 1e-05
 F32 = jnp.float32
@@ -70,14 +69,26 @@
     stats_ref[...] = jnp.broadcast_to(stats[:1], stats_ref.shape)
 
 
+def weight_chunks(chans):
+    line = 3 * chans
+    early = min(line, EARLY_BYTES // (2 * chans) // 256 * 256)
+    return early, line - early, line, 2 * chans, chans
+
+
 def conv_kernel(
     clip_ref, joined_ref, stats_ref, gains_ref, first_ref, weight_hbm, resid_ref, sent_ref,
     window_ref, weight_ref, sems,
 ):
-    copies = [
-        pltpu.make_async_copy(weight_hbm.at[tap + EARLY], weight_ref.at[tap], sems.at[tap])
-        for tap in range(9 - EARLY)
-    ]
+    chunks = weight_chunks(joined_ref.shape[1])
+    early = chunks[0]
+    copies, row = [], early
+    for at, size in enumerate(chunks[1:]):
+        copies.append(
+            pltpu.make_async_copy(
+                weight_hbm.at[pl.ds(row, size)], weight_ref.at[pl.ds(row - early, size)], sems.at[at]
+            )
+        )
+        row += size
     for copy in copies:
         copy.start()
     pixels, chans = joined_ref.shape
@@ -122,23 +133,20 @@
         window_ref[there, 2 * chans :] = right.astype(BF16)
 
     total = joined_ref[...]
-    tap = 0
-    for count in COUNTS:
-        if tap == 0:
+    row = 0
+    for at, size in enumerate(chunks):
+        if at == 0:
             weights = first_ref[...]
         else:
-            taps = slice(tap - EARLY, tap - EARLY + count)
-            for copy in copies[taps]:
-                copy.wait()
-            weights = weight_ref[taps]
-        row = tap // 3 * W
-        start = tap % 3 * chans
+            copies[at - 1].wait()
+            weights = weight_ref[row - early : row - early + size]
+        line, start = divmod(row, 3 * chans)
         total = total + jnp.dot(
-            window_ref[row : row + pixels, start : start + count * chans],
-            weights.reshape(count * chans, chans),
+            window_ref[line * W : line * W + pixels, start : start + size],
+            weights,
             preferred_element_type=F32,
         )
-        tap += count
+        row += size
     resid_ref[...] = total
     sent_ref[...] = total.astype(BF16)
 
@@ -219,7 +227,7 @@
 def fetch_kernel(count, *refs):
     sem = refs[-1]
     taps_hbm, taps_ref = refs[count], refs[-2]
-    copy = pltpu.make_async_copy(taps_hbm.at[pl.ds(0, EARLY)], taps_ref, sem)
+    copy = pltpu.make_async_copy(taps_hbm.at[pl.ds(0, taps_ref.shape[0])], taps_ref, sem)
     copy.start()
     for i in range(count):
         refs[count + 1 + i][...] = refs[i][...]
@@ -230,7 +238,8 @@
     count = len(arrays)
     size = sum(a.size * a.dtype.itemsize for a in arrays)
     shapes = [jax.ShapeDtypeStruct(a.shape, a.dtype) for a in arrays]
-    shapes.append(jax.ShapeDtypeStruct((EARLY,) + conv_weight.shape[1:], conv_weight.dtype))
+    chans = conv_weight.shape[1]
+    shapes.append(jax.ShapeDtypeStruct((weight_chunks(chans)[0], chans), conv_weight.dtype))
     return pl.pallas_call(
         functools.partial(fetch_kernel, count),
         out_shape=tuple(shapes),
@@ -259,6 +268,7 @@
     frame_count, per_dev, _ = control.shape
     rows = frame_count * per_dev
     own_control = exchange(control.reshape(rows, chans)).reshape(devices, f_dev, per_dev, chans)
+    conv_weight = conv_weight.reshape(9 * chans, chans)
     gains = jnp.stack((gn_gain, gn_bias, ln_gain))
     skip, zero_weight, gains, first_taps = fetch(conv_weight, skip, zero_weight, gains)
     first_frame = lax.axis_index("frames") * f_dev if frame_count > CLIP else jnp.int32(0)
@@ -291,8 +301,8 @@
             out_specs=(VMEM, VMEM),
             scratch_shapes=[
                 pltpu.VMEM((pixels + 2 * W, 3 * chans), BF16),
-                pltpu.VMEM((9 - EARLY, chans, chans), BF16),
-                pltpu.SemaphoreType.DMA((9 - EARLY,)),
+                pltpu.VMEM((9 * chans - weight_chunks(chans)[0], chans), BF16),
+                pltpu.SemaphoreType.DMA((4,)),
             ],
             compiler_params=params(50),
             cost_estimate=cost(18 * pixels * chans * chans, 9e6),

time: 65.7 us -> 65.8 us (level)
  no operation moved by 1% of the time
where the time goes in v8:
time: 65.8 us; the launch traced here: 65.3 us
  blocking collectives  37.2 us (57%)
  Pallas kernels  9.55 us (15%)
  starting transfers between devices  7.33 us (11%)
  waiting for transfers between devices  6.27 us (10%)
  local copies, waits for them, and re-layouts  4.19 us (6%)
  other arithmetic  0.8 us (1%)
    all_to_all x3, blocking collectives, exchange(): lax.all_to_all(blocks, 'frames', split_axis=0, concat_axis=0, tiled=True)  37.2 us
    all_to_all x1, starting transfers between devices, exchange(): lax.all_to_all(blocks, 'frames', split_axis=0, concat_axis=0, tiled=True)  7.33 us
    all_to_all x1, waiting for transfers between devices, exchange(): lax.all_to_all(blocks, 'frames', split_axis=0, concat_axis=0, tiled=True)  6.27 us
    pallas_call x1, Pallas kernels, body(): pl.pallas_call(conv_kernel, out_shape=(jax.ShapeDtypeStruct((pixels, chan...  4.19 us
    pallas_call x1, Pallas kernels, body(): pl.pallas_call(functools.partial(attend_kernel, per_dev), out_shape=jax.S...  2.83 us
    unnamed x8, local copies, waits for them, and re-layouts  2.12 us
    another operation x3, local copies, waits for them, and re-layouts, body(): gains = jnp.stack((gn_gain, gn_bias, ln_gain))  2.07 us
    pallas_call x1, Pallas kernels, fetch(): pl.pallas_call(functools.partial(fetch_kernel, count), out_shape=tuple(sh...  1.55 us
  transfers between devices with their start and end apart: 1, of which 1 were waited for; matrix products, arithmetic and copies ran while one was open for 3% of the time, Pallas kernels for 2%

profile of v8, /device:TPU:0, one launch (start us, length us, event | category | flops | bytes accessed | tf_op | source)
XLA Modules:
  0.0 65.3 jit_solution(4146149216577285718)
XLA Ops:
  0.0 7.3 %all-to-all-start = ((bf16[32,8,640]{2,1,0:T(8,128)(2,1)}), bf16[32,8,640]{2,1,0:T(8,128)(2,1)S(1)}, u32[]{:S(2)}, u32[]{:S(2)}) async-start(bf16[32,8,640]{2,1,0:T(8,128)(2,1)} %param.10), calls=%async_computation | async-start | bytes 655360 | tf_op jit(solution)/shard_map/all_to_all | solution.py:260
  7.3 0.7 %stack.13 = f32[1,640]{1,0:T(1,128)S(1)} reshape(f32[640]{0:T(1024)} %param.12) | data formatting | bytes 5120 | tf_op jit(solution)/shard_map/stack | solution.py:272
  8.0 0.7 %stack.14 = f32[1,640]{1,0:T(1,128)S(1)} reshape(f32[640]{0:T(1024)} %param.13) | data formatting | bytes 5120 | tf_op jit(solution)/shard_map/stack | solution.py:272
  8.7 0.7 %stack.15 = f32[1,640]{1,0:T(1,128)S(1)} reshape(f32[640]{0:T(1024)} %param.15) | data formatting | bytes 5120 | tf_op jit(solution)/shard_map/stack | solution.py:272
  9.4 0.0 copy-start.2
  9.4 1.1 %copy-done.2 = bf16[640,640]{1,0:T(8,128)(2,1)S(1)} copy-done((bf16[640,640]{1,0:T(8,128)(2,1)S(1)}, bf16[640,640]{1,0:T(8,128)(2,1)}, u32[]{:S(2)}) %copy-start.2) | copy-done | bytes 819224
  10.6 0.0 copy-start.3
  10.6 1.0 %copy-done.3 = bf16[1,256,640]{2,1,0:T(8,128)(2,1)S(1)} copy-done((bf16[1,256,640]{2,1,0:T(8,128)(2,1)S(1)}, bf16[1,256,640]{2,1,0:T(8,128)(2,1)}, u32[]{:S(2)}) %copy-start.3) | copy-done | bytes 327704
  11.5 1.6 %fetch.1 = (bf16[1,256,640]{2,1,0:T(8,128)(2,1)S(1)}, bf16[640,640]{1,0:T(8,128)(2,1)S(1)}, f32[3,640]{1,0:T(4,128)S(1)}, bf16[1536,640]{1,0:T(8,128)(2,1)S(1)}) custom-call(bf16[1,256,640]{2,1,0:T(8,128)(2,1)S(1)} %copy-done.3, bf16[640,640]{1,0:T(8,128)(2,1)S(1)} %copy-done.2, f32[3,640]{1,0:T(4,128)S(1)} %pad_maximum_fusion.refs_2_, ...), custom_call_target="tpu_custom_call" | custom-call | bytes 2309120 | tf_op jit(solution)/shard_map/fetch/pallas_call | solution.py:243
  13.1 6.3 %all-to-all-done = bf16[32,8,640]{2,1,0:T(8,128)(2,1)S(1)} async-done(((bf16[32,8,640]{2,1,0:T(8,128)(2,1)}), bf16[32,8,640]{2,1,0:T(8,128)(2,1)S(1)}, u32[]{:S(2)}, u32[]{:S(2)}) %all-to-all-start) | async-done | bytes 327712 | tf_op jit(solution)/shard_map/all_to_all | solution.py:260
  19.4 1.0 %join.1 = (f32[256,640]{1,0:T(8,128)S(1)}, f32[32,128]{1,0:T(8,128)S(1)}) custom-call(bf16[256,640]{1,0:T(8,128)(2,1)S(1)} %bitcast.19, bf16[256,640]{1,0:T(8,128)(2,1)S(1)} %bitcast.17, bf16[640,640]{1,0:T(8,128)(2,1)S(1)} %get-tuple-element.14.weight_ref), custom_call_target="tpu_custom_call" | custom-call | flops 209715200 | bytes 32000000 | tf_op jit(solution)/shard_map/join/pallas_call | solution.py:277
  20.4 9.3 %all_to_all.39 = f32[32,1,128]{2,1,0:T(1,128)S(1)} all-to-all(f32[32,1,128]{2,1,0:T(1,128)S(1)} %bitcast.21), channel_id=1, replica_groups=mesh['groups'=1,'frames'=32] {'frames'}, dimensions={0} | all-to-all | bytes 32768 | tf_op jit(solution)/shard_map/all_to_all | solution.py:260
  29.7 0.0 copy-start
  29.7 0.0 copy-start.1
  29.7 4.2 %conv.1 = (f32[256,640]{1,0:T(8,128)S(1)}, bf16[256,640]{1,0:T(8,128)(2,1)S(1)}) custom-call(s32[1]{0:T(128)} %constant.15.clone.1.clip_ref, f32[256,640]{1,0:T(8,128)S(1)} %get-tuple-element.15.joined_ref, f32[32,128]{1,0:T(8,128)S(1)} %bitcast.20, f32[3,640]{1,0:T(4,128)S(1)} %get-tuple-element.17.gains_ref, ...), custom_call_target="tpu_custom_call" | custom-call | flops 1887436800 | bytes 9000000 | tf_op jit(solution)/shard_map/conv/pallas_call | solution.py:294
  33.9 13.8 %all_to_all.40 = bf16[32,8,640]{2,1,0:T(8,128)(2,1)S(1)} all-to-all(bf16[32,8,640]{2,1,0:T(8,128)(2,1)S(1)} %bitcast.18), channel_id=1, replica_groups=mesh['groups'=1,'frames'=32] {'frames'}, dimensions={0} | all-to-all | bytes 655360 | tf_op jit(solution)/shard_map/all_to_all | solution.py:260
  47.6 0.0 copy-done
  47.6 0.0 copy-done.1
  47.6 2.8 %attend.1 = bf16[256,640]{1,0:T(8,128)(2,1)S(1)} custom-call(bf16[256,640]{1,0:T(8,128)(2,1)S(1)} %bitcast.15, f32[3,640]{1,0:T(4,128)S(1)} %get-tuple-element.17.gains_ref, bf16[640,1920]{1,0:T(8,128)(2,1)S(1)} %copy-done, bf16[640,640]{1,0:T(8,128)(2,1)S(1)} %copy-done.1), custom_call_target="tpu_custom_call" | custom-call | flops 838860800 | bytes 4000000 | tf_op jit(solution)/shard_map/attend/pallas_call | solution.py:322
  50.5 14.1 %all_to_all.41 = bf16[32,8,640]{2,1,0:T(8,128)(2,1)S(1)} all-to-all(bf16[32,8,640]{2,1,0:T(8,128)(2,1)S(1)} %bitcast.16), channel_id=1, replica_groups=mesh['groups'=1,'frames'=32] {'frames'}, dimensions={0} | all-to-all | bytes 655360 | tf_op jit(solution)/shard_map/all_to_all | solution.py:260
  64.6 0.8 %fusion.1 = bf16[1,256,640]{2,1,0:T(8,128)(2,1)} fusion(f32[256,640]{1,0:T(8,128)S(1)} %get-tuple-element.19, bf16[32,8,640]{2,1,0:T(8,128)(2,1)S(1)} %all_to_all.41), kind=kLoop, calls=%fused_computation.2 | loop fusion | flops 491520 | bytes 1310720 | tf_op jit(solution)/shard_map/convert_element_type | solution.py:339
  (1 shorter events, 0.0 us)
Async XLA Ops:
  0.0 19.4 %all-to-all-start = ((bf16[32,8,640]{2,1,0:T(8,128)(2,1)}), bf16[32,8,640]{2,1,0:T(8,128)(2,1)S(1)}, u32[]{:S(2)}, u32[]{:S(2)}) async-start(bf16[32,8,640]{2,1,0:T(8,128)(2,1)} %param.10), calls=%async_computation | async-start | bytes 655360 | tf_op jit(solution)/shard_map/all_to_all | solution.py:260
  9.4 1.1 %copy-start.2 = (bf16[640,640]{1,0:T(8,128)(2,1)S(1)}, bf16[640,640]{1,0:T(8,128)(2,1)}, u32[]{:S(2)}) copy-start(bf16[640,640]{1,0:T(8,128)(2,1)} %refs_1_.1) | copy-start | bytes 2457604
  10.6 1.0 %copy-start.3 = (bf16[1,256,640]{2,1,0:T(8,128)(2,1)S(1)}, bf16[1,256,640]{2,1,0:T(8,128)(2,1)}, u32[]{:S(2)}) copy-start(bf16[1,256,640]{2,1,0:T(8,128)(2,1)} %refs_0_.1) | copy-start | bytes 983044
  29.7 18.0 %copy-start = (bf16[640,1920]{1,0:T(8,128)(2,1)S(1)}, bf16[640,1920]{1,0:T(8,128)(2,1)}, u32[]{:S(2)}) copy-start(bf16[640,1920]{1,0:T(8,128)(2,1)} %qkv_ref.1) | copy-start | bytes 7372804
  29.7 18.0 %copy-start.1 = (bf16[640,640]{1,0:T(8,128)(2,1)S(1)}, bf16[640,640]{1,0:T(8,128)(2,1)}, u32[]{:S(2)}) copy-start(bf16[640,640]{1,0:T(8,128)(2,1)} %out_ref.1) | copy-start | bytes 2457604

commit v9 on v6

--- a/solution.py
+++ b/solution.py
@@ -51,18 +51,20 @@
     return jnp.concatenate(blocks, axis=axis)
 
 
-def join_kernel(skip_ref, control_ref, weight_ref, joined_ref, stats_ref):
+def join_kernel(
+    skip_ref, control_ref, weight_ref, gather_ref, spread_ref, joined_ref, stats_ref
+):
     pixels, chans = skip_ref.shape
     zero_out = jnp.dot(control_ref[...], weight_ref[...], preferred_element_type=F32).astype(BF16)
     joined = skip_ref[...].astype(F32) + zero_out.astype(F32)
     joined_ref[...] = joined
-    members = group_members(chans, 0)
+    members = gather_ref[...]
     sums = jnp.broadcast_to(jnp.sum(joined, axis=0, keepdims=True), (8, chans))
     group_sums = member_dot(sums, members)
     lane_id = lax.broadcasted_iota(jnp.int32, (8, LANES), 1)
     group_mean = jnp.where(lane_id < GROUPS, group_sums, 0.0)
     group_mean = group_mean * (1.0 / (pixels * (chans // GROUPS)))
-    chan_mean = member_dot(group_mean, group_members(chans, 1))[:1]
+    chan_mean = member_dot(group_mean, spread_ref[...])[:1]
     spread = jnp.sum(jnp.square(joined_ref[...] - chan_mean), axis=0, keepdims=True)
     group_spread = member_dot(jnp.broadcast_to(spread, (8, chans)), members)
     stats = jnp.where(lane_id < GROUPS, group_sums, group_spread)
@@ -71,8 +73,8 @@
 
 
 def conv_kernel(
-    clip_ref, joined_ref, stats_ref, gains_ref, first_ref, weight_hbm, resid_ref, sent_ref,
-    window_ref, weight_ref, sems,
+    clip_ref, joined_ref, stats_ref, spread_ref, gains_ref, first_ref, weight_hbm, resid_ref,
+    sent_ref, window_ref, weight_ref, sems,
 ):
     copies = [
         pltpu.make_async_copy(weight_hbm.at[tap + EARLY], weight_ref.at[tap], sems.at[tap])
@@ -100,7 +102,7 @@
     lane_var = jnp.where(lane_id < GROUPS, lane_between, lane_mean)
     lane_mean = jnp.where(lane_id < GROUPS, lane_mean, 0.0)
     chan_stats = member_dot(
-        jnp.where(row_id == 0, lane_mean, lane_var), group_members(chans, 1)
+        jnp.where(row_id == 0, lane_mean, lane_var), spread_ref[...]
     )
     chan_mean, chan_var = chan_stats[:1], chan_stats[1:2]
     edge = jnp.zeros((W, 3 * chans), BF16)
@@ -217,25 +219,30 @@
 
 
 def fetch_kernel(count, *refs):
-    sem = refs[-1]
-    taps_hbm, taps_ref = refs[count], refs[-2]
+    taps_hbm = refs[count]
+    taps_ref, gather_ref, spread_ref, sem = refs[-4:]
     copy = pltpu.make_async_copy(taps_hbm.at[pl.ds(0, EARLY)], taps_ref, sem)
     copy.start()
     for i in range(count):
         refs[count + 1 + i][...] = refs[i][...]
+    gather_ref[...] = group_members(gather_ref.shape[0], 0)
+    spread_ref[...] = group_members(spread_ref.shape[1], 1)
     copy.wait()
 
 
 def fetch(conv_weight, *arrays):
     count = len(arrays)
+    chans = conv_weight.shape[2]
     size = sum(a.size * a.dtype.itemsize for a in arrays)
     shapes = [jax.ShapeDtypeStruct(a.shape, a.dtype) for a in arrays]
     shapes.append(jax.ShapeDtypeStruct((EARLY,) + conv_weight.shape[1:], conv_weight.dtype))
+    shapes.append(jax.ShapeDtypeStruct((chans, LANES), BF16))
+    shapes.append(jax.ShapeDtypeStruct((LANES, chans), BF16))
     return pl.pallas_call(
         functools.partial(fetch_kernel, count),
         out_shape=tuple(shapes),
         in_specs=[VMEM] * count + [pl.BlockSpec(memory_space=pl.ANY)],
-        out_specs=(VMEM,) * (count + 1),
+        out_specs=(VMEM,) * (count + 3),
         scratch_shapes=[pltpu.SemaphoreType.DMA],
         compiler_params=params(44),
         cost_estimate=cost(0, 2 * size),
@@ -260,7 +267,9 @@
     rows = frame_count * per_dev
     own_control = exchange(control.reshape(rows, chans)).reshape(devices, f_dev, per_dev, chans)
     gains = jnp.stack((gn_gain, gn_bias, ln_gain))
-    skip, zero_weight, gains, first_taps = fetch(conv_weight, skip, zero_weight, gains)
+    skip, zero_weight, gains, first_taps, gather, spread = fetch(
+        conv_weight, skip, zero_weight, gains
+    )
     first_frame = lax.axis_index("frames") * f_dev if frame_count > CLIP else jnp.int32(0)
     joined, stats = [], []
     for f in range(f_dev):
@@ -270,12 +279,12 @@
                 jax.ShapeDtypeStruct((pixels, chans), F32),
                 jax.ShapeDtypeStruct((devices, LANES), F32),
             ),
-            in_specs=[VMEM] * 3,
+            in_specs=[VMEM] * 5,
             out_specs=(VMEM, VMEM),
             compiler_params=params(8),
             cost_estimate=cost(2 * pixels * chans * chans, 32e6),
             name="join",
-        )(skip[f], own_control[:, f].reshape(pixels, chans), zero_weight)
+        )(skip[f], own_control[:, f].reshape(pixels, chans), zero_weight, gather, spread)
         joined.append(frame_joined)
         stats.append(frame_stats)
     all_stats = exchange(jnp.stack(stats, axis=1).reshape(devices * f_dev, LANES))
@@ -287,7 +296,7 @@
                 jax.ShapeDtypeStruct((pixels, chans), F32),
                 jax.ShapeDtypeStruct((pixels, chans), BF16),
             ),
-            in_specs=[SMEM] + [VMEM] * 4 + [pl.BlockSpec(memory_space=pl.ANY)],
+            in_specs=[SMEM] + [VMEM] * 5 + [pl.BlockSpec(memory_space=pl.ANY)],
             out_specs=(VMEM, VMEM),
             scratch_shapes=[
                 pltpu.VMEM((pixels + 2 * W, 3 * chans), BF16),
@@ -301,6 +310,7 @@
             ((first_frame + f) // CLIP).reshape(1),
             joined[f],
             all_stats,
+            spread,
             gains,
             first_taps,
             conv_weight,

time: 65.7 us -> 65.6 us (level)
  no operation moved by 1% of the time
where the time goes in v9:
time: 65.6 us; the launch traced here: 65.2 us
  blocking collectives  37.2 us (57%)
  Pallas kernels  9.31 us (14%)
  starting transfers between devices  7.33 us (11%)
  waiting for transfers between devices  6.39 us (10%)
  local copies, waits for them, and re-layouts  4.19 us (6%)
  other arithmetic  0.8 us (1%)
    all_to_all x3, blocking collectives, exchange(): lax.all_to_all(blocks, 'frames', split_axis=0, concat_axis=0, tiled=True)  37.2 us
    all_to_all x1, starting transfers between devices, exchange(): lax.all_to_all(blocks, 'frames', split_axis=0, concat_axis=0, tiled=True)  7.33 us
    all_to_all x1, waiting for transfers between devices, exchange(): lax.all_to_all(blocks, 'frames', split_axis=0, concat_axis=0, tiled=True)  6.39 us
    pallas_call x1, Pallas kernels, body(): pl.pallas_call(conv_kernel, out_shape=(jax.ShapeDtypeStruct((pixels, chan...  4.08 us
    pallas_call x1, Pallas kernels, body(): pl.pallas_call(functools.partial(attend_kernel, per_dev), out_shape=jax.S...  2.83 us
    unnamed x8, local copies, waits for them, and re-layouts  2.12 us
    another operation x3, local copies, waits for them, and re-layouts, body(): gains = jnp.stack((gn_gain, gn_bias, ln_gain))  2.07 us
    pallas_call x1, Pallas kernels, fetch(): pl.pallas_call(functools.partial(fetch_kernel, count), out_shape=tuple(sh...  1.44 us
  transfers between devices with their start and end apart: 1, of which 1 were waited for; matrix products, arithmetic and copies ran while one was open for 3% of the time, Pallas kernels for 2%

profile of v9, /device:TPU:0, one launch (start us, length us, event | category | flops | bytes accessed | tf_op | source)
XLA Modules:
  0.0 65.2 jit_solution(14168044142510380958)
XLA Ops:
  0.0 7.3 %all-to-all-start = ((bf16[32,8,640]{2,1,0:T(8,128)(2,1)}), bf16[32,8,640]{2,1,0:T(8,128)(2,1)S(1)}, u32[]{:S(2)}, u32[]{:S(2)}) async-start(bf16[32,8,640]{2,1,0:T(8,128)(2,1)} %param.10), calls=%async_computation | async-start | bytes 655360 | tf_op jit(solution)/shard_map/all_to_all | solution.py:258
  7.3 0.7 %stack.13 = f32[1,640]{1,0:T(1,128)S(1)} reshape(f32[640]{0:T(1024)} %param.12) | data formatting | bytes 5120 | tf_op jit(solution)/shard_map/stack | solution.py:269
  8.0 0.7 %stack.14 = f32[1,640]{1,0:T(1,128)S(1)} reshape(f32[640]{0:T(1024)} %param.13) | data formatting | bytes 5120 | tf_op jit(solution)/shard_map/stack | solution.py:269
  8.7 0.7 %stack.15 = f32[1,640]{1,0:T(1,128)S(1)} reshape(f32[640]{0:T(1024)} %param.15) | data formatting | bytes 5120 | tf_op jit(solution)/shard_map/stack | solution.py:269
  9.4 0.0 copy-start.2
  9.4 1.1 %copy-done.2 = bf16[640,640]{1,0:T(8,128)(2,1)S(1)} copy-done((bf16[640,640]{1,0:T(8,128)(2,1)S(1)}, bf16[640,640]{1,0:T(8,128)(2,1)}, u32[]{:S(2)}) %copy-start.2) | copy-done | bytes 819224
  10.6 0.0 copy-start.3
  10.6 1.0 %copy-done.3 = bf16[1,256,640]{2,1,0:T(8,128)(2,1)S(1)} copy-done((bf16[1,256,640]{2,1,0:T(8,128)(2,1)S(1)}, bf16[1,256,640]{2,1,0:T(8,128)(2,1)}, u32[]{:S(2)}) %copy-start.3) | copy-done | bytes 327704
  11.5 1.4 %fetch.1 = (bf16[1,256,640]{2,1,0:T(8,128)(2,1)S(1)}, bf16[640,640]{1,0:T(8,128)(2,1)S(1)}, f32[3,640]{1,0:T(4,128)S(1)}, bf16[2,640,640]{2,1,0:T(8,128)(2,1)S(1...) custom-call(bf16[1,256,640]{2,1,0:T(8,128)(2,1)S(1)} %copy-done.3, bf16[640,640]{1,0:T(8,128)(2,1)S(1)} %copy-done.2, ...), custom_call_target="tpu_custom_call" | custom-call | bytes 2309120 | tf_op jit(solution)/shard_map/fetch/pallas_call | solution.py:241
  13.0 6.4 %all-to-all-done = bf16[32,8,640]{2,1,0:T(8,128)(2,1)S(1)} async-done(((bf16[32,8,640]{2,1,0:T(8,128)(2,1)}), bf16[32,8,640]{2,1,0:T(8,128)(2,1)S(1)}, u32[]{:S(2)}, u32[]{:S(2)}) %all-to-all-start) | async-done | bytes 327712 | tf_op jit(solution)/shard_map/all_to_all | solution.py:258
  19.4 1.0 %join.1 = (f32[256,640]{1,0:T(8,128)S(1)}, f32[32,128]{1,0:T(8,128)S(1)}) custom-call(bf16[256,640]{1,0:T(8,128)(2,1)S(1)} %bitcast.17, bf16[256,640]{1,0:T(8,128)(2,1)S(1)} %bitcast.16, bf16[640,640]{1,0:T(8,128)(2,1)S(1)} %get-tuple-element.16.weight_ref, bf16[640,128]{1,0:T(8,128)(2,1)S(1)} %get-tuple-element.17.gather_ref, ...), custom_call_target="tpu_custom_call" | custom-call | flops 209715200 | bytes 32000000 | tf_op jit(solution)/shard_map/join/pallas_call | solution.py:276
  20.3 9.3 %all_to_all.39 = f32[32,1,128]{2,1,0:T(1,128)S(1)} all-to-all(f32[32,1,128]{2,1,0:T(1,128)S(1)} %bitcast.20), channel_id=1, replica_groups=mesh['groups'=1,'frames'=32] {'frames'}, dimensions={0} | all-to-all | bytes 32768 | tf_op jit(solution)/shard_map/all_to_all | solution.py:258
  29.7 0.0 copy-start
  29.7 0.0 copy-start.1
  29.7 4.1 %conv.1 = (f32[256,640]{1,0:T(8,128)S(1)}, bf16[256,640]{1,0:T(8,128)(2,1)S(1)}) custom-call(s32[1]{0:T(128)} %constant.15.clone.1.clip_ref, f32[256,640]{1,0:T(8,128)S(1)} %get-tuple-element.19.joined_ref, f32[32,128]{1,0:T(8,128)S(1)} %bitcast.19, bf16[128,640]{1,0:T(8,128)(2,1)S(1)} %get-tuple-element.18.spread_ref, ...), custom_call_target="tpu_custom_call" | custom-call | flops 1887436800 | bytes 9000000 | tf_op jit(solution)/shard_map/conv/pallas_call | solution.py:293
  33.8 13.8 %all_to_all.40 = bf16[32,8,640]{2,1,0:T(8,128)(2,1)S(1)} all-to-all(bf16[32,8,640]{2,1,0:T(8,128)(2,1)S(1)} %bitcast.18), channel_id=1, replica_groups=mesh['groups'=1,'frames'=32] {'frames'}, dimensions={0} | all-to-all | bytes 655360 | tf_op jit(solution)/shard_map/all_to_all | solution.py:258
  47.5 0.0 copy-done
  47.5 0.0 copy-done.1
  47.5 2.8 %attend.1 = bf16[256,640]{1,0:T(8,128)(2,1)S(1)} custom-call(bf16[256,640]{1,0:T(8,128)(2,1)S(1)} %bitcast.14, f32[3,640]{1,0:T(4,128)S(1)} %get-tuple-element.21.gains_ref, bf16[640,1920]{1,0:T(8,128)(2,1)S(1)} %copy-done, bf16[640,640]{1,0:T(8,128)(2,1)S(1)} %copy-done.1), custom_call_target="tpu_custom_call" | custom-call | flops 838860800 | bytes 4000000 | tf_op jit(solution)/shard_map/attend/pallas_call | solution.py:322
  50.3 14.1 %all_to_all.41 = bf16[32,8,640]{2,1,0:T(8,128)(2,1)S(1)} all-to-all(bf16[32,8,640]{2,1,0:T(8,128)(2,1)S(1)} %bitcast.15), channel_id=1, replica_groups=mesh['groups'=1,'frames'=32] {'frames'}, dimensions={0} | all-to-all | bytes 655360 | tf_op jit(solution)/shard_map/all_to_all | solution.py:258
  64.4 0.8 %fusion.1 = bf16[1,256,640]{2,1,0:T(8,128)(2,1)} fusion(f32[256,640]{1,0:T(8,128)S(1)} %get-tuple-element.23, bf16[32,8,640]{2,1,0:T(8,128)(2,1)S(1)} %all_to_all.41), kind=kLoop, calls=%fused_computation.2 | loop fusion | flops 491520 | bytes 1310720 | tf_op jit(solution)/shard_map/convert_element_type | solution.py:339
  (1 shorter events, 0.0 us)
Async XLA Ops:
  0.0 19.4 %all-to-all-start = ((bf16[32,8,640]{2,1,0:T(8,128)(2,1)}), bf16[32,8,640]{2,1,0:T(8,128)(2,1)S(1)}, u32[]{:S(2)}, u32[]{:S(2)}) async-start(bf16[32,8,640]{2,1,0:T(8,128)(2,1)} %param.10), calls=%async_computation | async-start | bytes 655360 | tf_op jit(solution)/shard_map/all_to_all | solution.py:258
  9.4 1.1 %copy-start.2 = (bf16[640,640]{1,0:T(8,128)(2,1)S(1)}, bf16[640,640]{1,0:T(8,128)(2,1)}, u32[]{:S(2)}) copy-start(bf16[640,640]{1,0:T(8,128)(2,1)} %refs_1_.1) | copy-start | bytes 2457604
  10.6 1.0 %copy-start.3 = (bf16[1,256,640]{2,1,0:T(8,128)(2,1)S(1)}, bf16[1,256,640]{2,1,0:T(8,128)(2,1)}, u32[]{:S(2)}) copy-start(bf16[1,256,640]{2,1,0:T(8,128)(2,1)} %refs_0_.1) | copy-start | bytes 983044
  29.7 17.9 %copy-start = (bf16[640,1920]{1,0:T(8,128)(2,1)S(1)}, bf16[640,1920]{1,0:T(8,128)(2,1)}, u32[]{:S(2)}) copy-start(bf16[640,1920]{1,0:T(8,128)(2,1)} %qkv_ref.1) | copy-start | bytes 7372804
  29.7 17.9 %copy-start.1 = (bf16[640,640]{1,0:T(8,128)(2,1)S(1)}, bf16[640,640]{1,0:T(8,128)(2,1)}, u32[]{:S(2)}) copy-start(bf16[640,640]{1,0:T(8,128)(2,1)} %out_ref.1) | copy-start | bytes 2457604

commit v10 on v6

--- a/solution.py
+++ b/solution.py
@@ -15,7 +15,7 @@
 W = 32
 LANES = 128
 EARLY = 2
-COUNTS = (2, 1, 3, 3)
+COUNTS = (2, 1, 3, 2, 1)
 
 norm_epsilon = 1e-05
 F32 = jnp.float32

time: 65.7 us -> 65.8 us (level)
  no operation moved by 1% of the time
where the time goes in v10:
time: 65.8 us; the launch traced here: 65.4 us
  blocking collectives  37.2 us (57%)
  Pallas kernels  9.5 us (14%)
  starting transfers between devices  7.33 us (11%)
  waiting for transfers between devices  6.39 us (10%)
  local copies, waits for them, and re-layouts  4.19 us (6%)
  other arithmetic  0.8 us (1%)
    all_to_all x3, blocking collectives, exchange(): lax.all_to_all(blocks, 'frames', split_axis=0, concat_axis=0, tiled=True)  37.2 us
    all_to_all x1, starting transfers between devices, exchange(): lax.all_to_all(blocks, 'frames', split_axis=0, concat_axis=0, tiled=True)  7.33 us
    all_to_all x1, waiting for transfers between devices, exchange(): lax.all_to_all(blocks, 'frames', split_axis=0, concat_axis=0, tiled=True)  6.39 us
    pallas_call x1, Pallas kernels, body(): pl.pallas_call(conv_kernel, out_shape=(jax.ShapeDtypeStruct((pixels, chan...  4.26 us
    pallas_call x1, Pallas kernels, body(): pl.pallas_call(functools.partial(attend_kernel, per_dev), out_shape=jax.S...  2.83 us
    unnamed x8, local copies, waits for them, and re-layouts  2.12 us
    another operation x3, local copies, waits for them, and re-layouts, body(): gains = jnp.stack((gn_gain, gn_bias, ln_gain))  2.07 us
    pallas_call x1, Pallas kernels, fetch(): pl.pallas_call(functools.partial(fetch_kernel, count), out_shape=tuple(sh...  1.44 us
  transfers between devices with their start and end apart: 1, of which 1 were waited for; matrix products, arithmetic and copies ran while one was open for 3% of the time, Pallas kernels for 2%

profile of v10, /device:TPU:0, one launch (start us, length us, event | category | flops | bytes accessed | tf_op | source)
XLA Modules:
  0.0 65.4 jit_solution(7230637968302541828)
XLA Ops:
  0.0 7.3 %all-to-all-start = ((bf16[32,8,640]{2,1,0:T(8,128)(2,1)}), bf16[32,8,640]{2,1,0:T(8,128)(2,1)S(1)}, u32[]{:S(2)}, u32[]{:S(2)}) async-start(bf16[32,8,640]{2,1,0:T(8,128)(2,1)} %param.10), calls=%async_computation | async-start | bytes 655360 | tf_op jit(solution)/shard_map/all_to_all | solution.py:251
  7.3 0.7 %stack.13 = f32[1,640]{1,0:T(1,128)S(1)} reshape(f32[640]{0:T(1024)} %param.12) | data formatting | bytes 5120 | tf_op jit(solution)/shard_map/stack | solution.py:262
  8.0 0.7 %stack.14 = f32[1,640]{1,0:T(1,128)S(1)} reshape(f32[640]{0:T(1024)} %param.13) | data formatting | bytes 5120 | tf_op jit(solution)/shard_map/stack | solution.py:262
  8.7 0.7 %stack.15 = f32[1,640]{1,0:T(1,128)S(1)} reshape(f32[640]{0:T(1024)} %param.15) | data formatting | bytes 5120 | tf_op jit(solution)/shard_map/stack | solution.py:262
  9.4 0.0 copy-start.2
  9.4 1.1 %copy-done.2 = bf16[640,640]{1,0:T(8,128)(2,1)S(1)} copy-done((bf16[640,640]{1,0:T(8,128)(2,1)S(1)}, bf16[640,640]{1,0:T(8,128)(2,1)}, u32[]{:S(2)}) %copy-start.2) | copy-done | bytes 819224
  10.6 0.0 copy-start.3
  10.6 1.0 %copy-done.3 = bf16[1,256,640]{2,1,0:T(8,128)(2,1)S(1)} copy-done((bf16[1,256,640]{2,1,0:T(8,128)(2,1)S(1)}, bf16[1,256,640]{2,1,0:T(8,128)(2,1)}, u32[]{:S(2)}) %copy-start.3) | copy-done | bytes 327704
  11.5 1.4 %fetch.1 = (bf16[1,256,640]{2,1,0:T(8,128)(2,1)S(1)}, bf16[640,640]{1,0:T(8,128)(2,1)S(1)}, f32[3,640]{1,0:T(4,128)S(1)}, bf16[2,640,640]{2,1,0:T(8,128)(2,1)S(1)}) custom-call(bf16[1,256,640]{2,1,0:T(8,128)(2,1)S(1)} %copy-done.3, bf16[640,640]{1,0:T(8,128)(2,1)S(1)} %copy-done.2, f32[3,640]{1,0:T(4,128)S(1)} %pad_maximum_fusion.refs_2_, ...), custom_call_target="tpu_custom_call" | custom-call | bytes 2309120 | tf_op jit(solution)/shard_map/fetch/pallas_call | solution.py:234
  13.0 6.4 %all-to-all-done = bf16[32,8,640]{2,1,0:T(8,128)(2,1)S(1)} async-done(((bf16[32,8,640]{2,1,0:T(8,128)(2,1)}), bf16[32,8,640]{2,1,0:T(8,128)(2,1)S(1)}, u32[]{:S(2)}, u32[]{:S(2)}) %all-to-all-start) | async-done | bytes 327712 | tf_op jit(solution)/shard_map/all_to_all | solution.py:251
  19.4 1.0 %join.1 = (f32[256,640]{1,0:T(8,128)S(1)}, f32[32,128]{1,0:T(8,128)S(1)}) custom-call(bf16[256,640]{1,0:T(8,128)(2,1)S(1)} %bitcast.18, bf16[256,640]{1,0:T(8,128)(2,1)S(1)} %bitcast.16, bf16[640,640]{1,0:T(8,128)(2,1)S(1)} %get-tuple-element.14.weight_ref), custom_call_target="tpu_custom_call" | custom-call | flops 209715200 | bytes 32000000 | tf_op jit(solution)/shard_map/join/pallas_call | solution.py:267
  20.4 9.3 %all_to_all.39 = f32[32,1,128]{2,1,0:T(1,128)S(1)} all-to-all(f32[32,1,128]{2,1,0:T(1,128)S(1)} %bitcast.20), channel_id=1, replica_groups=mesh['groups'=1,'frames'=32] {'frames'}, dimensions={0} | all-to-all | bytes 32768 | tf_op jit(solution)/shard_map/all_to_all | solution.py:251
  29.7 0.0 copy-start
  29.7 0.0 copy-start.1
  29.7 4.3 %conv.1 = (f32[256,640]{1,0:T(8,128)S(1)}, bf16[256,640]{1,0:T(8,128)(2,1)S(1)}) custom-call(s32[1]{0:T(128)} %constant.15.clone.1.clip_ref, f32[256,640]{1,0:T(8,128)S(1)} %get-tuple-element.15.joined_ref, f32[32,128]{1,0:T(8,128)S(1)} %bitcast.19, f32[3,640]{1,0:T(4,128)S(1)} %get-tuple-element.17.gains_ref, ...), custom_call_target="tpu_custom_call" | custom-call | flops 1887436800 | bytes 9000000 | tf_op jit(solution)/shard_map/conv/pallas_call | solution.py:284
  33.9 13.8 %all_to_all.40 = bf16[32,8,640]{2,1,0:T(8,128)(2,1)S(1)} all-to-all(bf16[32,8,640]{2,1,0:T(8,128)(2,1)S(1)} %bitcast.17), channel_id=1, replica_groups=mesh['groups'=1,'frames'=32] {'frames'}, dimensions={0} | all-to-all | bytes 655360 | tf_op jit(solution)/shard_map/all_to_all | solution.py:251
  47.7 0.0 copy-done
  47.7 0.0 copy-done.1
  47.7 2.8 %attend.1 = bf16[256,640]{1,0:T(8,128)(2,1)S(1)} custom-call(bf16[256,640]{1,0:T(8,128)(2,1)S(1)} %bitcast.14, f32[3,640]{1,0:T(4,128)S(1)} %get-tuple-element.17.gains_ref, bf16[640,1920]{1,0:T(8,128)(2,1)S(1)} %copy-done, bf16[640,640]{1,0:T(8,128)(2,1)S(1)} %copy-done.1), custom_call_target="tpu_custom_call" | custom-call | flops 838860800 | bytes 4000000 | tf_op jit(solution)/shard_map/attend/pallas_call | solution.py:312
  50.5 14.1 %all_to_all.41 = bf16[32,8,640]{2,1,0:T(8,128)(2,1)S(1)} all-to-all(bf16[32,8,640]{2,1,0:T(8,128)(2,1)S(1)} %bitcast.15), channel_id=1, replica_groups=mesh['groups'=1,'frames'=32] {'frames'}, dimensions={0} | all-to-all | bytes 655360 | tf_op jit(solution)/shard_map/all_to_all | solution.py:251
  64.6 0.8 %fusion.1 = bf16[1,256,640]{2,1,0:T(8,128)(2,1)} fusion(f32[256,640]{1,0:T(8,128)S(1)} %get-tuple-element.19, bf16[32,8,640]{2,1,0:T(8,128)(2,1)S(1)} %all_to_all.41), kind=kLoop, calls=%fused_computation.2 | loop fusion | flops 491520 | bytes 1310720 | tf_op jit(solution)/shard_map/convert_element_type | solution.py:329
  (1 shorter events, 0.0 us)
Async XLA Ops:
  0.0 19.4 %all-to-all-start = ((bf16[32,8,640]{2,1,0:T(8,128)(2,1)}), bf16[32,8,640]{2,1,0:T(8,128)(2,1)S(1)}, u32[]{:S(2)}, u32[]{:S(2)}) async-start(bf16[32,8,640]{2,1,0:T(8,128)(2,1)} %param.10), calls=%async_computation | async-start | bytes 655360 | tf_op jit(solution)/shard_map/all_to_all | solution.py:251
  9.4 1.1 %copy-start.2 = (bf16[640,640]{1,0:T(8,128)(2,1)S(1)}, bf16[640,640]{1,0:T(8,128)(2,1)}, u32[]{:S(2)}) copy-start(bf16[640,640]{1,0:T(8,128)(2,1)} %refs_1_.1) | copy-start | bytes 2457604
  10.6 1.0 %copy-start.3 = (bf16[1,256,640]{2,1,0:T(8,128)(2,1)S(1)}, bf16[1,256,640]{2,1,0:T(8,128)(2,1)}, u32[]{:S(2)}) copy-start(bf16[1,256,640]{2,1,0:T(8,128)(2,1)} %refs_0_.1) | copy-start | bytes 983044
  29.7 18.0 %copy-start = (bf16[640,1920]{1,0:T(8,128)(2,1)S(1)}, bf16[640,1920]{1,0:T(8,128)(2,1)}, u32[]{:S(2)}) copy-start(bf16[640,1920]{1,0:T(8,128)(2,1)} %qkv_ref.1) | copy-start | bytes 7372804
  29.7 18.0 %copy-start.1 = (bf16[640,640]{1,0:T(8,128)(2,1)S(1)}, bf16[640,640]{1,0:T(8,128)(2,1)}, u32[]{:S(2)}) copy-start(bf16[640,640]{1,0:T(8,128)(2,1)} %out_ref.1) | copy-start | bytes 2457604
